TPU v7x, 32 devices: a whole 2x2x4 slice. The times are simulated.
32 devices in a mesh: space: 8 (over z, x), tm: 4 (over y, core).
Axes of the slice: x: 2, y: 2, z: 4, core: 2. Of those that a mesh axis runs over, the one named last changes fastest.
Arguments:
- adjoint: bfloat16 [8, 64, 320, 512], P('tm', 'space'), may hold values from -6 to 6
- jacobian_diag: bfloat16 [8, 64, 320, 320], P('tm', 'space'), may hold values from -0.3125 to 0.3125
- jacobian_off: bfloat16 [8, 64, 2, 320, 320], P('tm', 'space'), may hold values from -0.3125 to 0.3125
- off_columns: int32 [64, 2], P('space'), may hold values from 0 to 15
- left_faces: int32 [8, 4], P('space'), may hold values from 0 to 7
- right_faces: int32 [8, 4], P('space'), may hold values from 0 to 7
- objective_grad: bfloat16 [8, 64, 320, 512], P('tm', 'space'), may hold values from -6 to 6
- pseudo_step: float32 [8, 64, 320], P('tm', 'space'), may hold values from 0.05 to 0.3
Outputs:
- adjoint_next: bfloat16 [8, 64, 320, 512], P('tm', 'space')
Inputs may be any that keep to these rules, and one draw needn't show every extreme that they name: `off_columns`: codes of column blocks: below 8 a block of the same partition, then 4 slots of the previous partition's right interface, then 4 slots of the next partition's left interface. `left_faces`: block numbers within the partition, repeats possible. `right_faces`: block numbers within the partition, repeats possible.
All inputs are finite; a program needn't handle non-finite values.
Results may differ from a plain program's by a relative error of at most 0.004.
Values may be sent and summed in bfloat16 or wider, within the bound.
No kernel may reach another device: no remote copies, remote signals or barrier semaphores. Data moves between devices by JAX's collectives and lax.ppermute only.
A program may use at most 320 MiB of HBM per device.

v0:
```python
import math

import jax
import jax.numpy as jnp
from jax import lax
from jax.sharding import PartitionSpec as P


def padded(array, sides, width):
    for axis, dim in sides:
        size, length = (lax.axis_size(axis), array.shape[dim])
        up = [(i, (i + 1) % size) for i in range(size)]
        down = [(j, i) for i, j in up]
        last = lax.slice_in_dim(array, length - width, length, axis=dim)
        initial = lax.slice_in_dim(array, 0, width, axis=dim)
        before = lax.ppermute(last, axis, up)
        after = lax.ppermute(initial, axis, down)
        array = jnp.concatenate([before, array, after], axis=dim)
    return array


def time_table(count):
    table = []
    for first in range(count):
        row_values = []
        for second in range(count):
            if first != second:
                delta = first - second
                parity = 1.0 - 2.0 * (delta % 2)
                row_values.append(0.5 * parity / math.tan(math.pi * delta / count))
            else:
                row_values.append(0.0)
        table.append(row_values)
    return table


def split_pick(picker, values):
    upper = values.astype(jnp.bfloat16)
    lower = (values - upper.astype(jnp.float32)).astype(jnp.bfloat16)
    first = jnp.einsum("sc,nsbo->ncbo", picker, upper, preferred_element_type=jnp.float32)
    second = jnp.einsum("sc,nsbo->ncbo", picker, lower, preferred_element_type=jnp.float32)
    return first + second


def per_device(
    adjoint,
    jacobian_diag,
    jacobian_off,
    off_columns,
    left_faces,
    right_faces,
    objective_grad,
    pseudo_step,
):
    inst_here = adjoint.shape[0]
    blocks_here = adjoint.shape[1]
    iface_count = left_faces.shape[1]
    couple_count = off_columns.shape[1]
    instances = inst_here * lax.axis_size("tm")
    table = jnp.asarray(time_table(instances), dtype=jnp.float32)
    total = jnp.einsum(
        "nrbc,nrbo->nrco", jacobian_diag, adjoint, preferred_element_type=jnp.float32
    )
    extended = blocks_here + 2 * iface_count
    column_ids = jnp.arange(extended, dtype=jnp.int32)
    spread = jnp.zeros((inst_here, extended) + adjoint.shape[2:], jnp.float32)
    for slot in range(couple_count):
        terms = jnp.einsum(
            "nrbc,nrbo->nrco", jacobian_off[:, :, slot], adjoint, preferred_element_type=jnp.float32
        ).astype(jnp.bfloat16)
        selector = (off_columns[:, slot][:, None] == column_ids[None, :]).astype(jnp.bfloat16)
        spread = spread + jnp.einsum(
            "rc,nrbo->ncbo", selector, terms, preferred_element_type=jnp.float32
        )
    outgoing = spread[:, blocks_here:]
    arrived = padded(outgoing.astype(jnp.bfloat16), (("space", 1),), iface_count).astype(
        outgoing.dtype
    )
    from_before = arrived[:, :iface_count]
    from_after = arrived[:, 3 * iface_count :]
    local_ids = jnp.arange(blocks_here, dtype=jnp.int32)
    pick_left = (left_faces[0][:, None] == local_ids[None, :]).astype(jnp.bfloat16)
    pick_right = (right_faces[0][:, None] == local_ids[None, :]).astype(jnp.bfloat16)
    total = total + spread[:, :blocks_here]
    total = total + split_pick(pick_left, from_before)
    total = total + split_pick(pick_right, from_after)
    own_columns = lax.dynamic_slice(
        table, (jnp.int32(0), lax.axis_index("tm") * inst_here), (instances, inst_here)
    )
    carry = jnp.zeros(adjoint.shape, jnp.float32)
    piece = lax.all_gather(adjoint, "tm", axis=0, tiled=True)
    start = jnp.int32(0)
    for step in range(piece.shape[0]):
        weights = lax.dynamic_slice(own_columns, (start + step, jnp.int32(0)), (1, inst_here))[0]
        carry = carry + weights[:, None, None, None] * piece[step].astype(jnp.float32)[None]
    residual = total + carry - objective_grad.astype(jnp.float32)
    updated = adjoint.astype(jnp.float32) - pseudo_step[:, :, :, None] * residual
    return updated.astype(jnp.bfloat16)


def solution(mesh):
    in_specs = (
        P("tm", "space", None, None),
        P("tm", "space", None, None),
        P("tm", "space", None, None, None),
        P("space", None),
        P("space", None),
        P("space", None),
        P("tm", "space", None, None),
        P("tm", "space", None),
    )
    out_specs = P("tm", "space", None, None)
    return jax.shard_map(
        per_device, mesh=mesh, in_specs=in_specs, out_specs=out_specs, check_vma=False
    )
```

profile of v0, /device:TPU:0, one launch (start us, length us, event | category | flops | bytes accessed | tf_op | source)
XLA Modules:
  0.0 306.1 jit_solution(8174836306967760709)
XLA Ops:
  6.5 0.0 copy-start.4
  6.5 0.0 all-gather.2.cloned.1.call-start
  6.5 0.0 slice-start
  6.5 0.7 all-gather.2.cloned.1.call-update
  7.3 0.0 copy-done.4
  7.3 0.0 slice-start.1
  7.3 6.8 %fusion.12 = bf16[2,8,320,512]{3,2,1,0:T(8,128)(2,1)S(1)} fusion(bf16[2,8,320,512]{3,2,1,0:T(8,128)(2,1)} %param.9, bf16[2,8,2,320,320]{4,3,2,1,0:T(8,128)(2,1)} %param.11), kind=kOutput, calls=%fused_computation.22 | convolution fusion | flops 1677721600 | bytes 14417920 | tf_op jit(solution)/shard_map/nrbc,nrbo->nrco/dot_general | solution.py:68
  14.1 0.0 slice-done
  14.1 0.0 slice-done.1
  14.1 5.5 %fusion.14 = bf16[2,8,320,512]{3,2,1,0:T(8,128)(2,1)S(1)} fusion(bf16[2,8,320,512]{3,2,1,0:T(8,128)(2,1)S(1)} %bitcast.102, bf16[2,8,2,320,320]{4,3,2,1,0:T(8,128)(2,1)} %param.11), kind=kOutput, calls=%fused_computation.24 | convolution fusion | flops 1677721600 | bytes 14417920 | tf_op jit(solution)/shard_map/nrbc,nrbo->nrco/dot_general | solution.py:68
  19.6 13.4 %fusion.11 = f32[2,320,512,16]{2,3,1,0:T(8,128)} fusion(bf16[2,8,320,512]{3,2,1,0:T(8,128)(2,1)S(1)} %fusion.12, s32[8]{0:T(128)S(1)} %get-tuple-element.32), kind=kOutput, calls=%fused_computation.21 | convolution fusion | flops 83886208 | bytes 26214432 | tf_op jit(solution)/shard_map/rc,nrbo->ncbo/dot_general | solution.py:72
  33.0 9.1 %fusion.10 = f32[2,320,512,16]{2,3,1,0:T(8,128)} fusion(bf16[2,8,320,512]{3,2,1,0:T(8,128)(2,1)S(1)} %fusion.14, s32[8]{0:T(128)S(1)} %get-tuple-element.31), kind=kOutput, calls=%fused_computation.20 | convolution fusion | flops 83886208 | bytes 26214432 | tf_op jit(solution)/shard_map/rc,nrbo->ncbo/dot_general | solution.py:72
  42.1 38.8 %fusion.50 = (bf16[2,16,320,512]{3,2,1,0:T(8,128)(2,1)S(1)}, f32[2,16,320,512]{3,2,1,0:T(8,128)}) fusion(f32[2,320,512,16]{2,3,1,0:T(8,128)} %fusion.11, f32[2,320,512,16]{2,3,1,0:T(8,128)} %fusion.10), kind=kLoop, calls=%fused_computation.80 | loop fusion | flops 10485760 | bytes 73400320 | tf_op jit(solution)/shard_map/convert.8
  81.0 2.9 fusion.52
  83.9 5.5 %collective-permute-start.1 = (bf16[2,4,320,512]{3,2,1,0:T(8,128)(2,1)}, bf16[2,4,320,512]{3,2,1,0:T(8,128)(2,1)S(1)}, u32[]{:S(2)}, u32[]{:S(2)}) collective-permute-start(bf16[2,4,320,512]{3,2,1,0:T(8,128)(2,1)} %get-tuple-element.22), channel_id=1, source_target_pairs={{4,0},{8,4},{12,8},{16,12},{20,16},{24,20},{28,24},{0,28},{5,1},{9... | collective-permute-start | bytes 7864328 | tf_op jit(solution)/shard_map/ppermute | solution.py:17
  89.4 0.0 copy-start.1
  89.4 0.0 collective-permute-start
  89.4 2.9 slice.77
  92.3 0.0 copy-done.1
  92.3 0.1 constant_dynamic-slice_fusion
  92.4 107.3 %collective-permute-done.1 = bf16[2,4,320,512]{3,2,1,0:T(8,128)(2,1)S(1)} collective-permute-done((bf16[2,4,320,512]{3,2,1,0:T(8,128)(2,1)}, bf16[2,4,320,512]{3,2,1,0:T(8,128)(2,1)S(1)}, u32[]{:S(2)}, u32[]{:S(2)}) %collective-permute-start.1) | collective-permute-done | bytes 2621472 | tf_op jit(solution)/shard_map/ppermute | solution.py:17
  199.6 0.3 collective-permute-done
  199.9 2.1 convert_convert_fusion
  202.0 0.0 copy-start.2
  202.0 0.9 fusion.8
  202.9 0.0 copy-done.2
  202.9 6.0 %fusion.26 = f32[2,320,512,8]{2,3,1,0:T(8,128)} fusion(bf16[2,4,320,512]{3,2,1,0:T(8,128)(2,1)S(1)} %get-tuple-element.33, s32[4]{0:T(128)S(1)} %bitcast.103), kind=kOutput, calls=%fused_computation.47 | convolution fusion | flops 20971552 | bytes 13107216 | tf_op jit(solution)/shard_map/sc,nsbo->ncbo/dot_general | solution.py:41
  208.9 0.0 copy-start.3
  208.9 5.9 %fusion.28 = f32[2,320,512,8]{2,3,1,0:T(8,128)} fusion(bf16[2,4,320,512]{3,2,1,0:T(8,128)(2,1)S(1)} %get-tuple-element.19, s32[4]{0:T(128)S(1)} %bitcast.104), kind=kOutput, calls=%fused_computation.49 | convolution fusion | flops 20971552 | bytes 13107216 | tf_op jit(solution)/shard_map/sc,nsbo->ncbo/dot_general | solution.py:40
  214.8 0.0 copy-done.3
  214.8 6.0 %fusion.30 = f32[2,320,512,8]{2,3,1,0:T(8,128)} fusion(bf16[2,4,320,512]{3,2,1,0:T(8,128)(2,1)S(1)} %get-tuple-element.34, s32[4]{0:T(128)S(1)} %bitcast.105), kind=kOutput, calls=%fused_computation.51 | convolution fusion | flops 20971552 | bytes 13107216 | tf_op jit(solution)/shard_map/sc,nsbo->ncbo/dot_general | solution.py:41
  220.8 6.0 %fusion.32 = f32[2,320,512,8]{2,3,1,0:T(8,128)} fusion(bf16[2,4,320,512]{3,2,1,0:T(8,128)(2,1)S(1)} %get-tuple-element.5, s32[4]{0:T(128)S(1)} %bitcast.106), kind=kOutput, calls=%fused_computation.53 | convolution fusion | flops 20971552 | bytes 13107216 | tf_op jit(solution)/shard_map/sc,nsbo->ncbo/dot_general | solution.py:40
  226.8 0.0 copy-start
  226.8 0.0 all-gather.2.cloned.1.call-done
  226.8 19.2 %fusion.25 = (f32[8,320,512]{2,1,0:T(8,128)}, f32[8,320,512]{2,1,0:T(8,128)}, f32[8,320,512]{2,1,0:T(8,128)}, f32[8,320,512]{2,1,0:T(8,128)}, f32[8,320,512]{2,1...) fusion(bf16[8,8,320,512]{3,2,1,0:T(8,128)(2,1)} %all-gather.2.cloned.1.call-done), kind=kLoop, calls=%fused_computation.43 | loop fusion | flops 10485760 | bytes 62914560 | tf_op jit(solution)/shard_map/mul | solution.py:95
  246.0 0.0 copy-done
  246.0 53.2 %fusion.7 = bf16[2,8,320,512]{3,2,1,0:T(8,128)(2,1)} fusion(f32[2,16,320,512]{3,2,1,0:T(8,128)} %get-tuple-element.10, f32[2,320,512,8]{2,3,1,0:T(8,128)} %fusion.26, f32[2,320,512,8]{2,3,1,0:T(8,128)} %fusion.28, f32[2,320,512,8]{2,3,1,0:T(8,128)} %fusion.30, f32[2,320,512,8]{2,3,1,0:T(8,128)} %fusion.32, bf16[2,8,320,512]{3,2,1,0:T(8,128)(2,1)} %param.15, ...), kind=kOutput, calls=%fused_computation.9 | convolution fusion | flops 1748500480 | bytes 119296064 | tf_op jit(solution)/shard_map/nrbc,nrbo->nrco/dot_general | solution.py:61
  (3 shorter events, 0.0 us)
Async XLA Ops:
  6.5 0.7 copy-start.4
  6.5 220.2 %all-gather.2.cloned.1.call-start = ((), (), s32[]{:S(2)}) async-start(), calls=%async_computation | async-start | bytes 26214400 | tf_op jit(solution)/shard_map/all_gather | solution.py:91
  6.5 7.5 %slice-start = ((s8[5242880]{0:T(1024)(128)(4,1)}), s8[1048576]{0:T(1024)(128)(4,1)S(1)}, s32[]{:S(2)}) async-start(s8[5242880]{0:T(1024)(128)(4,1)} %bitcast.101), calls=%async_computation.1 | async-start | bytes 2097152
  7.3 6.8 %slice-start.1 = ((s8[5242880]{0:T(1024)(128)(4,1)}), s8[4194304]{0:T(1024)(128)(4,1)S(1)}, s32[]{:S(2)}) async-start(s8[5242880]{0:T(1024)(128)(4,1)} %bitcast.101), calls=%async_computation.2 | async-start | bytes 8388608
  83.9 115.8 %collective-permute-start.1 = (bf16[2,4,320,512]{3,2,1,0:T(8,128)(2,1)}, bf16[2,4,320,512]{3,2,1,0:T(8,128)(2,1)S(1)}, u32[]{:S(2)}, u32[]{:S(2)}) collective-permute-start(bf16[2,4,320,512]{3,2,1,0:T(8,128)(2,1)} %get-tuple-element.22), channel_id=1, source_target_pairs={{4,0},{8,4},{12,8},{16,12},{20,16},{24,20},{28,24},{0,28},{5,1},{9... | collective-permute-start | bytes 7864328 | tf_op jit(solution)/shard_map/ppermute | solution.py:17
  89.4 2.9 copy-start.1
  89.4 110.5 %collective-permute-start = (bf16[2,4,320,512]{3,2,1,0:T(8,128)(2,1)}, bf16[2,4,320,512]{3,2,1,0:T(8,128)(2,1)}, u32[]{:S(2)}, u32[]{:S(2)}) collective-permute-start(bf16[2,4,320,512]{3,2,1,0:T(8,128)(2,1)} %get-tuple-element.21), channel_id=1, source_target_pairs={{0,4},{4,8},{8,12},{12,16},{16,20},{20,24},{24,28},{28,0},{1,5},{5... | collective-permute-start | bytes 7864328 | tf_op jit(solution)/shard_map/ppermute | solution.py:16
  202.0 0.9 copy-start.2
  208.9 5.9 %copy-start.3 = (s32[1,4]{1,0:T(1,128)S(1)}, s32[1,4]{1,0:T(1,128)}, u32[]{:S(2)}) copy-start(s32[1,4]{1,0:T(1,128)} %param.13) | copy-start | bytes 52
  226.8 19.2 %copy-start = (f32[2,8,320]{2,1,0:T(8,128)S(1)}, f32[2,8,320]{2,1,0:T(8,128)}, u32[]{:S(2)}) copy-start(f32[2,8,320]{2,1,0:T(8,128)} %param.16) | copy-start | bytes 61444
Sparse Core Ops, SparseCore 0:
  8.9 134.3 all-gather.1
where the time goes:
time: 306 us
  matrix products  112 us (37%)
  waiting for transfers between devices  108 us (35%)
  other arithmetic  61 us (20%)
  between operations  13.5 us (4%)
  local copies, waits for them, and re-layouts  5.92 us (2%)
  starting transfers between devices  5.49 us (2%)
    ppermute x1, waiting for transfers between devices, padded(): after = lax.ppermute(initial, axis, down)  107 us
    dot_general x1, matrix products, per_device(): jnp.einsum('nrbc,nrbo->nrco', jacobian_diag, adjoint, preferred_element_t...  53.2 us
    another operation x1, other arithmetic  38.8 us
    dot_general x2, matrix products, per_device(): jnp.einsum('rc,nrbo->ncbo', selector, terms, preferred_element_type=jnp.f...  22.5 us
    mul x1, other arithmetic, per_device(): weights[:, None, None, None] * piece[step].astype(jnp.float32)[None]  19.2 us
    dot_general x2, matrix products, per_device(): jnp.einsum('nrbc,nrbo->nrco', jacobian_off[:, :, slot], adjoint, preferre...  12.3 us
    dot_general x2, matrix products, split_pick(): jnp.einsum('sc,nsbo->ncbo', picker, lower, preferred_element_type=jnp.flo...  12 us
    dot_general x2, matrix products, split_pick(): jnp.einsum('sc,nsbo->ncbo', picker, upper, preferred_element_type=jnp.flo...  11.9 us
  transfers between devices with their start and end apart: 3, of which 2 were waited for; matrix products, arithmetic and copies ran while one was open for 35% of the time, Pallas kernels for 0%

commit v1 on v0

v1 whole, which is shorter than its diff:
```python
import functools
import math

import jax
import jax.numpy as jnp
from jax import lax
from jax.experimental import pallas as pl
from jax.experimental.pallas import tpu as pltpu
from jax.sharding import PartitionSpec as P


ANY = pl.BlockSpec(memory_space=pl.ANY)
SMEM = pl.BlockSpec(memory_space=pltpu.SMEM)
SLOTS = 3


def time_table(count):
    table = []
    for first in range(count):
        row_values = []
        for second in range(count):
            if first != second:
                delta = first - second
                parity = 1.0 - 2.0 * (delta % 2)
                row_values.append(0.5 * parity / math.tan(math.pi * delta / count))
            else:
                row_values.append(0.0)
        table.append(row_values)
    return table


def transposed_product(jacobian, state):
    return lax.dot_general(
        jacobian, state, (((0,), (0,)), ((), ())), preferred_element_type=jnp.float32
    )


def remote_kernel(inst, low, high, pieces, first, codes, state_hbm, off_hbm, *rest):
    outs, rest = rest[: len(pieces)], rest[len(pieces) :]
    if first:
        passed_hbm, *rest = rest
        *rest, passed, read_sem, write_sem = rest
    acc, states, jacobians, picked, state_sem, off_sem = rest
    blocks = codes.shape[1]

    def scan(term, found):
        code = codes[lax.div(term, blocks), lax.rem(term, blocks)]
        picked[found] = term
        return found + jnp.where((code >= low) & (code < high), 1, 0)

    found = lax.fori_loop(0, codes.shape[0] * blocks, scan, jnp.int32(0))

    def copies(index):
        slot = lax.rem(index, SLOTS)
        term = picked[index]
        row = lax.rem(term, blocks)
        return (
            pltpu.make_async_copy(state_hbm.at[inst, row], states.at[slot], state_sem.at[slot]),
            pltpu.make_async_copy(
                off_hbm.at[inst, row, lax.div(term, blocks)], jacobians.at[slot], off_sem.at[slot]
            ),
        )

    for ahead in range(SLOTS - 1):

        @pl.when(ahead < found)
        def _():
            for copy in copies(jnp.int32(ahead)):
                copy.start()

    if first:
        source = state_hbm.at[:, pl.ds(0, first)]
        pltpu.make_async_copy(source, passed, read_sem).start()
    acc[...] = jnp.zeros_like(acc)

    def one(index, carry):
        @pl.when(index + SLOTS - 1 < found)
        def _():
            for copy in copies(index + SLOTS - 1):
                copy.start()

        for copy in copies(index):
            copy.wait()
        slot = lax.rem(index, SLOTS)
        term = transposed_product(jacobians[slot], states[slot]).astype(jnp.bfloat16)
        chosen = picked[index]
        place = codes[lax.div(chosen, blocks), lax.rem(chosen, blocks)] - low
        acc[place] += term.astype(jnp.float32)
        return carry

    lax.fori_loop(0, found, one, 0)
    if first:
        pltpu.make_async_copy(source, passed, read_sem).wait()
        write = pltpu.make_async_copy(passed, passed_hbm, write_sem)
        write.start()
    for out, (slot_low, slot_high, row_low, row_high) in zip(outs, pieces):
        for slot in range(slot_low, slot_high):
            out[0, slot - slot_low] = acc[slot, row_low:row_high].astype(jnp.bfloat16)
    if first:
        write.wait()


def remote_terms(inst, low, high, pieces, codes, adjoint, off, first=0):
    insts, blocks, dof, wide = adjoint.shape
    couple = off.shape[2]
    shapes = [
        jax.ShapeDtypeStruct((1, b - a, d - c, wide), jnp.bfloat16) for a, b, c, d in pieces
    ]
    out_specs = [pl.BlockSpec(memory_space=pltpu.VMEM)] * len(pieces)
    extra = []
    if first:
        passed = (insts, first, dof, wide)
        shapes.append(jax.ShapeDtypeStruct(passed, jnp.bfloat16))
        out_specs.append(ANY)
        extra = [
            pltpu.VMEM(passed, jnp.bfloat16),
            pltpu.SemaphoreType.DMA(()),
            pltpu.SemaphoreType.DMA(()),
        ]
    work = high - low
    return pl.pallas_call(
        functools.partial(remote_kernel, inst, low, high, pieces, first),
        out_shape=shapes,
        in_specs=[SMEM, ANY, ANY],
        out_specs=out_specs,
        scratch_shapes=[
            pltpu.VMEM((high - low, dof, wide), jnp.float32),
            pltpu.VMEM((SLOTS, dof, wide), jnp.bfloat16),
            pltpu.VMEM((SLOTS, dof, dof), jnp.bfloat16),
            pltpu.SMEM((couple * blocks + 1,), jnp.int32),
            pltpu.SemaphoreType.DMA((SLOTS,)),
            pltpu.SemaphoreType.DMA((SLOTS,)),
            *extra,
        ],
        cost_estimate=pl.CostEstimate(
            flops=2 * work * dof * dof * wide,
            bytes_accessed=work * 2 * dof * (dof + wide),
            transcendentals=0,
        ),
    )(codes, adjoint, off)


def local_kernel(
    insts, couple, first, codes, here, table, adj_all, near_all, far_all, relay_all,
    state, diag, off, grad, step, base, acc,
):
    inst, row = pl.program_id(0), pl.program_id(1)
    blocks = pl.num_programs(1)

    @pl.when(row == 0)
    def _():
        acc[...] = jnp.zeros_like(acc)

    acc[row] += transposed_product(diag[0, 0], state[0, 0])
    for slot in range(couple):
        code = codes[slot, row]

        @pl.when(code < blocks)
        def _():
            term = transposed_product(off[0, 0, slot], state[0, 0]).astype(jnp.bfloat16)
            acc[code] += term.astype(jnp.float32)

    @pl.when(row == blocks - 1)
    def _():
        def mix(total, block, sources, at):
            for index, source in enumerate(sources):
                for other in range(insts):
                    sender = here[0] ^ (at + index)
                    weight = table[sender * insts + other, here[0] * insts + inst]
                    total += weight * source[other, block].astype(jnp.float32)
            return total

        def finish(block, carry):
            total = acc[block] - grad[0, block].astype(jnp.float32)
            total = mix(total, block, (adj_all, near_all), 0)
            mine = adj_all[inst, block].astype(jnp.float32)
            base[0, block] = mine - step[0, block] * total
            return carry

        def finish_far(block, carry):
            total = mix(jnp.zeros(acc.shape[1:], jnp.float32), block, (far_all, relay_all), 2)
            base[0, block] -= step[0, block] * total
            return carry

        lax.fori_loop(0, base.shape[1], finish, 0)
        lax.fori_loop(0, first, finish_far, 0)


def local_part(codes, here, table, adjoint, near, far, relay, diag, off, grad, step):
    insts, blocks, dof, wide = adjoint.shape
    couple = off.shape[2]
    first = far.shape[1]

    def whole(shape):
        return pl.BlockSpec(shape, lambda n, r: (0, 0, 0, 0), pipeline_mode=pl.Buffered(1))

    return pl.pallas_call(
        functools.partial(local_kernel, insts, couple, first),
        grid=(insts, blocks),
        out_shape=jax.ShapeDtypeStruct(adjoint.shape, jnp.float32),
        in_specs=[
            SMEM,
            SMEM,
            SMEM,
            whole(adjoint.shape),
            whole(near.shape),
            whole(far.shape),
            whole(relay.shape),
            pl.BlockSpec((1, 1, dof, wide), lambda n, r: (n, r, 0, 0)),
            pl.BlockSpec((1, 1, dof, dof), lambda n, r: (n, r, 0, 0)),
            pl.BlockSpec((1, 1, couple, dof, dof), lambda n, r: (n, r, 0, 0, 0)),
            pl.BlockSpec((1, blocks, dof, wide), lambda n, r: (n, 0, 0, 0)),
            pl.BlockSpec((1, blocks, dof, 1), lambda n, r: (n, 0, 0, 0)),
        ],
        out_specs=pl.BlockSpec((1, blocks, dof, wide), lambda n, r: (n, 0, 0, 0)),
        scratch_shapes=[pltpu.VMEM((blocks, dof, wide), jnp.float32)],
        cost_estimate=pl.CostEstimate(
            flops=4 * insts * blocks * dof * dof * wide,
            bytes_accessed=insts * blocks * dof * (6 * dof + 12 * wide),
            transcendentals=0,
        ),
        name="local_part",
    )(codes, here, table, adjoint, near, far, relay, adjoint, diag, off, grad, step)


def mix_kernel(insts, pieces, here, table, own, near, *outs):
    for inst in range(insts):
        total = None
        for index, source in enumerate((own, near)):
            for other in range(insts):
                sender, target = here[0] ^ index, here[0] ^ 2
                weight = table[sender * insts + other, target * insts + inst]
                term = weight * source[other, 0].astype(jnp.float32)
                total = term if total is None else total + term
        total = total.astype(jnp.bfloat16)
        for out, (which, low, high) in zip(outs, pieces):
            if which == inst:
                out[0, 0] = total[low:high]


def mix(here, table, adjoint, near, first, pieces):
    insts, blocks, dof, wide = adjoint.shape
    state = pl.BlockSpec((insts, 1, dof, wide), lambda r: (0, r + first, 0, 0))
    count = blocks - first
    return pl.pallas_call(
        functools.partial(mix_kernel, insts, pieces),
        grid=(count,),
        out_shape=[
            jax.ShapeDtypeStruct((1, count, high - low, wide), jnp.bfloat16)
            for _, low, high in pieces
        ],
        in_specs=[SMEM, SMEM, state, state],
        out_specs=[
            pl.BlockSpec((1, 1, high - low, wide), lambda r: (0, r, 0, 0))
            for _, low, high in pieces
        ],
        cost_estimate=pl.CostEstimate(
            flops=8 * insts * count * dof * wide,
            bytes_accessed=6 * insts * count * dof * wide,
            transcendentals=0,
        ),
        name="mix",
    )(here, table, adjoint, near)


def final_kernel(group, first, places, left, right, base, step, far, *rest):
    arrivals = rest[: len(places)]
    out, total = rest[-2:]
    start = pl.program_id(0) * group

    def one(inner, carry):
        block = start + inner
        known = far[0, jnp.maximum(block - first, 0)]
        total[...] = jnp.where(block >= first, known, 0).astype(jnp.float32)
        for arrived, (side, offset) in zip(arrivals, places):
            faces = (left, right)[side]
            for slot in range(arrived.shape[1]):

                @pl.when(faces[0, offset + slot] == block)
                def _():
                    total[...] += arrived[0, slot].astype(jnp.float32)

        out[0, inner] = (base[0, inner] - step[0, inner] * total[...]).astype(jnp.bfloat16)
        return carry

    lax.fori_loop(0, group, one, 0)


def final_part(inst, row_low, row_high, group, left, right, base, step, far, arrivals, out, limit):
    _, blocks, _, wide = base.shape
    rows = row_high - row_low
    at = row_low // rows
    state = pl.BlockSpec((1, group, rows, wide), lambda g: (inst, g, at, 0))
    whole = lambda x: pl.BlockSpec(x.shape, lambda g: (0, 0, 0, 0), pipeline_mode=pl.Buffered(1))
    terms = [x for _, _, x in arrivals]
    places = [(side, offset) for side, offset, _ in arrivals]
    operands = [left, right, base, step, far, *terms]
    specs = [
        SMEM,
        SMEM,
        state,
        pl.BlockSpec((1, group, rows, 1), lambda g: (inst, g, at, 0)),
        whole(far),
        *[whole(x) for x in terms],
    ]
    aliases = {}
    if out is not None:
        aliases = {len(operands): 0}
        operands.append(out)
        specs.append(ANY)
    return pl.pallas_call(
        functools.partial(final_kernel, group, blocks - far.shape[1], places),
        grid=(blocks // group,),
        out_shape=jax.ShapeDtypeStruct(base.shape, jnp.bfloat16),
        in_specs=specs,
        out_specs=state,
        scratch_shapes=[pltpu.VMEM((rows, wide), jnp.float32)],
        input_output_aliases=aliases,
        cost_estimate=pl.CostEstimate(
            flops=20 * blocks * rows * wide,
            bytes_accessed=10 * blocks * rows * wide,
            transcendentals=0,
        ),
        compiler_params=pltpu.CompilerParams(vmem_limit_bytes=limit << 20),
    )(*operands)


def per_device(adjoint, diag, off, off_columns, left, right, grad, step):
    insts, blocks, dof, _ = adjoint.shape
    iface = left.shape[1]
    parts, times = lax.axis_size("space"), lax.axis_size("tm")
    if times != 4 or insts != 2:
        raise ValueError("unsupported tm size")
    instances = insts * times
    here = lax.axis_index("tm").astype(jnp.int32)[None]
    table = jnp.asarray(time_table(instances), dtype=jnp.float32)
    swap_core = [(i, i ^ 1) for i in range(times)]
    swap_chip = [(i, i ^ 2) for i in range(times)]
    up = [(i, (i + 1) % parts) for i in range(parts)]
    down = [(j, i) for i, j in up]
    codes = off_columns.T

    cut, first, ends = 256, 2, blocks + 2 * iface

    half = iface // 2
    up0, passed = remote_terms(
        0, ends - half, ends, [(0, half, 0, dof)], codes, adjoint, off, first
    )
    before0 = lax.ppermute(up0, "space", up)
    far0 = lax.ppermute(passed, "tm", swap_chip)
    near = lax.ppermute(adjoint, "tm", swap_core)
    pieces = [(iface, 2 * iface - half, 0, dof), (0, iface, 0, dof)]
    up0b, down0 = remote_terms(0, blocks, ends - half, pieces, codes, adjoint, off)
    before0b = lax.ppermute(up0b, "space", up)
    after0 = lax.ppermute(down0, "space", down)
    pieces = [
        (iface, 2 * iface, 0, cut),
        (0, iface, 0, cut),
        (iface, 2 * iface, cut, dof),
        (0, iface, cut, dof),
    ]
    up1a, down1a, up1b, down1b = remote_terms(1, blocks, ends, pieces, codes, adjoint, off)
    mixed = mix(here, table, adjoint, near, first, [(0, 0, dof), (1, 0, cut), (1, cut, dof)])
    far1 = lax.ppermute(mixed[0], "tm", swap_chip)
    far2a = lax.ppermute(mixed[1], "tm", swap_chip)
    far2b = lax.ppermute(mixed[2], "tm", swap_chip)
    before1a = lax.ppermute(up1a, "space", up)
    after1a = lax.ppermute(down1a, "space", down)
    before1b = lax.ppermute(up1b, "space", up)
    after1b = lax.ppermute(down1b, "space", down)
    relay = lax.ppermute(far0, "tm", swap_core)
    step = step[..., None]
    base = local_part(codes, here, table, adjoint, near, far0, relay, diag, off, grad, step)
    arrivals = [(0, iface - half, before0), (0, 0, before0b), (1, 0, after0)]
    out = final_part(0, 0, dof, 1, left, right, base, step, far1, arrivals, None, 16)
    arrivals = [(0, 0, before1a), (1, 0, after1a)]
    out = final_part(1, 0, cut, 1, left, right, base, step, far2a, arrivals, out, 16)
    arrivals = [(0, 0, before1b), (1, 0, after1b)]
    return final_part(1, cut, dof, blocks, left, right, base, step, far2b, arrivals, out, 12)


def solution(mesh):
    in_specs = (
        P("tm", "space", None, None),
        P("tm", "space", None, None),
        P("tm", "space", None, None, None),
        P("space", None),
        P("space", None),
        P("space", None),
        P("tm", "space", None, None),
        P("tm", "space", None),
    )
    out_specs = P("tm", "space", None, None)
    return jax.shard_map(
        per_device, mesh=mesh, in_specs=in_specs, out_specs=out_specs, check_vma=False
    )
```

time: 306 us -> 162 us (0.53)
  matrix products: 112 us -> 0 us
  Pallas kernels: 0 us -> 75.3 us
  other arithmetic: 61 us -> 0.01 us
  waiting for transfers between devices: 108 us -> 50.7 us
  starting transfers between devices: 5.49 us -> 20.8 us
  between operations: 13.5 us -> 0.17 us
  local copies, waits for them, and re-layouts: 5.92 us -> 14.4 us
    dot_general x9 -> x0, matrix products: 112 us -> none  [the longest x1 53.2 us: per_device(): jnp.einsum('nrbc,nrbo->nrco', jacobian_diag, adjoint, preferred_element_t...]
    pallas_call x0 -> x8, Pallas kernels: none -> 75.3 us  [the longest x1 31.6 us: local_part(): pl.pallas_call(functools.partial(local_kernel, insts, couple, first), gri...]
    ppermute x2 -> x13, waiting for transfers between devices: 108 us -> 50.7 us  [the longest x1 29.5 us: per_device(): before0b = lax.ppermute(up0b, 'space', up)]
    another operation x1 -> x0, other arithmetic: 38.8 us -> none
    mul x1 -> x0, other arithmetic: 19.2 us -> none  [per_device(): weights[:, None, None, None] * piece[step].astype(jnp.float32)[None]]
    ppermute x2 -> x13, starting transfers between devices: 5.49 us -> 20.8 us  [the longest x1 4.72 us: per_device(): after1b = lax.ppermute(down1b, 'space', down)]
    unnamed x14 -> x32, local copies, waits for them, and re-layouts: 0.03 us -> 12.1 us
    slice x2 -> x0, local copies, waits for them, and re-layouts: 5.81 us -> none  [the longest x1 2.91 us: padded(): last = lax.slice_in_dim(array, length - width, length, axis=dim)]
  transfers between devices with their start and end apart: 3 -> 13, of which waited for: 2 -> 3; matrix products, arithmetic and copies ran while one was open for 35% -> 1% of each run, Pallas kernels for 0% -> 45%
where the time goes in v1:
time: 162 us; the launch traced here: 161 us
  Pallas kernels  75.3 us (46%)
  waiting for transfers between devices  50.7 us (31%)
  starting transfers between devices  20.8 us (13%)
  local copies, waits for them, and re-layouts  14.4 us (9%)
    pallas_call x1, Pallas kernels, local_part(): pl.pallas_call(functools.partial(local_kernel, insts, couple, first), gri...  31.6 us
    ppermute x1, waiting for transfers between devices, per_device(): before0b = lax.ppermute(up0b, 'space', up)  29.5 us
    pallas_call x3, Pallas kernels, remote_terms(): pl.pallas_call(functools.partial(remote_kernel, inst, low, high, pieces,...  22.2 us
    ppermute x1, waiting for transfers between devices, per_device(): before1a = lax.ppermute(up1a, 'space', up)  20.8 us
    pallas_call x3, Pallas kernels, final_part(): pl.pallas_call(functools.partial(final_kernel, group, blocks - far.shape[...  14.3 us
    unnamed x32, local copies, waits for them, and re-layouts  12.1 us
    pallas_call x1, Pallas kernels, mix(): pl.pallas_call(functools.partial(mix_kernel, insts, pieces), grid=(count,...  7.32 us
    ppermute x1, starting transfers between devices, per_device(): after1b = lax.ppermute(down1b, 'space', down)  4.72 us
  transfers between devices with their start and end apart: 13, of which 3 were waited for; matrix products, arithmetic and copies ran while one was open for 1% of the time, Pallas kernels for 45%

profile of v1, /device:TPU:0, one launch (start us, length us, event | category | flops | bytes accessed | tf_op | source)
XLA Modules:
  0.0 161.5 jit_solution(12929813795000489410)
XLA Ops:
  0.0 0.5 collective-permute-start
  0.5 4.4 %shard_map.91 = (bf16[1,2,320,512]{3,2,1,0:T(8,128)(2,1)}, bf16[2,2,320,512]{3,2,1,0:T(8,128)(2,1)}) custom-call(s32[2,8]{1,0:T(2,128)} %bitcast.6, bf16[2,8,320,512]{3,2,1,0:T(8,128)(2,1)} %state_hbm.5, bf16[2,8,2,320,320]{4,3,2,1,0:T(8,128)(2,1)} %off_hbm.5), custom_call_target="tpu_custom_call" | custom-call | flops 209715200 | bytes 1064960 | tf_op jit(solution)/shard_map/pallas_call | solution.py:121
  4.9 2.6 %collective-permute-start.1 = (bf16[2,2,320,512]{3,2,1,0:T(8,128)(2,1)}, bf16[2,2,320,512]{3,2,1,0:T(8,128)(2,1)}, u32[]{:S(2)}, u32[]{:S(2)}) collective-permute-start(bf16[2,2,320,512]{3,2,1,0:T(8,128)(2,1)} %get-tuple-element.16), channel_id=1, source_target_pairs={{0,2},{1,3},{2,0},{3,1},{4,6},{5,7},{6,4},{7,5},{8,10},{9,11},{10,... | collective-permute-start | bytes 3932168 | tf_op jit(solution)/shard_map/ppermute | solution.py:350
  7.5 1.7 %collective-permute-start.10 = (bf16[1,2,320,512]{3,2,1,0:T(8,128)(2,1)}, bf16[1,2,320,512]{3,2,1,0:T(8,128)(2,1)S(1)}, u32[]{:S(2)}, u32[]{:S(2)}) collective-permute-start(bf16[1,2,320,512]{3,2,1,0:T(8,128)(2,1)} %get-tuple-element.24), channel_id=1, source_target_pairs={{0,4},{4,8},{8,12},{12,16},{16,20},{20,24},{24,28},{28,0},{1,5},{5... | collective-permute-start | bytes 1966088 | tf_op jit(solution)/shard_map/ppermute | solution.py:349
  9.2 0.0 collective-permute-done.near_all.near
  9.2 7.3 %mix.1 = (bf16[1,6,320,512]{3,2,1,0:T(8,128)(2,1)}, bf16[1,6,256,512]{3,2,1,0:T(8,128)(2,1)}, bf16[1,6,64,512]{3,2,1,0:T(8,128)(2,1)}) custom-call(s32[1]{0:T(128)} %bitcast.1.here, f32[8,8]{1,0:T(8,128)} %constant.6.clone.table, bf16[2,8,320,512]{3,2,1,0:T(8,128)(2,1)} %state_hbm.5, bf16[2,8,320,512]{3,2,1,0:T(8,128)(2,1)} %collective-permute-done.near_all.near), custom_call_target="tpu_custom_call" | custom-call | flops 15728640 | bytes 11796480 | tf_op jit(solution)/shard_map/mix/pallas_call | solution.py:245
  16.5 2.7 %collective-permute-start.9 = (bf16[1,6,320,512]{3,2,1,0:T(8,128)(2,1)}, bf16[1,6,320,512]{3,2,1,0:T(8,128)(2,1)S(1)}, u32[]{:S(2)}, u32[]{:S(2)}) collective-permute-start(bf16[1,6,320,512]{3,2,1,0:T(8,128)(2,1)} %get-tuple-element.23), channel_id=1, source_target_pairs={{0,2},{1,3},{2,0},{3,1},{4,6},{5,7},{6,4},{7,5},{8,10},{9,11},{10,... | collective-permute-start | bytes 5898248 | tf_op jit(solution)/shard_map/ppermute | solution.py:364
  19.3 8.5 %shard_map.93 = (bf16[1,2,320,512]{3,2,1,0:T(8,128)(2,1)}, bf16[1,4,320,512]{3,2,1,0:T(8,128)(2,1)}) custom-call(s32[2,8]{1,0:T(2,128)} %bitcast.7, bf16[2,8,320,512]{3,2,1,0:T(8,128)(2,1)} %state_hbm.5, bf16[2,8,2,320,320]{4,3,2,1,0:T(8,128)(2,1)} %off_hbm.5), custom_call_target="tpu_custom_call" | custom-call | flops 629145600 | bytes 3194880 | tf_op jit(solution)/shard_map/pallas_call | solution.py:121
  27.8 0.0 copy-start.12
  27.8 0.1 collective-permute-start.11
  27.9 9.3 %shard_map.92 = (bf16[1,4,256,512]{3,2,1,0:T(8,128)(2,1)}, bf16[1,4,256,512]{3,2,1,0:T(8,128)(2,1)}, bf16[1,4,64,512]{3,2,1,0:T(8,128)(2,1)}, bf16[1,4,64,512]{3,2,1,0:T(8,128)(2,1)}) custom-call(s32[2,8]{1,0:T(2,128)} %bitcast.8, bf16[2,8,320,512]{3,2,1,0:T(8,128)(2,1)} %state_hbm.5, bf16[2,8,2,320,320]{4,3,2,1,0:T(8,128)(2,1)} %off_hbm.5), custom_call_target="tpu_custom_call" | custom-call | flops 838860800 | bytes 4259840 | tf_op jit(solution)/shard_map/pallas_call | solution.py:121
  37.2 0.1 collective-permute-start.7
  37.2 0.0 collective-permute-done.10.rest_0_
  37.2 4.7 %collective-permute-start.12 = (bf16[1,4,320,512]{3,2,1,0:T(8,128)(2,1)}, bf16[1,4,320,512]{3,2,1,0:T(8,128)(2,1)S(1)}, u32[]{:S(2)}, u32[]{:S(2)}) collective-permute-start(bf16[1,4,320,512]{3,2,1,0:T(8,128)(2,1)} %get-tuple-element.26), channel_id=1, source_target_pairs={{4,0},{8,4},{12,8},{16,12},{20,16},{24,20},{28,24},{0,28},{5,1},{9... | collective-permute-start | bytes 3932168 | tf_op jit(solution)/shard_map/ppermute | solution.py:355
  41.9 0.0 collective-permute-done.1.far_all
  41.9 0.0 collective-permute-start.2
  41.9 29.5 %collective-permute-done.11.rest_1_ = bf16[1,2,320,512]{3,2,1,0:T(8,128)(2,1)S(1)} collective-permute-done((bf16[1,2,320,512]{3,2,1,0:T(8,128)(2,1)}, bf16[1,2,320,512]{3,2,1,0:T(8,128)(2,1)S(1)}, u32[]{:S(2)}, u32[]{:S(2)}) %collective-permute-start.11) | collective-permute-done | bytes 655392 | tf_op jit(solution)/shard_map/ppermute | solution.py:354
  71.4 0.0 copy-start.8
  71.4 0.8 copy-done.8
  72.2 0.0 collective-permute-start.6
  72.2 20.8 %collective-permute-done.7.rest_0_ = bf16[1,4,256,512]{3,2,1,0:T(8,128)(2,1)S(1)} collective-permute-done((bf16[1,4,256,512]{3,2,1,0:T(8,128)(2,1)}, bf16[1,4,256,512]{3,2,1,0:T(8,128)(2,1)S(1)}, u32[]{:S(2)}, u32[]{:S(2)}) %collective-permute-start.7) | collective-permute-done | bytes 1048608 | tf_op jit(solution)/shard_map/ppermute | solution.py:367
  93.1 0.0 copy-start.6
  93.1 1.0 copy-done.6
  94.0 3.5 %collective-permute-start.8 = (bf16[1,4,256,512]{3,2,1,0:T(8,128)(2,1)}, bf16[1,4,256,512]{3,2,1,0:T(8,128)(2,1)}, u32[]{:S(2)}, u32[]{:S(2)}) collective-permute-start(bf16[1,4,256,512]{3,2,1,0:T(8,128)(2,1)} %get-tuple-element.22), channel_id=1, source_target_pairs={{4,0},{8,4},{12,8},{16,12},{20,16},{24,20},{28,24},{0,28},{5,1},{9... | collective-permute-start | bytes 3145736 | tf_op jit(solution)/shard_map/ppermute | solution.py:368
  97.5 0.4 collective-permute-done.12.rest_2_
  97.9 0.0 copy-start.4
  97.9 1.1 copy-done.4
  99.0 0.3 collective-permute-start.3
  99.3 0.0 copy-done.12
  99.3 2.3 %copy.12.step = f32[2,8,320,1]{3,2,1,0:T(8,128)} copy(f32[2,8,320,1]{2,1,0,3:T(8,128)S(1)} %bitcast.5) | data formatting | bytes 40960 | tf_op jit(solution)/shard_map/broadcast_in_dim | solution.py:372
  101.6 0.0 collective-permute-done.2.relay_all
  101.6 0.0 collective-permute-start.4
  101.6 0.0 collective-permute-done.9.far
  101.6 0.0 copy-start.2
  101.6 1.3 copy-done.2
  102.9 0.0 copy-start.1
  102.9 0.0 copy-start.10
  102.9 0.0 copy-start.11
  102.9 4.7 %collective-permute-start.5 = (bf16[1,4,64,512]{3,2,1,0:T(8,128)(2,1)}, bf16[1,4,64,512]{3,2,1,0:T(8,128)(2,1)}, u32[]{:S(2)}, u32[]{:S(2)}) collective-permute-start(bf16[1,4,64,512]{3,2,1,0:T(8,128)(2,1)} %get-tuple-element.19), channel_id=1, source_target_pairs={{4,0},{8,4},{12,8},{16,12},{20,16},{24,20},{28,24},{0,28},{5,1},{9... | collective-permute-start | bytes 786440 | tf_op jit(solution)/shard_map/ppermute | solution.py:370
  107.6 31.6 %local_part.1.base = f32[2,8,320,512]{3,2,1,0:T(8,128)} custom-call(s32[2,8]{1,0:T(2,128)} %bitcast.9, s32[1]{0:T(128)} %bitcast.1.here, f32[8,8]{1,0:T(8,128)} %constant.6.clone.table, bf16[2,8,320,512]{3,2,1,0:T(8,128)(2,1)} %state_hbm.5, bf16[2,8,320,512]{3,2,1,0:T(8,128)(2,1)} %collective-permute-done.near_all.near, ...), custom_call_target="tpu_custom_call" | custom-call | flops 3355443200 | bytes 41287680 | tf_op jit(solution)/shard_map/local_part/pallas_call | solution.py:197
  139.2 0.0 copy-done.1
  139.2 0.0 copy-done.10
  139.2 0.0 copy-done.11
  139.2 0.0 copy-start
  139.2 4.0 %copy-done = f32[2,8,320,512]{3,2,1,0:T(8,128)S(1)} copy-done((f32[2,8,320,512]{3,2,1,0:T(8,128)S(1)}, f32[2,8,320,512]{3,2,1,0:T(8,128)}, u32[]{:S(2)}) %copy-start) | copy-done | bytes 10485784
  143.2 0.0 copy-start.3
  143.2 1.5 copy-done.3
  144.7 0.0 copy-start.5
  144.7 1.3 copy-done.5
  146.0 0.0 copy-start.9
  146.0 1.1 copy-done.9
  147.1 0.0 slice-start
  147.1 5.0 %shard_map.94.rest_2_ = bf16[2,8,320,512]{3,2,1,0:T(8,128)(2,1)} custom-call(s32[1,4]{1,0:T(1,128)S(1)} %copy-done.10, s32[1,4]{1,0:T(1,128)S(1)} %copy-done.11, f32[2,8,320,512]{3,2,1,0:T(8,128)S(1)} %copy-done, f32[2,8,320,1]{3,2,1,0:T(8,128)S(1)} %copy-done.1, bf16[1,6,320,512]{3,2,1,0:T(8,128)(2,1)S(1)} %copy-done.3, ...), custom_call_target="tpu_custom_call" | custom-call | flops 26214400 | bytes 13107200 | tf_op jit(solution)/shard_map/pallas_call | solution.py:311
  152.1 0.0 collective-permute-done.8.rest_1_
  152.1 0.0 collective-permute-done.6.far
  152.1 0.0 copy-done.7
  152.2 6.1 %shard_map.95.rest_2_ = bf16[2,8,320,512]{3,2,1,0:T(8,128)(2,1)} custom-call(s32[1,4]{1,0:T(1,128)S(1)} %copy-done.10, s32[1,4]{1,0:T(1,128)S(1)} %copy-done.11, f32[2,8,320,512]{3,2,1,0:T(8,128)S(1)} %copy-done, f32[2,8,320,1]{3,2,1,0:T(8,128)S(1)} %copy-done.1, ...), custom_call_target="tpu_custom_call", output_to_operand_aliasing={{}: (7, {})} | custom-call | flops 20971520 | bytes 10485760 | tf_op jit(solution)/shard_map/pallas_call | solution.py:311
  158.2 0.0 collective-permute-done.4.rest_0_
  158.2 0.0 collective-permute-done.5.rest_1_
  158.2 0.0 collective-permute-done.3.far
  158.2 0.0 slice-done
  158.3 0.0 slice-done.1
  158.3 0.0 slice-done.2
  158.3 3.2 %shard_map.96 = bf16[2,8,320,512]{3,2,1,0:T(8,128)(2,1)} custom-call(s32[1,4]{1,0:T(1,128)S(1)} %copy-done.10, s32[1,4]{1,0:T(1,128)S(1)} %copy-done.11, f32[2,8,320,512]{3,2,1,0:T(8,128)S(1)} %bitcast.4, f32[2,8,320,1]{3,2,1,0:T(8,128)S(1)} %copy-done.1, bf16[1,6,64,512]{3,2,1,0:T(8,128)(2,1)} %collective-permute-done.3.far, ...), custom_call_target="tpu_custom_call", output_to_operand_aliasing={{}: (7, {})} | custom-call | flops 5242880 | bytes 2621440 | tf_op jit(solution)/shard_map/pallas_call | solution.py:311
  (4 shorter events, 0.0 us)
Async XLA Ops:
  0.0 9.2 %collective-permute-start = (bf16[2,8,320,512]{3,2,1,0:T(8,128)(2,1)}, bf16[2,8,320,512]{3,2,1,0:T(8,128)(2,1)}, u32[]{:S(2)}, u32[]{:S(2)}) collective-permute-start(bf16[2,8,320,512]{3,2,1,0:T(8,128)(2,1)} %state_hbm.5), channel_id=1, source_target_pairs={{0,1},{1,0},{2,3},{3,2},{4,5},{5,4},{6,7},{7,6},{8,9},{9,8},{10,11... | collective-permute-start | bytes 15728648 | tf_op jit(solution)/shard_map/ppermute | solution.py:351
  4.9 37.0 %collective-permute-start.1 = (bf16[2,2,320,512]{3,2,1,0:T(8,128)(2,1)}, bf16[2,2,320,512]{3,2,1,0:T(8,128)(2,1)}, u32[]{:S(2)}, u32[]{:S(2)}) collective-permute-start(bf16[2,2,320,512]{3,2,1,0:T(8,128)(2,1)} %get-tuple-element.16), channel_id=1, source_target_pairs={{0,2},{1,3},{2,0},{3,1},{4,6},{5,7},{6,4},{7,5},{8,10},{9,11},{10,... | collective-permute-start | bytes 3932168 | tf_op jit(solution)/shard_map/ppermute | solution.py:350
  7.5 29.7 %collective-permute-start.10 = (bf16[1,2,320,512]{3,2,1,0:T(8,128)(2,1)}, bf16[1,2,320,512]{3,2,1,0:T(8,128)(2,1)S(1)}, u32[]{:S(2)}, u32[]{:S(2)}) collective-permute-start(bf16[1,2,320,512]{3,2,1,0:T(8,128)(2,1)} %get-tuple-element.24), channel_id=1, source_target_pairs={{0,4},{4,8},{8,12},{12,16},{16,20},{20,24},{24,28},{28,0},{1,5},{5... | collective-permute-start | bytes 1966088 | tf_op jit(solution)/shard_map/ppermute | solution.py:349
  16.5 85.0 %collective-permute-start.9 = (bf16[1,6,320,512]{3,2,1,0:T(8,128)(2,1)}, bf16[1,6,320,512]{3,2,1,0:T(8,128)(2,1)S(1)}, u32[]{:S(2)}, u32[]{:S(2)}) collective-permute-start(bf16[1,6,320,512]{3,2,1,0:T(8,128)(2,1)} %get-tuple-element.23), channel_id=1, source_target_pairs={{0,2},{1,3},{2,0},{3,1},{4,6},{5,7},{6,4},{7,5},{8,10},{9,11},{10,... | collective-permute-start | bytes 5898248 | tf_op jit(solution)/shard_map/ppermute | solution.py:364
  27.8 71.5 %copy-start.12 = (f32[2,8,320]{2,1,0:T(8,128)S(1)}, f32[2,8,320]{2,1,0:T(8,128)}, u32[]{:S(2)}) copy-start(f32[2,8,320]{2,1,0:T(8,128)} %param.16) | copy-start | bytes 61444
  27.8 43.6 %collective-permute-start.11 = (bf16[1,2,320,512]{3,2,1,0:T(8,128)(2,1)}, bf16[1,2,320,512]{3,2,1,0:T(8,128)(2,1)S(1)}, u32[]{:S(2)}, u32[]{:S(2)}) collective-permute-start(bf16[1,2,320,512]{3,2,1,0:T(8,128)(2,1)} %get-tuple-element.25), channel_id=1, source_target_pairs={{0,4},{4,8},{8,12},{12,16},{16,20},{20,24},{24,28},{28,0},{1,5},{5... | collective-permute-start | bytes 1966088 | tf_op jit(solution)/shard_map/ppermute | solution.py:354
  37.2 55.9 %collective-permute-start.7 = (bf16[1,4,256,512]{3,2,1,0:T(8,128)(2,1)}, bf16[1,4,256,512]{3,2,1,0:T(8,128)(2,1)S(1)}, u32[]{:S(2)}, u32[]{:S(2)}) collective-permute-start(bf16[1,4,256,512]{3,2,1,0:T(8,128)(2,1)} %get-tuple-element.21), channel_id=1, source_target_pairs={{0,4},{4,8},{8,12},{12,16},{16,20},{20,24},{24,28},{28,0},{1,5},{5... | collective-permute-start | bytes 3145736 | tf_op jit(solution)/shard_map/ppermute | solution.py:367
  37.2 60.7 %collective-permute-start.12 = (bf16[1,4,320,512]{3,2,1,0:T(8,128)(2,1)}, bf16[1,4,320,512]{3,2,1,0:T(8,128)(2,1)S(1)}, u32[]{:S(2)}, u32[]{:S(2)}) collective-permute-start(bf16[1,4,320,512]{3,2,1,0:T(8,128)(2,1)} %get-tuple-element.26), channel_id=1, source_target_pairs={{4,0},{8,4},{12,8},{16,12},{20,16},{24,20},{28,24},{0,28},{5,1},{9... | collective-permute-start | bytes 3932168 | tf_op jit(solution)/shard_map/ppermute | solution.py:355
  41.9 59.6 %collective-permute-start.2 = (bf16[2,2,320,512]{3,2,1,0:T(8,128)(2,1)}, bf16[2,2,320,512]{3,2,1,0:T(8,128)(2,1)}, u32[]{:S(2)}, u32[]{:S(2)}) collective-permute-start(bf16[2,2,320,512]{3,2,1,0:T(8,128)(2,1)} %collective-permute-done.1.far_all), channel_id=1, source_target_pairs={{0,1},{1,0},{2,3},{3,2},{4,5},{5,4},{6,7},{7,6},{8,9},{9,8},{10,11... | collective-permute-start | bytes 3932168 | tf_op jit(solution)/shard_map/ppermute | solution.py:371
  71.4 0.8 copy-start.8
  72.2 79.9 %collective-permute-start.6 = (bf16[1,6,256,512]{3,2,1,0:T(8,128)(2,1)}, bf16[1,6,256,512]{3,2,1,0:T(8,128)(2,1)}, u32[]{:S(2)}, u32[]{:S(2)}) collective-permute-start(bf16[1,6,256,512]{3,2,1,0:T(8,128)(2,1)} %get-tuple-element.20), channel_id=1, source_target_pairs={{0,2},{1,3},{2,0},{3,1},{4,6},{5,7},{6,4},{7,5},{8,10},{9,11},{10,... | collective-permute-start | bytes 4718600 | tf_op jit(solution)/shard_map/ppermute | solution.py:365
  93.1 1.0 copy-start.6
  94.0 58.1 %collective-permute-start.8 = (bf16[1,4,256,512]{3,2,1,0:T(8,128)(2,1)}, bf16[1,4,256,512]{3,2,1,0:T(8,128)(2,1)}, u32[]{:S(2)}, u32[]{:S(2)}) collective-permute-start(bf16[1,4,256,512]{3,2,1,0:T(8,128)(2,1)} %get-tuple-element.22), channel_id=1, source_target_pairs={{4,0},{8,4},{12,8},{16,12},{20,16},{24,20},{28,24},{0,28},{5,1},{9... | collective-permute-start | bytes 3145736 | tf_op jit(solution)/shard_map/ppermute | solution.py:368
  97.9 1.1 copy-start.4
  99.0 59.2 %collective-permute-start.3 = (bf16[1,6,64,512]{3,2,1,0:T(8,128)(2,1)}, bf16[1,6,64,512]{3,2,1,0:T(8,128)(2,1)}, u32[]{:S(2)}, u32[]{:S(2)}) collective-permute-start(bf16[1,6,64,512]{3,2,1,0:T(8,128)(2,1)} %get-tuple-element.17), channel_id=1, source_target_pairs={{0,2},{1,3},{2,0},{3,1},{4,6},{5,7},{6,4},{7,5},{8,10},{9,11},{10,... | collective-permute-start | bytes 1179656 | tf_op jit(solution)/shard_map/ppermute | solution.py:366
  101.6 56.7 %collective-permute-start.4 = (bf16[1,4,64,512]{3,2,1,0:T(8,128)(2,1)}, bf16[1,4,64,512]{3,2,1,0:T(8,128)(2,1)S(1)}, u32[]{:S(2)}, u32[]{:S(2)}) collective-permute-start(bf16[1,4,64,512]{3,2,1,0:T(8,128)(2,1)} %get-tuple-element.18), channel_id=1, source_target_pairs={{0,4},{4,8},{8,12},{12,16},{16,20},{20,24},{24,28},{28,0},{1,5},{5... | collective-permute-start | bytes 786440 | tf_op jit(solution)/shard_map/ppermute | solution.py:369
  101.6 1.3 copy-start.2
  102.9 36.3 %copy-start.1 = (f32[2,8,320,1]{3,2,1,0:T(8,128)S(1)}, f32[2,8,320,1]{3,2,1,0:T(8,128)}, u32[]{:S(2)}) copy-start(f32[2,8,320,1]{3,2,1,0:T(8,128)} %copy.12.step) | copy-start | bytes 61444
  102.9 36.3 %copy-start.10 = (s32[1,4]{1,0:T(1,128)S(1)}, s32[1,4]{1,0:T(1,128)}, u32[]{:S(2)}) copy-start(s32[1,4]{1,0:T(1,128)} %left.5) | copy-start | bytes 52
  102.9 36.3 %copy-start.11 = (s32[1,4]{1,0:T(1,128)S(1)}, s32[1,4]{1,0:T(1,128)}, u32[]{:S(2)}) copy-start(s32[1,4]{1,0:T(1,128)} %right.5) | copy-start | bytes 52
  102.9 55.3 %collective-permute-start.5 = (bf16[1,4,64,512]{3,2,1,0:T(8,128)(2,1)}, bf16[1,4,64,512]{3,2,1,0:T(8,128)(2,1)}, u32[]{:S(2)}, u32[]{:S(2)}) collective-permute-start(bf16[1,4,64,512]{3,2,1,0:T(8,128)(2,1)} %get-tuple-element.19), channel_id=1, source_target_pairs={{4,0},{8,4},{12,8},{16,12},{20,16},{24,20},{28,24},{0,28},{5,1},{9... | collective-permute-start | bytes 786440 | tf_op jit(solution)/shard_map/ppermute | solution.py:370
  139.2 4.0 %copy-start = (f32[2,8,320,512]{3,2,1,0:T(8,128)S(1)}, f32[2,8,320,512]{3,2,1,0:T(8,128)}, u32[]{:S(2)}) copy-start(f32[2,8,320,512]{3,2,1,0:T(8,128)} %local_part.1.base) | copy-start | bytes 31457284
  143.2 1.5 copy-start.3
  144.7 1.3 copy-start.5
  146.0 1.1 copy-start.9
  147.1 5.0 %copy-start.7 = (bf16[1,4,256,512]{3,2,1,0:T(8,128)(2,1)S(1)}, bf16[1,4,256,512]{3,2,1,0:T(8,128)(2,1)}, u32[]{:S(2)}) copy-start(bf16[1,4,256,512]{3,2,1,0:T(8,128)(2,1)} %copy-done.6) | copy-start | bytes 3145732
  147.1 11.1 %slice-start = ((s8[10485760]{0:T(1024)(128)(4,1)}), s8[2097152]{0:T(1024)(128)(4,1)S(1)}, s32[]{:S(2)}) async-start(s8[10485760]{0:T(1024)(128)(4,1)} %bitcast.3), calls=%async_computation | async-start | bytes 4194304
  147.1 11.1 %slice-start.1 = ((s8[10485760]{0:T(1024)(128)(4,1)}), s8[4194304]{0:T(1024)(128)(4,1)S(1)}, s32[]{:S(2)}) async-start(s8[10485760]{0:T(1024)(128)(4,1)} %bitcast.3), calls=%async_computation.1 | async-start | bytes 8388608
  152.1 6.1 %slice-start.2 = ((s8[10485760]{0:T(1024)(128)(4,1)}), s8[4194304]{0:T(1024)(128)(4,1)S(1)}, s32[]{:S(2)}) async-start(s8[10485760]{0:T(1024)(128)(4,1)} %bitcast.3), calls=%async_computation.2 | async-start | bytes 8388608

commit v2 on v1

v2 whole, which is shorter than its diff:
```python
import functools
import math

import jax
import jax.numpy as jnp
from jax import lax
from jax.experimental import pallas as pl
from jax.experimental.pallas import tpu as pltpu
from jax.sharding import PartitionSpec as P


ANY = pl.BlockSpec(memory_space=pl.ANY)
SMEM = pl.BlockSpec(memory_space=pltpu.SMEM)
SLOTS = 3


def time_table(count):
    table = []
    for first in range(count):
        row_values = []
        for second in range(count):
            if first != second:
                delta = first - second
                parity = 1.0 - 2.0 * (delta % 2)
                row_values.append(0.5 * parity / math.tan(math.pi * delta / count))
            else:
                row_values.append(0.0)
        table.append(row_values)
    return table


def transposed_product(jacobian, state):
    return lax.dot_general(
        jacobian, state, (((0,), (0,)), ((), ())), preferred_element_type=jnp.float32
    )


def parity():
    return lax.rem(lax.axis_index("space"), 2)


def remote_kernel(inst, iface, ranges, pieces, first, codes_hbm, state_hbm, off_hbm, *rest):
    outs, rest = rest[: len(pieces)], rest[len(pieces) :]
    if first:
        passed_hbm, *rest = rest
        *rest, passed, read_sem, write_sem = rest
    codes, code_sem, acc, states, jacobians, picked, places, *rest = rest
    state_sem, off_sem, ready, out_sem = rest
    load_codes = pltpu.make_async_copy(codes_hbm, codes, code_sem)
    load_codes.start()
    if first:
        source = state_hbm.at[:, pl.ds(0, first)]
        pltpu.make_async_copy(source, passed, read_sem).start()
    blocks = codes.shape[1]
    odd = parity()
    lows = (blocks + iface * (1 - odd), blocks + iface * odd)
    acc[...] = jnp.zeros_like(acc)
    load_codes.wait()

    def scan(term, found):
        code = codes[lax.div(term, blocks), lax.rem(term, blocks)]
        hits, place, base = 0, 0, 0
        for kind, offset, count in ranges:
            at = code - (lows[kind] + offset)
            inside = (at >= 0) & (at < count)
            place = jnp.where(inside, at + base, place)
            hits = jnp.where(inside, 1, hits)
            base += count
        picked[found] = term
        places[found] = place
        return found + hits

    found = lax.fori_loop(0, codes.shape[0] * blocks, scan, jnp.int32(0))

    def copies(index):
        slot = lax.rem(index, SLOTS)
        term = picked[index]
        row = lax.rem(term, blocks)
        return (
            pltpu.make_async_copy(state_hbm.at[inst, row], states.at[slot], state_sem.at[slot]),
            pltpu.make_async_copy(
                off_hbm.at[inst, row, lax.div(term, blocks)], jacobians.at[slot], off_sem.at[slot]
            ),
        )

    for ahead in range(SLOTS - 1):

        @pl.when(ahead < found)
        def _():
            for copy in copies(jnp.int32(ahead)):
                copy.start()

    def one(index, carry):
        @pl.when(index + SLOTS - 1 < found)
        def _():
            for copy in copies(index + SLOTS - 1):
                copy.start()

        for copy in copies(index):
            copy.wait()
        slot = lax.rem(index, SLOTS)
        term = transposed_product(jacobians[slot], states[slot]).astype(jnp.bfloat16)
        acc[places[index]] += term.astype(jnp.float32)
        return carry

    if first:
        pltpu.make_async_copy(source, passed, read_sem).wait()
        write = pltpu.make_async_copy(passed, passed_hbm, write_sem)
        write.start()
    lax.fori_loop(0, found, one, 0)
    writes = []
    for slot in range(acc.shape[0]):
        ready[slot] = acc[slot].astype(jnp.bfloat16)
        for out, (slot_low, slot_high, row_low, row_high) in zip(outs, pieces):
            if slot_low <= slot < slot_high:
                piece = ready.at[slot, pl.ds(row_low, row_high - row_low)]
                copy = pltpu.make_async_copy(
                    piece, out.at[0, slot - slot_low], out_sem.at[len(writes)]
                )
                copy.start()
                writes.append(copy)
    for copy in writes:
        copy.wait()
    if first:
        write.wait()


def remote_terms(inst, iface, ranges, pieces, codes, adjoint, off, first=0):
    insts, blocks, dof, wide = adjoint.shape
    couple = off.shape[2]
    shapes = [
        jax.ShapeDtypeStruct((1, b - a, d - c, wide), jnp.bfloat16) for a, b, c, d in pieces
    ]
    out_specs = [ANY] * len(pieces)
    extra = []
    if first:
        passed = (insts, first, dof, wide)
        shapes.append(jax.ShapeDtypeStruct(passed, jnp.bfloat16))
        out_specs.append(ANY)
        extra = [
            pltpu.VMEM(passed, jnp.bfloat16),
            pltpu.SemaphoreType.DMA(()),
            pltpu.SemaphoreType.DMA(()),
        ]
    work = sum(count for _, _, count in ranges)
    return pl.pallas_call(
        functools.partial(remote_kernel, inst, iface, ranges, pieces, first),
        out_shape=shapes,
        in_specs=[ANY, ANY, ANY],
        out_specs=out_specs,
        scratch_shapes=[
            pltpu.SMEM((couple, blocks), jnp.int32),
            pltpu.SemaphoreType.DMA(()),
            pltpu.VMEM((work, dof, wide), jnp.float32),
            pltpu.VMEM((SLOTS, dof, wide), jnp.bfloat16),
            pltpu.VMEM((SLOTS, dof, dof), jnp.bfloat16),
            pltpu.SMEM((couple * blocks + 1,), jnp.int32),
            pltpu.SMEM((couple * blocks + 1,), jnp.int32),
            pltpu.SemaphoreType.DMA((SLOTS,)),
            pltpu.SemaphoreType.DMA((SLOTS,)),
            pltpu.VMEM((work, dof, wide), jnp.bfloat16),
            pltpu.SemaphoreType.DMA((sum(b - a for a, b, _, _ in pieces),)),
            *extra,
        ],
        cost_estimate=pl.CostEstimate(
            flops=2 * work * dof * dof * wide,
            bytes_accessed=work * 2 * dof * (dof + wide),
            transcendentals=0,
        ),
    )(codes, adjoint, off)


def local_kernel(
    inst, insts, couple, first, codes, here, table, left, right, adj_all, near_all, far_all,
    relay_all, arrived, state, diag, off, grad, step, base, acc,
):
    row = pl.program_id(0)
    blocks = pl.num_programs(0)

    @pl.when(row == 0)
    def _():
        acc[...] = jnp.zeros_like(acc)

    acc[row] += transposed_product(diag[0, 0], state[0, 0])
    for slot in range(couple):
        code = codes[slot, row]

        @pl.when(code < blocks)
        def _():
            term = transposed_product(off[0, 0, slot], state[0, 0]).astype(jnp.bfloat16)
            acc[code] += term.astype(jnp.float32)

    @pl.when(row == blocks - 1)
    def _():
        odd = parity()
        for slot in range(arrived.shape[1]):
            block = jnp.where(odd == 0, left[0, slot], right[0, slot])
            acc[block] += arrived[0, slot].astype(jnp.float32)

        def mix(total, block, sources, at):
            for index, source in enumerate(sources):
                for other in range(insts):
                    sender = here[0] ^ (at + index)
                    weight = table[sender * insts + other, here[0] * insts + inst]
                    total += weight * source[other, block].astype(jnp.float32)
            return total

        def finish(block, carry):
            total = acc[block] - grad[0, block].astype(jnp.float32)
            total = mix(total, block, (adj_all, near_all), 0)
            mine = adj_all[inst, block].astype(jnp.float32)
            base[0, block] = mine - step[0, block] * total
            return carry

        def finish_far(block, carry):
            total = mix(jnp.zeros(acc.shape[1:], jnp.float32), block, (far_all, relay_all), 2)
            base[0, block] -= step[0, block] * total
            return carry

        lax.fori_loop(0, base.shape[1], finish, 0)
        lax.fori_loop(0, first, finish_far, 0)


def local_part(
    inst, codes, here, table, left, right, adjoint, near, far, relay, arrived, diag, off, grad, step
):
    insts, blocks, dof, wide = adjoint.shape
    couple = off.shape[2]
    first = far.shape[1]

    def whole(x):
        return pl.BlockSpec(x.shape, lambda r: (0, 0, 0, 0), pipeline_mode=pl.Buffered(1))

    return pl.pallas_call(
        functools.partial(local_kernel, inst, insts, couple, first),
        grid=(blocks,),
        out_shape=jax.ShapeDtypeStruct((1, blocks, dof, wide), jnp.float32),
        in_specs=[
            SMEM,
            SMEM,
            SMEM,
            SMEM,
            SMEM,
            whole(adjoint),
            whole(near),
            whole(far),
            whole(relay),
            whole(arrived),
            pl.BlockSpec((1, 1, dof, wide), lambda r: (inst, r, 0, 0)),
            pl.BlockSpec((1, 1, dof, dof), lambda r: (inst, r, 0, 0)),
            pl.BlockSpec((1, 1, couple, dof, dof), lambda r: (inst, r, 0, 0, 0)),
            pl.BlockSpec((1, blocks, dof, wide), lambda r: (inst, 0, 0, 0)),
            pl.BlockSpec((1, blocks, dof, 1), lambda r: (inst, 0, 0, 0)),
        ],
        out_specs=pl.BlockSpec((1, blocks, dof, wide), lambda r: (0, 0, 0, 0)),
        scratch_shapes=[pltpu.VMEM((blocks, dof, wide), jnp.float32)],
        cost_estimate=pl.CostEstimate(
            flops=4 * blocks * dof * dof * wide,
            bytes_accessed=blocks * dof * (6 * dof + 12 * wide),
            transcendentals=0,
        ),
    )(
        codes, here, table, left, right, adjoint, near, far, relay, arrived, adjoint, diag, off,
        grad, step,
    )


def mix_kernel(insts, pieces, here, table, own, near, *outs):
    for inst in range(insts):
        total = None
        for index, source in enumerate((own, near)):
            for other in range(insts):
                sender, target = here[0] ^ index, here[0] ^ 2
                weight = table[sender * insts + other, target * insts + inst]
                term = weight * source[other, 0].astype(jnp.float32)
                total = term if total is None else total + term
        total = total.astype(jnp.bfloat16)
        for out, (which, low, high) in zip(outs, pieces):
            if which == inst:
                out[0, 0] = total[low:high]


def mix(here, table, adjoint, near, first, pieces):
    insts, blocks, dof, wide = adjoint.shape
    state = pl.BlockSpec((insts, 1, dof, wide), lambda r: (0, r + first, 0, 0))
    count = blocks - first
    return pl.pallas_call(
        functools.partial(mix_kernel, insts, pieces),
        grid=(count,),
        out_shape=[
            jax.ShapeDtypeStruct((1, count, high - low, wide), jnp.bfloat16)
            for _, low, high in pieces
        ],
        in_specs=[SMEM, SMEM, state, state],
        out_specs=[
            pl.BlockSpec((1, 1, high - low, wide), lambda r: (0, r, 0, 0))
            for _, low, high in pieces
        ],
        cost_estimate=pl.CostEstimate(
            flops=8 * insts * count * dof * wide,
            bytes_accessed=6 * insts * count * dof * wide,
            transcendentals=0,
        ),
        name="mix",
    )(here, table, adjoint, near)


def final_kernel(where, group, first, offsets, left, right, base, step, far, *rest):
    arrivals = rest[: len(offsets)]
    if where is None:
        out, total = rest[-2:]
    else:
        out_hbm, total, out, out_sem = rest[-4:]
        inst, row_low, rows = where
    start = pl.program_id(0) * group
    odd = parity()
    slots = [(x, s, offset + s) for x, offset in zip(arrivals, offsets) for s in range(x.shape[1])]

    def one(inner, carry):
        block = start + inner
        place = 0 if group == 1 else jnp.maximum(block - first, 0)
        chosen = [jnp.where(odd == 0, right[0, s], left[0, s]) == block for _, _, s in slots]
        touched = functools.reduce(jnp.logical_or, chosen)
        late = block >= first

        def put(value):
            out[0, inner] = (base[0, inner] - step[0, inner] * value).astype(jnp.bfloat16)

        @pl.when(late & ~touched)
        def _():
            put(far[0, place].astype(jnp.float32))

        @pl.when(~late & ~touched)
        def _():
            out[0, inner] = base[0, inner].astype(jnp.bfloat16)

        @pl.when(touched)
        def _():
            total[...] = jnp.where(late, far[0, place].astype(jnp.float32), 0.0)
            for (arrived, slot, _), hit in zip(slots, chosen):

                @pl.when(hit)
                def _():
                    total[...] += arrived[0, slot].astype(jnp.float32)

            put(total[...])

        if where is not None:
            write(block).start()
        return carry

    def write(block):
        target = out_hbm.at[inst, block, pl.ds(row_low, rows)]
        return pltpu.make_async_copy(out.at[0, block], target, out_sem.at[block])

    lax.fori_loop(0, group, one, 0)
    if where is not None:
        for block in range(group):
            write(block).wait()


def final_part(inst, row_low, row_high, group, left, right, base, step, far, arrivals, out, limit):
    insts = step.shape[0]
    _, blocks, dof, wide = base.shape
    rows = row_high - row_low
    at = row_low // rows
    first = blocks - far.shape[1]
    state = pl.BlockSpec((1, group, rows, wide), lambda g: (inst, g, at, 0))
    whole = lambda x: pl.BlockSpec(x.shape, lambda g: (0, 0, 0, 0), pipeline_mode=pl.Buffered(1))
    terms = [x for _, x in arrivals]
    operands = [left, right, base, step, far, *terms]
    specs = [
        SMEM,
        SMEM,
        pl.BlockSpec((1, group, rows, wide), lambda g: (0, g, at, 0)),
        pl.BlockSpec((1, group, rows, 1), lambda g: (inst, g, at, 0)),
        whole(far)
        if group > 1
        else pl.BlockSpec((1, 1, rows, wide), lambda g: (0, jnp.maximum(g - first, 0), 0, 0)),
        *[whole(x) for x in terms],
    ]
    last = group == blocks
    scratch = [pltpu.VMEM((rows, wide), jnp.float32)]
    if last:
        scratch.append(pltpu.VMEM((1, blocks, rows, wide), jnp.bfloat16))
        scratch.append(pltpu.SemaphoreType.DMA((blocks,)))
    aliases = {}
    if out is not None:
        aliases = {len(operands): 0}
        operands.append(out)
        specs.append(ANY)
    return pl.pallas_call(
        functools.partial(
            final_kernel,
            (inst, row_low, rows) if last else None,
            group,
            first,
            [offset for offset, _ in arrivals],
        ),
        grid=(blocks // group,),
        out_shape=jax.ShapeDtypeStruct((insts, blocks, dof, wide), jnp.bfloat16),
        in_specs=specs,
        out_specs=ANY if last else state,
        scratch_shapes=scratch,
        input_output_aliases=aliases,
        cost_estimate=pl.CostEstimate(
            flops=20 * blocks * rows * wide,
            bytes_accessed=10 * blocks * rows * wide,
            transcendentals=0,
        ),
        compiler_params=pltpu.CompilerParams(vmem_limit_bytes=limit << 20),
    )(*operands)


def per_device(adjoint, diag, off, off_columns, left, right, grad, step):
    insts, blocks, dof, _ = adjoint.shape
    iface = left.shape[1]
    parts, times = lax.axis_size("space"), lax.axis_size("tm")
    if times != 4 or insts != 2 or parts % 2:
        raise ValueError("unsupported mesh")
    instances = insts * times
    here = lax.axis_index("tm").astype(jnp.int32)[None]
    table = jnp.asarray(time_table(instances), dtype=jnp.float32)
    swap_core = [(i, i ^ 1) for i in range(times)]
    swap_chip = [(i, i ^ 2) for i in range(times)]
    pair = [(i, i ^ 1) for i in range(parts)]
    other = [(i, (i + 2 * (i % 2) - 1) % parts) for i in range(parts)]
    codes = off_columns.T
    cut, first, half = 256, 2, iface // 2

    ranges, pieces = [(0, half, iface - half)], [(0, iface - half, 0, dof)]
    pair0a, passed = remote_terms(0, iface, ranges, pieces, codes, adjoint, off, first)
    far0 = lax.ppermute(passed, "tm", swap_chip)
    from_pair0a = lax.ppermute(pair0a, "space", pair)
    near = lax.ppermute(adjoint, "tm", swap_core)
    ranges = [(1, 0, iface), (0, 0, half)]
    pieces = [(0, iface, 0, dof), (iface, iface + half, 0, dof)]
    other0, pair0b = remote_terms(0, iface, ranges, pieces, codes, adjoint, off)
    from_other0 = lax.ppermute(other0, "space", other)
    from_pair0b = lax.ppermute(pair0b, "space", pair)
    mixed = mix(here, table, adjoint, near, first, [(0, 0, dof), (1, 0, cut), (1, cut, dof)])
    far1 = lax.ppermute(mixed[0], "tm", swap_chip)
    far2a = lax.ppermute(mixed[1], "tm", swap_chip)
    far2b = lax.ppermute(mixed[2], "tm", swap_chip)
    ranges = [(1, 0, iface), (0, 0, iface)]
    pieces = [(0, iface, 0, dof), (iface, 2 * iface, 0, cut), (iface, 2 * iface, cut, dof)]
    other1, pair1a, pair1b = remote_terms(1, iface, ranges, pieces, codes, adjoint, off)
    from_other1 = lax.ppermute(other1, "space", other)
    from_pair1a = lax.ppermute(pair1a, "space", pair)
    from_pair1b = lax.ppermute(pair1b, "space", pair)
    relay = lax.ppermute(far0, "tm", swap_core)
    step = step[..., None]
    common = (codes, here, table, left, right, adjoint, near, far0, relay)
    base0 = local_part(0, *common, from_other0, diag, off, grad, step)
    base1 = local_part(1, *common, from_other1, diag, off, grad, step)
    faces = (left, right)
    arrivals = [(half, from_pair0a), (0, from_pair0b)]
    out = final_part(0, 0, dof, 2, *faces, base0, step, far1, arrivals, None, 16)
    out = final_part(1, 0, cut, 4, *faces, base1, step, far2a, [(0, from_pair1a)], out, 20)
    arrivals = [(0, from_pair1b)]
    return final_part(1, cut, dof, blocks, *faces, base1, step, far2b, arrivals, out, 12)


def solution(mesh):
    in_specs = (
        P("tm", "space", None, None),
        P("tm", "space", None, None),
        P("tm", "space", None, None, None),
        P("space", None),
        P("space", None),
        P("space", None),
        P("tm", "space", None, None),
        P("tm", "space", None),
    )
    out_specs = P("tm", "space", None, None)
    return jax.shard_map(
        per_device, mesh=mesh, in_specs=in_specs, out_specs=out_specs, check_vma=False
    )
```

time: 162 us -> 167 us (1.031)
  waiting for transfers between devices: 50.7 us -> 65.8 us
  local copies, waits for them, and re-layouts: 14.4 us -> 5.98 us
  starting transfers between devices: 20.8 us -> 13.3 us
  Pallas kernels: 75.3 us -> 80.1 us
    ppermute x7 -> x6, waiting for transfers between devices: 50.7 us -> 65.8 us  [the longest x1 39.1 us: per_device(): from_pair0a = lax.ppermute(pair0a, 'space', pair)]
    unnamed x32 -> x18, local copies, waits for them, and re-layouts: 12.1 us -> 3.6 us
    ppermute x7 -> x6, starting transfers between devices: 14.8 us -> 7.63 us  [the longest x1 2.04 us: per_device(): from_other1 = lax.ppermute(other1, 'space', other)]
    pallas_call x7 -> x8, Pallas kernels: 68 us -> 72.7 us  [the longest x2 39.5 us: local_part(): pl.pallas_call(functools.partial(local_kernel, inst, insts, couple, first...]
    ppermute x1, starting transfers between devices: 2.75 us -> 0.54 us  [per_device(): far1 = lax.ppermute(mixed[0], 'tm', swap_chip)]
  transfers between devices with their start and end apart: 13 -> 12, of which waited for: 3 -> 2; matrix products, arithmetic and copies ran while one was open for 1% -> 1% of each run, Pallas kernels for 45% -> 47%
where the time goes in v2:
time: 167 us; the launch traced here: 165 us
  Pallas kernels  80.1 us (48%)
  waiting for transfers between devices  65.8 us (39%)
  starting transfers between devices  13.3 us (8%)
  local copies, waits for them, and re-layouts  5.98 us (4%)
    pallas_call x2, Pallas kernels, local_part(): pl.pallas_call(functools.partial(local_kernel, inst, insts, couple, first...  39.5 us
    ppermute x1, waiting for transfers between devices, per_device(): from_pair0a = lax.ppermute(pair0a, 'space', pair)  39.1 us
    ppermute x1, waiting for transfers between devices, per_device(): from_pair0b = lax.ppermute(pair0b, 'space', pair)  26.7 us
    pallas_call x3, Pallas kernels, remote_terms(): pl.pallas_call(functools.partial(remote_kernel, inst, iface, ranges, piec...  21.4 us
    pallas_call x3, Pallas kernels, final_part(): pl.pallas_call(functools.partial(final_kernel, (inst, row_low, rows) if l...  11.9 us
    pallas_call x1, Pallas kernels, mix(): pl.pallas_call(functools.partial(mix_kernel, insts, pieces), grid=(count,...  7.34 us
    unnamed x18, local copies, waits for them, and re-layouts  3.6 us
  transfers between devices with their start and end apart: 12, of which 2 were waited for; matrix products, arithmetic and copies ran while one was open for 1% of the time, Pallas kernels for 47%

profile of v2, /device:TPU:0, one launch (start us, length us, event | category | flops | bytes accessed | tf_op | source)
XLA Modules:
  0.0 165.3 jit_solution(11864696824602627792)
XLA Ops:
  0.0 0.5 collective-permute-start
  0.5 3.4 %shard_map.91 = (bf16[1,2,320,512]{3,2,1,0:T(8,128)(2,1)}, bf16[2,2,320,512]{3,2,1,0:T(8,128)(2,1)}) custom-call(s32[2,8]{1,0:T(2,128)} %bitcast.3, bf16[2,8,320,512]{3,2,1,0:T(8,128)(2,1)} %state.3, bf16[2,8,2,320,320]{4,3,2,1,0:T(8,128)(2,1)} %off.3), custom_call_target="tpu_custom_call" | custom-call | flops 209715200 | bytes 1064960 | tf_op jit(solution)/shard_map/pallas_call | solution.py:146
  3.9 2.6 %collective-permute-start.1 = (bf16[2,2,320,512]{3,2,1,0:T(8,128)(2,1)}, bf16[2,2,320,512]{3,2,1,0:T(8,128)(2,1)S(1)}, u32[]{:S(2)}, u32[]{:S(2)}) collective-permute-start(bf16[2,2,320,512]{3,2,1,0:T(8,128)(2,1)} %get-tuple-element.15), channel_id=1, source_target_pairs={{0,2},{1,3},{2,0},{3,1},{4,6},{5,7},{6,4},{7,5},{8,10},{9,11},{10,... | collective-permute-start | bytes 3932168 | tf_op jit(solution)/shard_map/ppermute | solution.py:433
  6.5 8.7 %shard_map.94 = (bf16[1,4,320,512]{3,2,1,0:T(8,128)(2,1)}, bf16[1,2,320,512]{3,2,1,0:T(8,128)(2,1)}) custom-call(s32[2,8]{1,0:T(2,128)} %bitcast.4, bf16[2,8,320,512]{3,2,1,0:T(8,128)(2,1)} %state.3, bf16[2,8,2,320,320]{4,3,2,1,0:T(8,128)(2,1)} %off.3), custom_call_target="tpu_custom_call" | custom-call | flops 629145600 | bytes 3194880 | tf_op jit(solution)/shard_map/pallas_call | solution.py:146
  15.2 1.6 collective-permute-start.8
  16.8 0.0 collective-permute-start.11
  16.8 2.0 %collective-permute-start.10 = (bf16[1,2,320,512]{3,2,1,0:T(8,128)(2,1)}, bf16[1,2,320,512]{3,2,1,0:T(8,128)(2,1)S(1)}, u32[]{:S(2)}, u32[]{:S(2)}) collective-permute-start(bf16[1,2,320,512]{3,2,1,0:T(8,128)(2,1)} %get-tuple-element.23), channel_id=1, source_target_pairs={{0,4},{4,0},{8,12},{12,8},{16,20},{20,16},{24,28},{28,24},{1,5},{5... | collective-permute-start | bytes 1966088 | tf_op jit(solution)/shard_map/ppermute | solution.py:434
  18.8 0.0 collective-permute-done.near_all.near
  18.8 7.3 %mix.1 = (bf16[1,6,320,512]{3,2,1,0:T(8,128)(2,1)}, bf16[1,6,256,512]{3,2,1,0:T(8,128)(2,1)}, bf16[1,6,64,512]{3,2,1,0:T(8,128)(2,1)}) custom-call(s32[1]{0:T(128)} %bitcast.1.here, f32[8,8]{1,0:T(8,128)} %constant.6.clone.table, bf16[2,8,320,512]{3,2,1,0:T(8,128)(2,1)} %state.3, bf16[2,8,320,512]{3,2,1,0:T(8,128)(2,1)} %collective-permute-done.near_all.near), custom_call_target="tpu_custom_call" | custom-call | flops 15728640 | bytes 11796480 | tf_op jit(solution)/shard_map/mix/pallas_call | solution.py:287
  26.1 0.0 copy-start.8
  26.1 0.5 collective-permute-start.9
  26.7 9.3 %shard_map.92 = (bf16[1,4,320,512]{3,2,1,0:T(8,128)(2,1)}, bf16[1,4,256,512]{3,2,1,0:T(8,128)(2,1)}, bf16[1,4,64,512]{3,2,1,0:T(8,128)(2,1)}) custom-call(s32[2,8]{1,0:T(2,128)} %bitcast.5, bf16[2,8,320,512]{3,2,1,0:T(8,128)(2,1)} %state.3, bf16[2,8,2,320,320]{4,3,2,1,0:T(8,128)(2,1)} %off.3), custom_call_target="tpu_custom_call" | custom-call | flops 838860800 | bytes 4259840 | tf_op jit(solution)/shard_map/pallas_call | solution.py:146
  36.0 26.7 %collective-permute-done.11.rest_1_ = bf16[1,2,320,512]{3,2,1,0:T(8,128)(2,1)S(1)} collective-permute-done((bf16[1,2,320,512]{3,2,1,0:T(8,128)(2,1)}, bf16[1,2,320,512]{3,2,1,0:T(8,128)(2,1)S(1)}, u32[]{:S(2)}, u32[]{:S(2)}) %collective-permute-start.11) | collective-permute-done | bytes 655392 | tf_op jit(solution)/shard_map/ppermute | solution.py:440
  62.7 2.0 %collective-permute-start.3 = (bf16[1,4,320,512]{3,2,1,0:T(8,128)(2,1)}, bf16[1,4,320,512]{3,2,1,0:T(8,128)(2,1)}, u32[]{:S(2)}, u32[]{:S(2)}) collective-permute-start(bf16[1,4,320,512]{3,2,1,0:T(8,128)(2,1)} %get-tuple-element.16), channel_id=1, source_target_pairs={{0,28},{4,8},{8,4},{12,16},{16,12},{20,24},{24,20},{28,0},{1,29},{... | collective-permute-start | bytes 3932168 | tf_op jit(solution)/shard_map/ppermute | solution.py:448
  64.7 0.0 collective-permute-done.1.far_all
  64.7 0.0 copy-start.7
  64.7 0.0 collective-permute-start.2
  64.7 39.1 %collective-permute-done.10.rest_0_ = bf16[1,2,320,512]{3,2,1,0:T(8,128)(2,1)S(1)} collective-permute-done((bf16[1,2,320,512]{3,2,1,0:T(8,128)(2,1)}, bf16[1,2,320,512]{3,2,1,0:T(8,128)(2,1)S(1)}, u32[]{:S(2)}, u32[]{:S(2)}) %collective-permute-start.10) | collective-permute-done | bytes 655392 | tf_op jit(solution)/shard_map/ppermute | solution.py:434
  103.8 0.0 copy-start.3
  103.8 0.5 collective-permute-start.6
  104.3 0.0 collective-permute-done.8.arrived
  104.3 0.0 collective-permute-start.7
  104.3 0.0 collective-permute-done.3.arrived
  104.3 1.6 collective-permute-start.4
  105.9 0.0 copy-done.8
  105.9 2.4 %copy.12.step = f32[2,8,320,1]{3,2,1,0:T(8,128)} copy(f32[2,8,320,1]{2,1,0,3:T(8,128)S(1)} %bitcast.8) | data formatting | bytes 40960 | tf_op jit(solution)/shard_map/broadcast_in_dim | solution.py:452
  108.3 0.0 collective-permute-done.2.relay_all
  108.3 2.0 %collective-permute-start.5 = (bf16[1,4,64,512]{3,2,1,0:T(8,128)(2,1)}, bf16[1,4,64,512]{3,2,1,0:T(8,128)(2,1)S(1)}, u32[]{:S(2)}, u32[]{:S(2)}) collective-permute-start(bf16[1,4,64,512]{3,2,1,0:T(8,128)(2,1)} %get-tuple-element.18), channel_id=1, source_target_pairs={{0,4},{4,0},{8,12},{12,8},{16,20},{20,16},{24,28},{28,24},{1,5},{5... | collective-permute-start | bytes 786440 | tf_op jit(solution)/shard_map/ppermute | solution.py:450
  110.2 0.0 copy-done.7
  110.2 0.0 copy-done.3
  110.2 19.7 %shard_map.93.base = f32[1,8,320,512]{3,2,1,0:T(8,128)} custom-call(s32[2,8]{1,0:T(2,128)} %bitcast.6, s32[1]{0:T(128)} %bitcast.1.here, f32[8,8]{1,0:T(8,128)} %constant.6.clone.table, s32[1,4]{1,0:T(1,128)} %left.9, s32[1,4]{1,0:T(1,128)} %right.9, bf16[2,8,320,512]{3,2,1,0:T(8,128)(2,1)} %state.3, ...), custom_call_target="tpu_custom_call" | custom-call | flops 1677721600 | bytes 20643840 | tf_op jit(solution)/shard_map/pallas_call | solution.py:234
  129.9 0.0 copy-start
  129.9 0.0 copy-start.5
  129.9 0.0 copy-start.6
  130.0 19.8 %shard_map.95.base = f32[1,8,320,512]{3,2,1,0:T(8,128)} custom-call(s32[2,8]{1,0:T(2,128)} %bitcast.7, s32[1]{0:T(128)} %bitcast.1.here, f32[8,8]{1,0:T(8,128)} %constant.6.clone.table, s32[1,4]{1,0:T(1,128)} %left.9, s32[1,4]{1,0:T(1,128)} %right.9, bf16[2,8,320,512]{3,2,1,0:T(8,128)(2,1)} %state.3, ...), custom_call_target="tpu_custom_call" | custom-call | flops 1677721600 | bytes 20643840 | tf_op jit(solution)/shard_map/pallas_call | solution.py:234
  149.8 0.0 collective-permute-done.9.far
  149.8 0.0 copy-done
  149.8 0.0 copy-done.5
  149.8 0.0 copy-done.6
  149.8 0.0 copy-start.2
  149.8 2.5 %copy-done.2 = f32[1,8,320,512]{3,2,1,0:T(8,128)S(1)} copy-done((f32[1,8,320,512]{3,2,1,0:T(8,128)S(1)}, f32[1,8,320,512]{3,2,1,0:T(8,128)}, u32[]{:S(2)}) %copy-start.2) | copy-done | bytes 5242904
  152.3 0.0 copy-start.4
  152.3 1.1 copy-done.4
  153.4 0.0 copy-start.1
  153.4 4.8 %shard_map.96.rest_1_ = bf16[2,8,320,512]{3,2,1,0:T(8,128)(2,1)} custom-call(s32[1,4]{1,0:T(1,128)S(1)} %copy-done.5, s32[1,4]{1,0:T(1,128)S(1)} %copy-done.6, f32[1,8,320,512]{3,2,1,0:T(8,128)S(1)} %copy-done.2, f32[2,8,320,1]{3,2,1,0:T(8,128)S(1)} %copy-done, bf16[1,6,320,512]{3,2,1,0:T(8,128)(2,1)} %collective-permute-done.9.far, ...), custom_call_target="tpu_custom_call" | custom-call | flops 26214400 | bytes 13107200 | tf_op jit(solution)/shard_map/pallas_call | solution.py:392
  158.2 0.0 collective-permute-done.7.rest_0_
  158.2 0.0 collective-permute-done.6.far
  158.2 0.0 copy-done.1
  158.2 4.4 %shard_map.97.rest_1_ = bf16[2,8,320,512]{3,2,1,0:T(8,128)(2,1)} custom-call(s32[1,4]{1,0:T(1,128)S(1)} %copy-done.5, s32[1,4]{1,0:T(1,128)S(1)} %copy-done.6, f32[1,8,320,512]{3,2,1,0:T(8,128)S(1)} %copy-done.1, f32[2,8,320,1]{3,2,1,0:T(8,128)S(1)} %copy-done, bf16[1,6,256,512]{3,2,1,0:T(8,128)(2,1)} %collective-permute-done.6.far, ...), custom_call_target="tpu_custom_call", output_to_operand_aliasing={{}: (6, {})} | custom-call | flops 20971520 | bytes 10485760 | tf_op jit(solution)/shard_map/pallas_call | solution.py:392
  162.6 0.0 collective-permute-done.5.rest_0_
  162.6 0.0 collective-permute-done.4.far
  162.6 2.7 %shard_map.98 = bf16[2,8,320,512]{3,2,1,0:T(8,128)(2,1)} custom-call(s32[1,4]{1,0:T(1,128)S(1)} %copy-done.5, s32[1,4]{1,0:T(1,128)S(1)} %copy-done.6, f32[1,8,320,512]{3,2,1,0:T(8,128)S(1)} %copy-done.1, f32[2,8,320,1]{3,2,1,0:T(8,128)S(1)} %copy-done, bf16[1,6,64,512]{3,2,1,0:T(8,128)(2,1)} %collective-permute-done.4.far, ...), custom_call_target="tpu_custom_call", output_to_operand_aliasing={{}: (6, {})} | custom-call | flops 5242880 | bytes 2621440 | tf_op jit(solution)/shard_map/pallas_call | solution.py:392
Async XLA Ops:
  0.0 18.8 %collective-permute-start = (bf16[2,8,320,512]{3,2,1,0:T(8,128)(2,1)}, bf16[2,8,320,512]{3,2,1,0:T(8,128)(2,1)}, u32[]{:S(2)}, u32[]{:S(2)}) collective-permute-start(bf16[2,8,320,512]{3,2,1,0:T(8,128)(2,1)} %state.3), channel_id=1, source_target_pairs={{0,1},{1,0},{2,3},{3,2},{4,5},{5,4},{6,7},{7,6},{8,9},{9,8},{10,11... | collective-permute-start | bytes 15728648 | tf_op jit(solution)/shard_map/ppermute | solution.py:435
  3.9 60.8 %collective-permute-start.1 = (bf16[2,2,320,512]{3,2,1,0:T(8,128)(2,1)}, bf16[2,2,320,512]{3,2,1,0:T(8,128)(2,1)S(1)}, u32[]{:S(2)}, u32[]{:S(2)}) collective-permute-start(bf16[2,2,320,512]{3,2,1,0:T(8,128)(2,1)} %get-tuple-element.15), channel_id=1, source_target_pairs={{0,2},{1,3},{2,0},{3,1},{4,6},{5,7},{6,4},{7,5},{8,10},{9,11},{10,... | collective-permute-start | bytes 3932168 | tf_op jit(solution)/shard_map/ppermute | solution.py:433
  15.2 89.1 %collective-permute-start.8 = (bf16[1,4,320,512]{3,2,1,0:T(8,128)(2,1)}, bf16[1,4,320,512]{3,2,1,0:T(8,128)(2,1)}, u32[]{:S(2)}, u32[]{:S(2)}) collective-permute-start(bf16[1,4,320,512]{3,2,1,0:T(8,128)(2,1)} %get-tuple-element.21), channel_id=1, source_target_pairs={{0,28},{4,8},{8,4},{12,16},{16,12},{20,24},{24,20},{28,0},{1,29},{... | collective-permute-start | bytes 3932168 | tf_op jit(solution)/shard_map/ppermute | solution.py:439
  16.8 45.9 %collective-permute-start.11 = (bf16[1,2,320,512]{3,2,1,0:T(8,128)(2,1)}, bf16[1,2,320,512]{3,2,1,0:T(8,128)(2,1)S(1)}, u32[]{:S(2)}, u32[]{:S(2)}) collective-permute-start(bf16[1,2,320,512]{3,2,1,0:T(8,128)(2,1)} %get-tuple-element.24), channel_id=1, source_target_pairs={{0,4},{4,0},{8,12},{12,8},{16,20},{20,16},{24,28},{28,24},{1,5},{5... | collective-permute-start | bytes 1966088 | tf_op jit(solution)/shard_map/ppermute | solution.py:440
  16.8 87.0 %collective-permute-start.10 = (bf16[1,2,320,512]{3,2,1,0:T(8,128)(2,1)}, bf16[1,2,320,512]{3,2,1,0:T(8,128)(2,1)S(1)}, u32[]{:S(2)}, u32[]{:S(2)}) collective-permute-start(bf16[1,2,320,512]{3,2,1,0:T(8,128)(2,1)} %get-tuple-element.23), channel_id=1, source_target_pairs={{0,4},{4,0},{8,12},{12,8},{16,20},{20,16},{24,28},{28,24},{1,5},{5... | collective-permute-start | bytes 1966088 | tf_op jit(solution)/shard_map/ppermute | solution.py:434
  26.1 79.8 %copy-start.8 = (f32[2,8,320]{2,1,0:T(8,128)S(1)}, f32[2,8,320]{2,1,0:T(8,128)}, u32[]{:S(2)}) copy-start(f32[2,8,320]{2,1,0:T(8,128)} %param.16) | copy-start | bytes 61444
  26.1 123.6 %collective-permute-start.9 = (bf16[1,6,320,512]{3,2,1,0:T(8,128)(2,1)}, bf16[1,6,320,512]{3,2,1,0:T(8,128)(2,1)}, u32[]{:S(2)}, u32[]{:S(2)}) collective-permute-start(bf16[1,6,320,512]{3,2,1,0:T(8,128)(2,1)} %get-tuple-element.22), channel_id=1, source_target_pairs={{0,2},{1,3},{2,0},{3,1},{4,6},{5,7},{6,4},{7,5},{8,10},{9,11},{10,... | collective-permute-start | bytes 5898248 | tf_op jit(solution)/shard_map/ppermute | solution.py:442
  62.7 41.6 %collective-permute-start.3 = (bf16[1,4,320,512]{3,2,1,0:T(8,128)(2,1)}, bf16[1,4,320,512]{3,2,1,0:T(8,128)(2,1)}, u32[]{:S(2)}, u32[]{:S(2)}) collective-permute-start(bf16[1,4,320,512]{3,2,1,0:T(8,128)(2,1)} %get-tuple-element.16), channel_id=1, source_target_pairs={{0,28},{4,8},{8,4},{12,16},{16,12},{20,24},{24,20},{28,0},{1,29},{... | collective-permute-start | bytes 3932168 | tf_op jit(solution)/shard_map/ppermute | solution.py:448
  64.7 45.5 %copy-start.7 = (bf16[2,2,320,512]{3,2,1,0:T(8,128)(2,1)}, bf16[2,2,320,512]{3,2,1,0:T(8,128)(2,1)S(1)}, u32[]{:S(2)}) copy-start(bf16[2,2,320,512]{3,2,1,0:T(8,128)(2,1)S(1)} %collective-permute-done.1.far_all) | copy-start | bytes 3932164
  64.7 43.6 %collective-permute-start.2 = (bf16[2,2,320,512]{3,2,1,0:T(8,128)(2,1)S(1)}, bf16[2,2,320,512]{3,2,1,0:T(8,128)(2,1)}, u32[]{:S(2)}, u32[]{:S(2)}) collective-permute-start(bf16[2,2,320,512]{3,2,1,0:T(8,128)(2,1)S(1)} %collective-permute-done.1.far_all), channel_id=1, source_target_pairs={{0,1},{1,0},{2,3},{3,2},{4,5},{5,4},{6,7},{7,6},{8,9},{9,8},{10,11... | collective-permute-start | bytes 3932168 | tf_op jit(solution)/shard_map/ppermute | solution.py:451
  103.8 6.5 %copy-start.3 = (bf16[1,2,320,512]{3,2,1,0:T(8,128)(2,1)}, bf16[1,2,320,512]{3,2,1,0:T(8,128)(2,1)S(1)}, u32[]{:S(2)}) copy-start(bf16[1,2,320,512]{3,2,1,0:T(8,128)(2,1)S(1)} %collective-permute-done.10.rest_0_) | copy-start | bytes 1966084
  103.8 54.4 %collective-permute-start.6 = (bf16[1,6,256,512]{3,2,1,0:T(8,128)(2,1)}, bf16[1,6,256,512]{3,2,1,0:T(8,128)(2,1)}, u32[]{:S(2)}, u32[]{:S(2)}) collective-permute-start(bf16[1,6,256,512]{3,2,1,0:T(8,128)(2,1)} %get-tuple-element.19), channel_id=1, source_target_pairs={{0,2},{1,3},{2,0},{3,1},{4,6},{5,7},{6,4},{7,5},{8,10},{9,11},{10,... | collective-permute-start | bytes 4718600 | tf_op jit(solution)/shard_map/ppermute | solution.py:443
  104.3 53.9 %collective-permute-start.7 = (bf16[1,4,256,512]{3,2,1,0:T(8,128)(2,1)}, bf16[1,4,256,512]{3,2,1,0:T(8,128)(2,1)}, u32[]{:S(2)}, u32[]{:S(2)}) collective-permute-start(bf16[1,4,256,512]{3,2,1,0:T(8,128)(2,1)} %get-tuple-element.20), channel_id=1, source_target_pairs={{0,4},{4,0},{8,12},{12,8},{16,20},{20,16},{24,28},{28,24},{1,5},{5... | collective-permute-start | bytes 3145736 | tf_op jit(solution)/shard_map/ppermute | solution.py:449
  104.3 58.3 %collective-permute-start.4 = (bf16[1,6,64,512]{3,2,1,0:T(8,128)(2,1)}, bf16[1,6,64,512]{3,2,1,0:T(8,128)(2,1)}, u32[]{:S(2)}, u32[]{:S(2)}) collective-permute-start(bf16[1,6,64,512]{3,2,1,0:T(8,128)(2,1)} %get-tuple-element.17), channel_id=1, source_target_pairs={{0,2},{1,3},{2,0},{3,1},{4,6},{5,7},{6,4},{7,5},{8,10},{9,11},{10,... | collective-permute-start | bytes 1179656 | tf_op jit(solution)/shard_map/ppermute | solution.py:444
  108.3 54.3 %collective-permute-start.5 = (bf16[1,4,64,512]{3,2,1,0:T(8,128)(2,1)}, bf16[1,4,64,512]{3,2,1,0:T(8,128)(2,1)S(1)}, u32[]{:S(2)}, u32[]{:S(2)}) collective-permute-start(bf16[1,4,64,512]{3,2,1,0:T(8,128)(2,1)} %get-tuple-element.18), channel_id=1, source_target_pairs={{0,4},{4,0},{8,12},{12,8},{16,20},{20,16},{24,28},{28,24},{1,5},{5... | collective-permute-start | bytes 786440 | tf_op jit(solution)/shard_map/ppermute | solution.py:450
  129.9 19.8 %copy-start = (f32[2,8,320,1]{3,2,1,0:T(8,128)S(1)}, f32[2,8,320,1]{3,2,1,0:T(8,128)}, u32[]{:S(2)}) copy-start(f32[2,8,320,1]{3,2,1,0:T(8,128)} %copy.12.step) | copy-start | bytes 61444
  129.9 19.8 %copy-start.5 = (s32[1,4]{1,0:T(1,128)S(1)}, s32[1,4]{1,0:T(1,128)}, u32[]{:S(2)}) copy-start(s32[1,4]{1,0:T(1,128)} %left.9) | copy-start | bytes 52
  129.9 19.8 %copy-start.6 = (s32[1,4]{1,0:T(1,128)S(1)}, s32[1,4]{1,0:T(1,128)}, u32[]{:S(2)}) copy-start(s32[1,4]{1,0:T(1,128)} %right.9) | copy-start | bytes 52
  149.8 2.5 %copy-start.2 = (f32[1,8,320,512]{3,2,1,0:T(8,128)S(1)}, f32[1,8,320,512]{3,2,1,0:T(8,128)}, u32[]{:S(2)}) copy-start(f32[1,8,320,512]{3,2,1,0:T(8,128)} %shard_map.95.base) | copy-start | bytes 15728644
  152.3 1.1 copy-start.4
  153.4 4.8 %copy-start.1 = (f32[1,8,320,512]{3,2,1,0:T(8,128)S(1)}, f32[1,8,320,512]{3,2,1,0:T(8,128)}, u32[]{:S(2)}) copy-start(f32[1,8,320,512]{3,2,1,0:T(8,128)} %shard_map.93.base) | copy-start | bytes 15728644

commit v3 on v2

--- a/solution.py
+++ b/solution.py
@@ -11,7 +11,10 @@
 
 ANY = pl.BlockSpec(memory_space=pl.ANY)
 SMEM = pl.BlockSpec(memory_space=pltpu.SMEM)
+VMEM = pl.BlockSpec(memory_space=pltpu.VMEM)
 SLOTS = 3
+ROOM = 56 << 20
+LOCAL_ROOM = 58 << 20
 
 
 def time_table(count):
@@ -42,10 +45,11 @@
 def remote_kernel(inst, iface, ranges, pieces, first, codes_hbm, state_hbm, off_hbm, *rest):
     outs, rest = rest[: len(pieces)], rest[len(pieces) :]
     if first:
-        passed_hbm, *rest = rest
-        *rest, passed, read_sem, write_sem = rest
-    codes, code_sem, acc, states, jacobians, picked, places, *rest = rest
-    state_sem, off_sem, ready, out_sem = rest
+        passed, *rest = rest
+        *rest, read_sem = rest
+    else:
+        *rest, ready, out_sem = rest
+    codes, code_sem, acc, states, jacobians, picked, places, state_sem, off_sem = rest
     load_codes = pltpu.make_async_copy(codes_hbm, codes, code_sem)
     load_codes.start()
     if first:
@@ -57,8 +61,9 @@
     acc[...] = jnp.zeros_like(acc)
     load_codes.wait()
 
-    def scan(term, found):
-        code = codes[lax.div(term, blocks), lax.rem(term, blocks)]
+    found = jnp.int32(0)
+    for term in range(codes.shape[0] * blocks):
+        code = codes[term // blocks, term % blocks]
         hits, place, base = 0, 0, 0
         for kind, offset, count in ranges:
             at = code - (lows[kind] + offset)
@@ -68,9 +73,7 @@
             base += count
         picked[found] = term
         places[found] = place
-        return found + hits
-
-    found = lax.fori_loop(0, codes.shape[0] * blocks, scan, jnp.int32(0))
+        found = found + hits
 
     def copies(index):
         slot = lax.rem(index, SLOTS)
@@ -103,11 +106,13 @@
         acc[places[index]] += term.astype(jnp.float32)
         return carry
 
+    lax.fori_loop(0, found, one, 0)
     if first:
+        for out, (slot_low, slot_high, row_low, row_high) in zip(outs, pieces):
+            for slot in range(slot_low, slot_high):
+                out[0, slot - slot_low] = acc[slot, row_low:row_high].astype(jnp.bfloat16)
         pltpu.make_async_copy(source, passed, read_sem).wait()
-        write = pltpu.make_async_copy(passed, passed_hbm, write_sem)
-        write.start()
-    lax.fori_loop(0, found, one, 0)
+        return
     writes = []
     for slot in range(acc.shape[0]):
         ready[slot] = acc[slot].astype(jnp.bfloat16)
@@ -121,28 +126,25 @@
                 writes.append(copy)
     for copy in writes:
         copy.wait()
-    if first:
-        write.wait()
 
 
 def remote_terms(inst, iface, ranges, pieces, codes, adjoint, off, first=0):
     insts, blocks, dof, wide = adjoint.shape
     couple = off.shape[2]
-    shapes = [
-        jax.ShapeDtypeStruct((1, b - a, d - c, wide), jnp.bfloat16) for a, b, c, d in pieces
-    ]
-    out_specs = [ANY] * len(pieces)
-    extra = []
+    work = sum(count for _, _, count in ranges)
+    shapes = [(1, b - a, d - c, wide) for a, b, c, d in pieces]
     if first:
-        passed = (insts, first, dof, wide)
-        shapes.append(jax.ShapeDtypeStruct(passed, jnp.bfloat16))
-        out_specs.append(ANY)
+        shapes.append((insts, first, dof, wide))
+        shapes = [pltpu.VMEM(shape, jnp.bfloat16) for shape in shapes]
+        out_specs = [VMEM] * len(shapes)
+        extra = [pltpu.SemaphoreType.DMA(())]
+    else:
+        shapes = [jax.ShapeDtypeStruct(shape, jnp.bfloat16) for shape in shapes]
+        out_specs = [ANY] * len(shapes)
         extra = [
-            pltpu.VMEM(passed, jnp.bfloat16),
-            pltpu.SemaphoreType.DMA(()),
-            pltpu.SemaphoreType.DMA(()),
+            pltpu.VMEM((work, dof, wide), jnp.bfloat16),
+            pltpu.SemaphoreType.DMA((sum(b - a for a, b, _, _ in pieces),)),
         ]
-    work = sum(count for _, _, count in ranges)
     return pl.pallas_call(
         functools.partial(remote_kernel, inst, iface, ranges, pieces, first),
         out_shape=shapes,
@@ -158,8 +160,6 @@
             pltpu.SMEM((couple * blocks + 1,), jnp.int32),
             pltpu.SemaphoreType.DMA((SLOTS,)),
             pltpu.SemaphoreType.DMA((SLOTS,)),
-            pltpu.VMEM((work, dof, wide), jnp.bfloat16),
-            pltpu.SemaphoreType.DMA((sum(b - a for a, b, _, _ in pieces),)),
             *extra,
         ],
         cost_estimate=pl.CostEstimate(
@@ -167,13 +167,15 @@
             bytes_accessed=work * 2 * dof * (dof + wide),
             transcendentals=0,
         ),
+        compiler_params=pltpu.CompilerParams(vmem_limit_bytes=ROOM),
     )(codes, adjoint, off)
 
 
 def local_kernel(
-    inst, insts, couple, first, codes, here, table, left, right, adj_all, near_all, far_all,
-    relay_all, arrived, state, diag, off, grad, step, base, acc,
+    inst, insts, couple, first, kept, codes, here, table, left, right, adj_all, near_all, far_all,
+    relay_all, arrived, state, diag, off, grad, step, base, *rest,
 ):
+    acc = rest[-1]
     row = pl.program_id(0)
     blocks = pl.num_programs(0)
 
@@ -210,6 +212,9 @@
             total = mix(total, block, (adj_all, near_all), 0)
             mine = adj_all[inst, block].astype(jnp.float32)
             base[0, block] = mine - step[0, block] * total
+            if kept:
+                low = base.shape[2] - kept
+                rest[1][block] = jnp.broadcast_to(step[0, block, low:], rest[1].shape[1:])
             return carry
 
         def finish_far(block, carry):
@@ -219,22 +224,28 @@
 
         lax.fori_loop(0, base.shape[1], finish, 0)
         lax.fori_loop(0, first, finish_far, 0)
+        if kept:
+            rest[0][...] = base[:, :, base.shape[2] - kept :]
 
 
 def local_part(
-    inst, codes, here, table, left, right, adjoint, near, far, relay, arrived, diag, off, grad, step
+    inst, kept, codes, here, table, left, right, adjoint, near, far, relay, arrived, diag, off, grad, step
 ):
     insts, blocks, dof, wide = adjoint.shape
     couple = off.shape[2]
     first = far.shape[1]
 
-    def whole(x):
-        return pl.BlockSpec(x.shape, lambda r: (0, 0, 0, 0), pipeline_mode=pl.Buffered(1))
-
+    once = functools.partial(pl.BlockSpec, pipeline_mode=pl.Buffered(1))
+    whole = lambda x: once(x.shape, lambda r: (0, 0, 0, 0))
+
+    shapes = [jax.ShapeDtypeStruct((1, blocks, dof, wide), jnp.float32)]
+    if kept:
+        shapes.append(pltpu.VMEM((1, blocks, kept, wide), jnp.float32))
+        shapes.append(pltpu.VMEM((blocks, kept, 128), jnp.float32))
     return pl.pallas_call(
-        functools.partial(local_kernel, inst, insts, couple, first),
+        functools.partial(local_kernel, inst, insts, couple, first, kept),
         grid=(blocks,),
-        out_shape=jax.ShapeDtypeStruct((1, blocks, dof, wide), jnp.float32),
+        out_shape=shapes,
         in_specs=[
             SMEM,
             SMEM,
@@ -249,11 +260,15 @@
             pl.BlockSpec((1, 1, dof, wide), lambda r: (inst, r, 0, 0)),
             pl.BlockSpec((1, 1, dof, dof), lambda r: (inst, r, 0, 0)),
             pl.BlockSpec((1, 1, couple, dof, dof), lambda r: (inst, r, 0, 0, 0)),
-            pl.BlockSpec((1, blocks, dof, wide), lambda r: (inst, 0, 0, 0)),
-            pl.BlockSpec((1, blocks, dof, 1), lambda r: (inst, 0, 0, 0)),
+            once((1, blocks, dof, wide), lambda r: (inst, 0, 0, 0)),
+            once((1, blocks, dof, 1), lambda r: (inst, 0, 0, 0)),
         ],
-        out_specs=pl.BlockSpec((1, blocks, dof, wide), lambda r: (0, 0, 0, 0)),
+        out_specs=[
+            pl.BlockSpec((1, blocks, dof, wide), lambda r: (0, 0, 0, 0)),
+            *[VMEM] * (len(shapes) - 1),
+        ],
         scratch_shapes=[pltpu.VMEM((blocks, dof, wide), jnp.float32)],
+        compiler_params=pltpu.CompilerParams(vmem_limit_bytes=LOCAL_ROOM),
         cost_estimate=pl.CostEstimate(
             flops=4 * blocks * dof * dof * wide,
             bytes_accessed=blocks * dof * (6 * dof + 12 * wide),
@@ -301,65 +316,63 @@
             bytes_accessed=6 * insts * count * dof * wide,
             transcendentals=0,
         ),
+        compiler_params=pltpu.CompilerParams(vmem_limit_bytes=ROOM),
         name="mix",
     )(here, table, adjoint, near)
 
 
-def final_kernel(where, group, first, offsets, left, right, base, step, far, *rest):
+def face_of(left, right, slot, odd):
+    return jnp.where(odd == 0, right[0, slot], left[0, slot])
+
+
+def final_kernel(group, first, offsets, left, right, base, step, far, *rest):
     arrivals = rest[: len(offsets)]
-    if where is None:
-        out, total = rest[-2:]
-    else:
-        out_hbm, total, out, out_sem = rest[-4:]
-        inst, row_low, rows = where
+    out, total = rest[-2:]
     start = pl.program_id(0) * group
     odd = parity()
     slots = [(x, s, offset + s) for x, offset in zip(arrivals, offsets) for s in range(x.shape[1])]
 
     def one(inner, carry):
         block = start + inner
-        place = 0 if group == 1 else jnp.maximum(block - first, 0)
-        chosen = [jnp.where(odd == 0, right[0, s], left[0, s]) == block for _, _, s in slots]
-        touched = functools.reduce(jnp.logical_or, chosen)
-        late = block >= first
-
-        def put(value):
-            out[0, inner] = (base[0, inner] - step[0, inner] * value).astype(jnp.bfloat16)
-
-        @pl.when(late & ~touched)
-        def _():
-            put(far[0, place].astype(jnp.float32))
-
-        @pl.when(~late & ~touched)
-        def _():
-            out[0, inner] = base[0, inner].astype(jnp.bfloat16)
-
-        @pl.when(touched)
-        def _():
-            total[...] = jnp.where(late, far[0, place].astype(jnp.float32), 0.0)
-            for (arrived, slot, _), hit in zip(slots, chosen):
-
-                @pl.when(hit)
-                def _():
-                    total[...] += arrived[0, slot].astype(jnp.float32)
-
-            put(total[...])
-
-        if where is not None:
-            write(block).start()
+        chosen = [face_of(left, right, s, odd) == block for _, _, s in slots]
+        update(
+            base.at[0, inner], step[0, inner], far.at[0], slots, chosen, block, first,
+            out.at[0, inner], total,
+        )
         return carry
 
-    def write(block):
-        target = out_hbm.at[inst, block, pl.ds(row_low, rows)]
-        return pltpu.make_async_copy(out.at[0, block], target, out_sem.at[block])
-
     lax.fori_loop(0, group, one, 0)
-    if where is not None:
-        for block in range(group):
-            write(block).wait()
-
-
-def final_part(inst, row_low, row_high, group, left, right, base, step, far, arrivals, out, limit):
+
+
+def update(base, step, far, slots, chosen, block, first, out, total):
+    place = jnp.maximum(block - first, 0)
+    touched = functools.reduce(jnp.logical_or, chosen)
+    late = block >= first
+
+    def put(value):
+        out[...] = (base[...] - step * value).astype(jnp.bfloat16)
+
+    @pl.when(late & ~touched)
+    def _():
+        put(far[place].astype(jnp.float32))
+
+    @pl.when(~late & ~touched)
+    def _():
+        out[...] = base[...].astype(jnp.bfloat16)
+
+    @pl.when(touched)
+    def _():
+        total[...] = jnp.where(late, far[place].astype(jnp.float32), 0.0)
+        for (arrived, slot, _), hit in zip(slots, chosen):
+
+            @pl.when(hit)
+            def _():
+                total[...] += arrived[0, slot].astype(jnp.float32)
+
+        put(total[...])
+
+
+def final_part(inst, row_low, row_high, group, left, right, base, step, far, arrivals, limit, out):
     insts = step.shape[0]
     _, blocks, dof, wide = base.shape
     rows = row_high - row_low
@@ -374,34 +387,21 @@
         SMEM,
         pl.BlockSpec((1, group, rows, wide), lambda g: (0, g, at, 0)),
         pl.BlockSpec((1, group, rows, 1), lambda g: (inst, g, at, 0)),
-        whole(far)
-        if group > 1
-        else pl.BlockSpec((1, 1, rows, wide), lambda g: (0, jnp.maximum(g - first, 0), 0, 0)),
+        whole(far),
         *[whole(x) for x in terms],
     ]
-    last = group == blocks
-    scratch = [pltpu.VMEM((rows, wide), jnp.float32)]
-    if last:
-        scratch.append(pltpu.VMEM((1, blocks, rows, wide), jnp.bfloat16))
-        scratch.append(pltpu.SemaphoreType.DMA((blocks,)))
     aliases = {}
     if out is not None:
         aliases = {len(operands): 0}
         operands.append(out)
         specs.append(ANY)
     return pl.pallas_call(
-        functools.partial(
-            final_kernel,
-            (inst, row_low, rows) if last else None,
-            group,
-            first,
-            [offset for offset, _ in arrivals],
-        ),
+        functools.partial(final_kernel, group, first, [offset for offset, _ in arrivals]),
         grid=(blocks // group,),
         out_shape=jax.ShapeDtypeStruct((insts, blocks, dof, wide), jnp.bfloat16),
         in_specs=specs,
-        out_specs=ANY if last else state,
-        scratch_shapes=scratch,
+        out_specs=state,
+        scratch_shapes=[pltpu.VMEM((rows, wide), jnp.float32)],
         input_output_aliases=aliases,
         cost_estimate=pl.CostEstimate(
             flops=20 * blocks * rows * wide,
@@ -412,8 +412,55 @@
     )(*operands)
 
 
+def last_kernel(inst, row_low, left, right, base, step, far, arrived, old, out_hbm, total, out, sem):
+    _, blocks, rows, wide = base.shape
+    first = blocks - far.shape[1]
+    odd = parity()
+    slots = [(arrived, s, s) for s in range(arrived.shape[1])]
+    faces = [face_of(left, right, s, odd) for _, _, s in slots]
+
+    def write(block):
+        target = out_hbm.at[inst, block, pl.ds(row_low, rows)]
+        return pltpu.make_async_copy(out.at[block], target, sem.at[block])
+
+    for block in range(blocks):
+        chosen = [face == block for face in faces]
+        spread = jnp.concatenate([step[block]] * (wide // 128), axis=-1)
+        update(
+            base.at[0, block], spread, far.at[0], slots, chosen, block, first,
+            out.at[block], total,
+        )
+        write(block).start()
+    for block in range(blocks):
+        write(block).wait()
+
+
+def last_part(inst, row_low, left, right, base, step, far, arrived, out):
+    _, blocks, rows, wide = base.shape
+    near_by = [pltpu.with_memory_space_constraint(x, pltpu.VMEM) for x in (far, arrived)]
+    return pl.pallas_call(
+        functools.partial(last_kernel, inst, row_low),
+        out_shape=jax.ShapeDtypeStruct(out.shape, jnp.bfloat16),
+        in_specs=[SMEM, SMEM, VMEM, VMEM, VMEM, VMEM, ANY],
+        out_specs=ANY,
+        scratch_shapes=[
+            pltpu.VMEM((rows, wide), jnp.float32),
+            pltpu.VMEM((blocks, rows, wide), jnp.bfloat16),
+            pltpu.SemaphoreType.DMA((blocks,)),
+        ],
+        input_output_aliases={6: 0},
+        cost_estimate=pl.CostEstimate(
+            flops=20 * blocks * rows * wide,
+            bytes_accessed=10 * blocks * rows * wide,
+            transcendentals=0,
+        ),
+        compiler_params=pltpu.CompilerParams(vmem_limit_bytes=8 << 20),
+        name="last",
+    )(left, right, base, step, *near_by, out)
+
+
 def per_device(adjoint, diag, off, off_columns, left, right, grad, step):
-    insts, blocks, dof, _ = adjoint.shape
+    insts, _, dof, _ = adjoint.shape
     iface = left.shape[1]
     parts, times = lax.axis_size("space"), lax.axis_size("tm")
     if times != 4 or insts != 2 or parts % 2:
@@ -451,14 +498,13 @@
     relay = lax.ppermute(far0, "tm", swap_core)
     step = step[..., None]
     common = (codes, here, table, left, right, adjoint, near, far0, relay)
-    base0 = local_part(0, *common, from_other0, diag, off, grad, step)
-    base1 = local_part(1, *common, from_other1, diag, off, grad, step)
+    (base0,) = local_part(0, 0, *common, from_other0, diag, off, grad, step)
+    base1, base1b, step1b = local_part(1, dof - cut, *common, from_other1, diag, off, grad, step)
     faces = (left, right)
     arrivals = [(half, from_pair0a), (0, from_pair0b)]
-    out = final_part(0, 0, dof, 2, *faces, base0, step, far1, arrivals, None, 16)
-    out = final_part(1, 0, cut, 4, *faces, base1, step, far2a, [(0, from_pair1a)], out, 20)
-    arrivals = [(0, from_pair1b)]
-    return final_part(1, cut, dof, blocks, *faces, base1, step, far2b, arrivals, out, 12)
+    out = final_part(0, 0, dof, 2, *faces, base0, step, far1, arrivals, 58, None)
+    out = final_part(1, 0, cut, 4, *faces, base1, step, far2a, [(0, from_pair1a)], 58, out)
+    return last_part(1, cut, *faces, base1b, step1b, far2b, from_pair1b, out)
 
 
 def solution(mesh):

time: 167 us -> 165 us (0.988)
    unnamed x18 -> x12, local copies, waits for them, and re-layouts: 3.6 us -> 2.32 us
  transfers between devices with their start and end apart: 12 -> 12, of which waited for: 2 -> 2; matrix products, arithmetic and copies ran while one was open for 1% -> 1% of each run, Pallas kernels for 47% -> 48%
where the time goes in v3:
time: 165 us; the launch traced here: 164 us
  Pallas kernels  79.9 us (48%)
  waiting for transfers between devices  66 us (40%)
  starting transfers between devices  13.3 us (8%)
  local copies, waits for them, and re-layouts  4.6 us (3%)
    pallas_call x2, Pallas kernels, local_part(): pl.pallas_call(functools.partial(local_kernel, inst, insts, couple, first...  39.5 us
    ppermute x1, waiting for transfers between devices, per_device(): from_pair0a = lax.ppermute(pair0a, 'space', pair)  39.1 us
    ppermute x1, waiting for transfers between devices, per_device(): from_pair0b = lax.ppermute(pair0b, 'space', pair)  26.9 us
    pallas_call x3, Pallas kernels, remote_terms(): pl.pallas_call(functools.partial(remote_kernel, inst, iface, ranges, piec...  20 us
    pallas_call x2, Pallas kernels, final_part(): pl.pallas_call(functools.partial(final_kernel, group, first, [offset for...  11.5 us
    pallas_call x1, Pallas kernels, mix(): pl.pallas_call(functools.partial(mix_kernel, insts, pieces), grid=(count,...  7.31 us
  transfers between devices with their start and end apart: 12, of which 2 were waited for; matrix products, arithmetic and copies ran while one was open for 1% of the time, Pallas kernels for 48%

profile of v3, /device:TPU:0, one launch (start us, length us, event | category | flops | bytes accessed | tf_op | source)
XLA Modules:
  0.0 163.9 jit_solution(925387292618902914)
XLA Ops:
  0.0 0.5 collective-permute-start
  0.5 2.4 %shard_map.91 = (bf16[1,2,320,512]{3,2,1,0:T(8,128)(2,1)S(1)}, bf16[2,2,320,512]{3,2,1,0:T(8,128)(2,1)S(1)}) custom-call(s32[2,8]{1,0:T(2,128)} %bitcast.3, bf16[2,8,320,512]{3,2,1,0:T(8,128)(2,1)} %state.3, bf16[2,8,2,320,320]{4,3,2,1,0:T(8,128)(2,1)} %off.3), custom_call_target="tpu_custom_call" | custom-call | flops 209715200 | bytes 1064960 | tf_op jit(solution)/shard_map/pallas_call | solution.py:148
  2.9 2.6 %collective-permute-start.1 = (bf16[2,2,320,512]{3,2,1,0:T(8,128)(2,1)S(1)}, bf16[2,2,320,512]{3,2,1,0:T(8,128)(2,1)S(1)}, u32[]{:S(2)}, u32[]{:S(2)}) collective-permute-start(bf16[2,2,320,512]{3,2,1,0:T(8,128)(2,1)S(1)} %get-tuple-element.18), channel_id=1, source_target_pairs={{0,2},{1,3},{2,0},{3,1},{4,6},{5,7},{6,4},{7,5},{8,10},{9,11},{10,... | collective-permute-start | bytes 3932168 | tf_op jit(solution)/shard_map/ppermute | solution.py:480
  5.5 8.4 %shard_map.94 = (bf16[1,4,320,512]{3,2,1,0:T(8,128)(2,1)}, bf16[1,2,320,512]{3,2,1,0:T(8,128)(2,1)}) custom-call(s32[2,8]{1,0:T(2,128)} %bitcast.4, bf16[2,8,320,512]{3,2,1,0:T(8,128)(2,1)} %state.3, bf16[2,8,2,320,320]{4,3,2,1,0:T(8,128)(2,1)} %off.3), custom_call_target="tpu_custom_call" | custom-call | flops 629145600 | bytes 3194880 | tf_op jit(solution)/shard_map/pallas_call | solution.py:148
  13.9 1.6 collective-permute-start.8
  15.5 0.0 collective-permute-start.11
  15.5 2.0 %collective-permute-start.10 = (bf16[1,2,320,512]{3,2,1,0:T(8,128)(2,1)S(1)}, bf16[1,2,320,512]{3,2,1,0:T(8,128)(2,1)}, u32[]{:S(2)}, u32[]{:S(2)}) collective-permute-start(bf16[1,2,320,512]{3,2,1,0:T(8,128)(2,1)S(1)} %get-tuple-element.29), channel_id=1, source_target_pairs={{0,4},{4,0},{8,12},{12,8},{16,20},{20,16},{24,28},{28,24},{1,5},{5... | collective-permute-start | bytes 1966088 | tf_op jit(solution)/shard_map/ppermute | solution.py:481
  17.5 0.0 collective-permute-done.near_all.near
  17.5 7.3 %mix.1 = (bf16[1,6,320,512]{3,2,1,0:T(8,128)(2,1)}, bf16[1,6,256,512]{3,2,1,0:T(8,128)(2,1)}, bf16[1,6,64,512]{3,2,1,0:T(8,128)(2,1)}) custom-call(s32[1]{0:T(128)} %bitcast.1.here, f32[8,8]{1,0:T(8,128)} %constant.6.clone.table, bf16[2,8,320,512]{3,2,1,0:T(8,128)(2,1)} %state.3, bf16[2,8,320,512]{3,2,1,0:T(8,128)(2,1)} %collective-permute-done.near_all.near), custom_call_target="tpu_custom_call" | custom-call | flops 15728640 | bytes 11796480 | tf_op jit(solution)/shard_map/mix/pallas_call | solution.py:302
  24.9 0.0 copy-start.5
  24.9 0.6 collective-permute-start.9
  25.4 9.2 %shard_map.92 = (bf16[1,4,320,512]{3,2,1,0:T(8,128)(2,1)}, bf16[1,4,256,512]{3,2,1,0:T(8,128)(2,1)}, bf16[1,4,64,512]{3,2,1,0:T(8,128)(2,1)}) custom-call(s32[2,8]{1,0:T(2,128)} %bitcast.5, bf16[2,8,320,512]{3,2,1,0:T(8,128)(2,1)} %state.3, bf16[2,8,2,320,320]{4,3,2,1,0:T(8,128)(2,1)} %off.3), custom_call_target="tpu_custom_call" | custom-call | flops 838860800 | bytes 4259840 | tf_op jit(solution)/shard_map/pallas_call | solution.py:148
  34.6 26.9 %collective-permute-done.11.rest_1_ = bf16[1,2,320,512]{3,2,1,0:T(8,128)(2,1)} collective-permute-done((bf16[1,2,320,512]{3,2,1,0:T(8,128)(2,1)}, bf16[1,2,320,512]{3,2,1,0:T(8,128)(2,1)}, u32[]{:S(2)}, u32[]{:S(2)}) %collective-permute-start.11) | collective-permute-done | bytes 655392 | tf_op jit(solution)/shard_map/ppermute | solution.py:487
  61.5 2.0 %collective-permute-start.3 = (bf16[1,4,320,512]{3,2,1,0:T(8,128)(2,1)}, bf16[1,4,320,512]{3,2,1,0:T(8,128)(2,1)S(1)}, u32[]{:S(2)}, u32[]{:S(2)}) collective-permute-start(bf16[1,4,320,512]{3,2,1,0:T(8,128)(2,1)} %get-tuple-element.19), channel_id=1, source_target_pairs={{0,28},{4,8},{8,4},{12,16},{16,12},{20,24},{24,20},{28,0},{1,29},{... | collective-permute-start | bytes 3932168 | tf_op jit(solution)/shard_map/ppermute | solution.py:495
  63.6 0.0 collective-permute-done.1.far_all
  63.6 0.0 copy-start.2
  63.6 0.0 collective-permute-start.2
  63.6 39.1 %collective-permute-done.10.rest_0_ = bf16[1,2,320,512]{3,2,1,0:T(8,128)(2,1)} collective-permute-done((bf16[1,2,320,512]{3,2,1,0:T(8,128)(2,1)S(1)}, bf16[1,2,320,512]{3,2,1,0:T(8,128)(2,1)}, u32[]{:S(2)}, u32[]{:S(2)}) %collective-permute-start.10) | collective-permute-done | bytes 655392 | tf_op jit(solution)/shard_map/ppermute | solution.py:481
  102.6 0.5 collective-permute-start.6
  103.1 0.0 collective-permute-done.8.arrived
  103.1 0.0 collective-permute-start.7
  103.1 0.0 collective-permute-done.3.arrived
  103.2 0.0 copy-start.4
  103.2 1.1 copy-done.4
  104.3 1.5 collective-permute-start.4
  105.8 0.0 copy-done.5
  105.8 2.3 %copy.12.step = f32[2,8,320,1]{3,2,1,0:T(8,128)} copy(f32[2,8,320,1]{2,1,0,3:T(8,128)S(1)} %bitcast.8) | data formatting | bytes 40960 | tf_op jit(solution)/shard_map/broadcast_in_dim | solution.py:499
  108.1 0.0 collective-permute-done.2.relay_all
  108.1 2.0 %collective-permute-start.5 = (bf16[1,4,64,512]{3,2,1,0:T(8,128)(2,1)}, bf16[1,4,64,512]{3,2,1,0:T(8,128)(2,1)S(1)}, u32[]{:S(2)}, u32[]{:S(2)}) collective-permute-start(bf16[1,4,64,512]{3,2,1,0:T(8,128)(2,1)} %get-tuple-element.23), channel_id=1, source_target_pairs={{0,4},{4,0},{8,12},{12,8},{16,20},{20,16},{24,28},{28,24},{1,5},{5... | collective-permute-start | bytes 786440 | tf_op jit(solution)/shard_map/ppermute | solution.py:497
  110.1 0.0 copy-done.2
  110.1 19.7 %shard_map.95.base = f32[1,8,320,512]{3,2,1,0:T(8,128)} custom-call(s32[2,8]{1,0:T(2,128)} %bitcast.6, s32[1]{0:T(128)} %bitcast.1.here, f32[8,8]{1,0:T(8,128)} %constant.6.clone.table, s32[1,4]{1,0:T(1,128)} %left.9, s32[1,4]{1,0:T(1,128)} %right.9, bf16[2,8,320,512]{3,2,1,0:T(8,128)(2,1)} %state.3, ...), custom_call_target="tpu_custom_call" | custom-call | flops 1677721600 | bytes 20643840 | tf_op jit(solution)/shard_map/pallas_call | solution.py:245
  129.9 19.8 %shard_map.93 = (f32[1,8,320,512]{3,2,1,0:T(8,128)}, f32[1,8,64,512]{3,2,1,0:T(8,128)S(1)}, f32[8,64,128]{2,1,0:T(8,128)S(1)}) custom-call(s32[2,8]{1,0:T(2,128)} %bitcast.7, s32[1]{0:T(128)} %bitcast.1.here, f32[8,8]{1,0:T(8,128)} %constant.6.clone.table, s32[1,4]{1,0:T(1,128)} %left.9, s32[1,4]{1,0:T(1,128)} %right.9, bf16[2,8,320,512]{3,2,1,0:T(8,128)(2,1)} %state.3, ...), custom_call_target="tpu_custom_call" | custom-call | flops 1677721600 | bytes 20643840 | tf_op jit(solution)/shard_map/pallas_call | solution.py:245
  149.6 0.0 collective-permute-done.9.far
  149.6 6.5 %shard_map.96.rest_1_ = bf16[2,8,320,512]{3,2,1,0:T(8,128)(2,1)} custom-call(s32[1,4]{1,0:T(1,128)} %left.9, s32[1,4]{1,0:T(1,128)} %right.9, f32[1,8,320,512]{3,2,1,0:T(8,128)} %shard_map.95.base, f32[2,8,320,1]{3,2,1,0:T(8,128)} %copy.12.step, bf16[1,6,320,512]{3,2,1,0:T(8,128)(2,1)} %collective-permute-done.9.far, ...), custom_call_target="tpu_custom_call" | custom-call | flops 26214400 | bytes 13107200 | tf_op jit(solution)/shard_map/pallas_call | solution.py:398
  156.1 0.0 collective-permute-done.7.rest_0_
  156.1 0.0 collective-permute-done.6.far
  156.1 0.0 copy-start.3
  156.1 1.2 copy-done.3
  157.3 0.0 copy-start
  157.3 0.0 copy-start.1
  157.3 5.0 %shard_map.97.old = bf16[2,8,320,512]{3,2,1,0:T(8,128)(2,1)} custom-call(s32[1,4]{1,0:T(1,128)} %left.9, s32[1,4]{1,0:T(1,128)} %right.9, f32[1,8,320,512]{3,2,1,0:T(8,128)} %get-tuple-element.24.base, f32[2,8,320,1]{3,2,1,0:T(8,128)} %copy.12.step, bf16[1,6,256,512]{3,2,1,0:T(8,128)(2,1)} %copy-done.3, ...), custom_call_target="tpu_custom_call", output_to_operand_aliasing={{}: (6, {})} | custom-call | flops 20971520 | bytes 10485760 | tf_op jit(solution)/shard_map/pallas_call | solution.py:398
  162.3 0.0 collective-permute-done.5.arrived
  162.3 0.0 collective-permute-done.4.far
  162.3 0.0 copy-done
  162.3 0.0 copy-done.1
  162.3 1.6 last.1
Async XLA Ops:
  0.0 17.5 %collective-permute-start = (bf16[2,8,320,512]{3,2,1,0:T(8,128)(2,1)}, bf16[2,8,320,512]{3,2,1,0:T(8,128)(2,1)}, u32[]{:S(2)}, u32[]{:S(2)}) collective-permute-start(bf16[2,8,320,512]{3,2,1,0:T(8,128)(2,1)} %state.3), channel_id=1, source_target_pairs={{0,1},{1,0},{2,3},{3,2},{4,5},{5,4},{6,7},{7,6},{8,9},{9,8},{10,11... | collective-permute-start | bytes 15728648 | tf_op jit(solution)/shard_map/ppermute | solution.py:482
  2.9 60.7 %collective-permute-start.1 = (bf16[2,2,320,512]{3,2,1,0:T(8,128)(2,1)S(1)}, bf16[2,2,320,512]{3,2,1,0:T(8,128)(2,1)S(1)}, u32[]{:S(2)}, u32[]{:S(2)}) collective-permute-start(bf16[2,2,320,512]{3,2,1,0:T(8,128)(2,1)S(1)} %get-tuple-element.18), channel_id=1, source_target_pairs={{0,2},{1,3},{2,0},{3,1},{4,6},{5,7},{6,4},{7,5},{8,10},{9,11},{10,... | collective-permute-start | bytes 3932168 | tf_op jit(solution)/shard_map/ppermute | solution.py:480
  13.9 89.2 %collective-permute-start.8 = (bf16[1,4,320,512]{3,2,1,0:T(8,128)(2,1)}, bf16[1,4,320,512]{3,2,1,0:T(8,128)(2,1)}, u32[]{:S(2)}, u32[]{:S(2)}) collective-permute-start(bf16[1,4,320,512]{3,2,1,0:T(8,128)(2,1)} %get-tuple-element.27), channel_id=1, source_target_pairs={{0,28},{4,8},{8,4},{12,16},{16,12},{20,24},{24,20},{28,0},{1,29},{... | collective-permute-start | bytes 3932168 | tf_op jit(solution)/shard_map/ppermute | solution.py:486
  15.5 46.0 %collective-permute-start.11 = (bf16[1,2,320,512]{3,2,1,0:T(8,128)(2,1)}, bf16[1,2,320,512]{3,2,1,0:T(8,128)(2,1)}, u32[]{:S(2)}, u32[]{:S(2)}) collective-permute-start(bf16[1,2,320,512]{3,2,1,0:T(8,128)(2,1)} %get-tuple-element.30), channel_id=1, source_target_pairs={{0,4},{4,0},{8,12},{12,8},{16,20},{20,16},{24,28},{28,24},{1,5},{5... | collective-permute-start | bytes 1966088 | tf_op jit(solution)/shard_map/ppermute | solution.py:487
  15.5 87.1 %collective-permute-start.10 = (bf16[1,2,320,512]{3,2,1,0:T(8,128)(2,1)S(1)}, bf16[1,2,320,512]{3,2,1,0:T(8,128)(2,1)}, u32[]{:S(2)}, u32[]{:S(2)}) collective-permute-start(bf16[1,2,320,512]{3,2,1,0:T(8,128)(2,1)S(1)} %get-tuple-element.29), channel_id=1, source_target_pairs={{0,4},{4,0},{8,12},{12,8},{16,20},{20,16},{24,28},{28,24},{1,5},{5... | collective-permute-start | bytes 1966088 | tf_op jit(solution)/shard_map/ppermute | solution.py:481
  24.9 81.0 %copy-start.5 = (f32[2,8,320]{2,1,0:T(8,128)S(1)}, f32[2,8,320]{2,1,0:T(8,128)}, u32[]{:S(2)}) copy-start(f32[2,8,320]{2,1,0:T(8,128)} %param.16) | copy-start | bytes 61444
  24.9 124.8 %collective-permute-start.9 = (bf16[1,6,320,512]{3,2,1,0:T(8,128)(2,1)}, bf16[1,6,320,512]{3,2,1,0:T(8,128)(2,1)}, u32[]{:S(2)}, u32[]{:S(2)}) collective-permute-start(bf16[1,6,320,512]{3,2,1,0:T(8,128)(2,1)} %get-tuple-element.28), channel_id=1, source_target_pairs={{0,2},{1,3},{2,0},{3,1},{4,6},{5,7},{6,4},{7,5},{8,10},{9,11},{10,... | collective-permute-start | bytes 5898248 | tf_op jit(solution)/shard_map/ppermute | solution.py:489
  61.5 41.6 %collective-permute-start.3 = (bf16[1,4,320,512]{3,2,1,0:T(8,128)(2,1)}, bf16[1,4,320,512]{3,2,1,0:T(8,128)(2,1)S(1)}, u32[]{:S(2)}, u32[]{:S(2)}) collective-permute-start(bf16[1,4,320,512]{3,2,1,0:T(8,128)(2,1)} %get-tuple-element.19), channel_id=1, source_target_pairs={{0,28},{4,8},{8,4},{12,16},{16,12},{20,24},{24,20},{28,0},{1,29},{... | collective-permute-start | bytes 3932168 | tf_op jit(solution)/shard_map/ppermute | solution.py:495
  63.6 46.6 %copy-start.2 = (bf16[2,2,320,512]{3,2,1,0:T(8,128)(2,1)}, bf16[2,2,320,512]{3,2,1,0:T(8,128)(2,1)S(1)}, u32[]{:S(2)}) copy-start(bf16[2,2,320,512]{3,2,1,0:T(8,128)(2,1)S(1)} %collective-permute-done.1.far_all) | copy-start | bytes 3932164
  63.6 44.5 %collective-permute-start.2 = (bf16[2,2,320,512]{3,2,1,0:T(8,128)(2,1)S(1)}, bf16[2,2,320,512]{3,2,1,0:T(8,128)(2,1)}, u32[]{:S(2)}, u32[]{:S(2)}) collective-permute-start(bf16[2,2,320,512]{3,2,1,0:T(8,128)(2,1)S(1)} %collective-permute-done.1.far_all), channel_id=1, source_target_pairs={{0,1},{1,0},{2,3},{3,2},{4,5},{5,4},{6,7},{7,6},{8,9},{9,8},{10,11... | collective-permute-start | bytes 3932168 | tf_op jit(solution)/shard_map/ppermute | solution.py:498
  102.6 53.5 %collective-permute-start.6 = (bf16[1,6,256,512]{3,2,1,0:T(8,128)(2,1)}, bf16[1,6,256,512]{3,2,1,0:T(8,128)(2,1)S(1)}, u32[]{:S(2)}, u32[]{:S(2)}) collective-permute-start(bf16[1,6,256,512]{3,2,1,0:T(8,128)(2,1)} %get-tuple-element.25), channel_id=1, source_target_pairs={{0,2},{1,3},{2,0},{3,1},{4,6},{5,7},{6,4},{7,5},{8,10},{9,11},{10,... | collective-permute-start | bytes 4718600 | tf_op jit(solution)/shard_map/ppermute | solution.py:490
  103.1 53.0 %collective-permute-start.7 = (bf16[1,4,256,512]{3,2,1,0:T(8,128)(2,1)}, bf16[1,4,256,512]{3,2,1,0:T(8,128)(2,1)}, u32[]{:S(2)}, u32[]{:S(2)}) collective-permute-start(bf16[1,4,256,512]{3,2,1,0:T(8,128)(2,1)} %get-tuple-element.26), channel_id=1, source_target_pairs={{0,4},{4,0},{8,12},{12,8},{16,20},{20,16},{24,28},{28,24},{1,5},{5... | collective-permute-start | bytes 3145736 | tf_op jit(solution)/shard_map/ppermute | solution.py:496
  103.2 1.2 copy-start.4
  104.3 58.0 %collective-permute-start.4 = (bf16[1,6,64,512]{3,2,1,0:T(8,128)(2,1)}, bf16[1,6,64,512]{3,2,1,0:T(8,128)(2,1)S(1)}, u32[]{:S(2)}, u32[]{:S(2)}) collective-permute-start(bf16[1,6,64,512]{3,2,1,0:T(8,128)(2,1)} %get-tuple-element.22), channel_id=1, source_target_pairs={{0,2},{1,3},{2,0},{3,1},{4,6},{5,7},{6,4},{7,5},{8,10},{9,11},{10,... | collective-permute-start | bytes 1179656 | tf_op jit(solution)/shard_map/ppermute | solution.py:491
  108.1 54.2 %collective-permute-start.5 = (bf16[1,4,64,512]{3,2,1,0:T(8,128)(2,1)}, bf16[1,4,64,512]{3,2,1,0:T(8,128)(2,1)S(1)}, u32[]{:S(2)}, u32[]{:S(2)}) collective-permute-start(bf16[1,4,64,512]{3,2,1,0:T(8,128)(2,1)} %get-tuple-element.23), channel_id=1, source_target_pairs={{0,4},{4,0},{8,12},{12,8},{16,20},{20,16},{24,28},{28,24},{1,5},{5... | collective-permute-start | bytes 786440 | tf_op jit(solution)/shard_map/ppermute | solution.py:497
  156.1 1.2 copy-start.3
  157.3 5.1 %copy-start = (s32[1,4]{1,0:T(1,128)S(1)}, s32[1,4]{1,0:T(1,128)}, u32[]{:S(2)}) copy-start(s32[1,4]{1,0:T(1,128)} %left.9) | copy-start | bytes 52
  157.3 5.1 %copy-start.1 = (s32[1,4]{1,0:T(1,128)S(1)}, s32[1,4]{1,0:T(1,128)}, u32[]{:S(2)}) copy-start(s32[1,4]{1,0:T(1,128)} %right.9) | copy-start | bytes 52

commit v4 on v3

--- a/solution.py
+++ b/solution.py
@@ -473,18 +473,19 @@
     pair = [(i, i ^ 1) for i in range(parts)]
     other = [(i, (i + 2 * (i % 2) - 1) % parts) for i in range(parts)]
     codes = off_columns.T
-    cut, first, half = 256, 2, iface // 2
+    cut, first, half = 240, 2, iface - 1
 
     ranges, pieces = [(0, half, iface - half)], [(0, iface - half, 0, dof)]
     pair0a, passed = remote_terms(0, iface, ranges, pieces, codes, adjoint, off, first)
     far0 = lax.ppermute(passed, "tm", swap_chip)
     from_pair0a = lax.ppermute(pair0a, "space", pair)
     near = lax.ppermute(adjoint, "tm", swap_core)
-    ranges = [(1, 0, iface), (0, 0, half)]
-    pieces = [(0, iface, 0, dof), (iface, iface + half, 0, dof)]
-    other0, pair0b = remote_terms(0, iface, ranges, pieces, codes, adjoint, off)
+    ranges, pieces = [(0, 0, half)], [(0, half, 0, dof)]
+    (pair0b,) = remote_terms(0, iface, ranges, pieces, codes, adjoint, off)
+    from_pair0b = lax.ppermute(pair0b, "space", pair)
+    ranges, pieces = [(1, 0, iface)], [(0, iface, 0, dof)]
+    (other0,) = remote_terms(0, iface, ranges, pieces, codes, adjoint, off)
     from_other0 = lax.ppermute(other0, "space", other)
-    from_pair0b = lax.ppermute(pair0b, "space", pair)
     mixed = mix(here, table, adjoint, near, first, [(0, 0, dof), (1, 0, cut), (1, cut, dof)])
     far1 = lax.ppermute(mixed[0], "tm", swap_chip)
     far2a = lax.ppermute(mixed[1], "tm", swap_chip)

time: 165 us -> 162 us (0.982)
  the two profiles are of different devices: /device:TPU:0 before, /device:TPU:6 now
where the time goes in v4:
time: 162 us; the launch traced here: 161 us
  Pallas kernels  80.2 us (50%)
  waiting for transfers between devices  55.1 us (34%)
  starting transfers between devices  21.5 us (13%)
  local copies, waits for them, and re-layouts  4.4 us (3%)
    pallas_call x2, Pallas kernels, local_part(): pl.pallas_call(functools.partial(local_kernel, inst, insts, couple, first...  43 us
    ppermute x1, waiting for transfers between devices, per_device(): from_pair0a = lax.ppermute(pair0a, 'space', pair)  31 us
    ppermute x1, waiting for transfers between devices, per_device(): from_other1 = lax.ppermute(other1, 'space', other)  24.2 us
    pallas_call x4, Pallas kernels, remote_terms(): pl.pallas_call(functools.partial(remote_kernel, inst, iface, ranges, piec...  17 us
    pallas_call x2, Pallas kernels, final_part(): pl.pallas_call(functools.partial(final_kernel, group, first, [offset for...  11.3 us
    pallas_call x1, Pallas kernels, mix(): pl.pallas_call(functools.partial(mix_kernel, insts, pieces), grid=(count,...  7.28 us
    ppermute x1, starting transfers between devices, per_device(): from_other0 = lax.ppermute(other0, 'space', other)  3.76 us
    ppermute x1, starting transfers between devices, per_device(): from_pair1a = lax.ppermute(pair1a, 'space', pair)  3.26 us
  transfers between devices with their start and end apart: 12, of which 2 were waited for; matrix products, arithmetic and copies ran while one was open for 1% of the time, Pallas kernels for 49%

profile of v4, /device:TPU:6, one launch (start us, length us, event | category | flops | bytes accessed | tf_op | source)
XLA Modules:
  0.0 161.4 jit_solution(1013689054470420550)
XLA Ops:
  0.0 0.0 collective-permute-start
  0.0 1.4 shard_map.91
  1.4 0.6 collective-permute-start.1
  2.0 3.6 %shard_map.96 = bf16[1,3,320,512]{3,2,1,0:T(8,128)(2,1)} custom-call(s32[2,8]{1,0:T(2,128)} %bitcast.4, bf16[2,8,320,512]{3,2,1,0:T(8,128)(2,1)} %state_hbm.7, bf16[2,8,2,320,320]{4,3,2,1,0:T(8,128)(2,1)} %off_hbm.7), custom_call_target="tpu_custom_call" | custom-call | flops 314572800 | bytes 1597440 | tf_op jit(solution)/shard_map/pallas_call | solution.py:148
  5.6 0.5 collective-permute-start.11
  6.1 5.2 %shard_map.94 = bf16[1,4,320,512]{3,2,1,0:T(8,128)(2,1)} custom-call(s32[2,8]{1,0:T(2,128)} %bitcast.5, bf16[2,8,320,512]{3,2,1,0:T(8,128)(2,1)} %state_hbm.7, bf16[2,8,2,320,320]{4,3,2,1,0:T(8,128)(2,1)} %off_hbm.7), custom_call_target="tpu_custom_call" | custom-call | flops 419430400 | bytes 2129920 | tf_op jit(solution)/shard_map/pallas_call | solution.py:148
  11.3 3.8 %collective-permute-start.8 = (bf16[1,4,320,512]{3,2,1,0:T(8,128)(2,1)}, bf16[1,4,320,512]{3,2,1,0:T(8,128)(2,1)}, u32[]{:S(2)}, u32[]{:S(2)}) collective-permute-start(bf16[1,4,320,512]{3,2,1,0:T(8,128)(2,1)} %shard_map.94), channel_id=1, source_target_pairs={{0,28},{4,8},{8,4},{12,16},{16,12},{20,24},{24,20},{28,0},{1,29},{... | collective-permute-start | bytes 3932168 | tf_op jit(solution)/shard_map/ppermute | solution.py:488
  15.1 3.2 %collective-permute-start.10 = (bf16[1,1,320,512]{3,2,1,0:T(8,128)(2,1)S(1)}, bf16[1,1,320,512]{3,2,1,0:T(8,128)(2,1)S(1)}, u32[]{:S(2)}, u32[]{:S(2)}) collective-permute-start(bf16[1,1,320,512]{3,2,1,0:T(8,128)(2,1)S(1)} %get-tuple-element.26), channel_id=1, source_target_pairs={{0,4},{4,0},{8,12},{12,8},{16,20},{20,16},{24,28},{28,24},{1,5},{5... | collective-permute-start | bytes 983048 | tf_op jit(solution)/shard_map/ppermute | solution.py:481
  18.3 0.0 collective-permute-done.near_all.near
  18.3 7.3 %mix.1 = (bf16[1,6,320,512]{3,2,1,0:T(8,128)(2,1)}, bf16[1,6,240,512]{3,2,1,0:T(8,128)(2,1)}, bf16[1,6,80,512]{3,2,1,0:T(8,128)(2,1)}) custom-call(s32[1]{0:T(128)} %bitcast.1.here, f32[8,8]{1,0:T(8,128)} %constant.6.clone.table, bf16[2,8,320,512]{3,2,1,0:T(8,128)(2,1)} %state_hbm.7, bf16[2,8,320,512]{3,2,1,0:T(8,128)(2,1)} %collective-permute-done.near_all.near), custom_call_target="tpu_custom_call" | custom-call | flops 15728640 | bytes 11796480 | tf_op jit(solution)/shard_map/mix/pallas_call | solution.py:302
  25.6 0.0 copy-start.7
  25.6 1.6 collective-permute-start.9
  27.1 6.8 %shard_map.92 = (bf16[1,4,320,512]{3,2,1,0:T(8,128)(2,1)}, bf16[1,4,240,512]{3,2,1,0:T(8,128)(2,1)}, bf16[1,4,80,512]{3,2,1,0:T(8,128)(2,1)}) custom-call(s32[2,8]{1,0:T(2,128)} %bitcast.6, bf16[2,8,320,512]{3,2,1,0:T(8,128)(2,1)} %state_hbm.7, bf16[2,8,2,320,320]{4,3,2,1,0:T(8,128)(2,1)} %off_hbm.7), custom_call_target="tpu_custom_call" | custom-call | flops 838860800 | bytes 4259840 | tf_op jit(solution)/shard_map/pallas_call | solution.py:148
  33.9 31.0 %collective-permute-done.10.rest_0_ = bf16[1,1,320,512]{3,2,1,0:T(8,128)(2,1)S(1)} collective-permute-done((bf16[1,1,320,512]{3,2,1,0:T(8,128)(2,1)S(1)}, bf16[1,1,320,512]{3,2,1,0:T(8,128)(2,1)S(1)}, u32[]{:S(2)}, u32[]{:S(2)}) %collective-permute-start.10) | collective-permute-done | bytes 327712 | tf_op jit(solution)/shard_map/ppermute | solution.py:481
  64.9 0.0 copy-start.6
  64.9 2.3 %collective-permute-start.3 = (bf16[1,4,320,512]{3,2,1,0:T(8,128)(2,1)}, bf16[1,4,320,512]{3,2,1,0:T(8,128)(2,1)S(1)}, u32[]{:S(2)}, u32[]{:S(2)}) collective-permute-start(bf16[1,4,320,512]{3,2,1,0:T(8,128)(2,1)} %get-tuple-element.17), channel_id=1, source_target_pairs={{0,28},{4,8},{8,4},{12,16},{16,12},{20,24},{24,20},{28,0},{1,29},{... | collective-permute-start | bytes 3932168 | tf_op jit(solution)/shard_map/ppermute | solution.py:496
  67.2 0.0 collective-permute-done.1.far_all
  67.2 0.0 copy-start.2
  67.2 0.0 collective-permute-start.2
  67.2 0.0 collective-permute-done.11.rest_1_
  67.2 1.6 collective-permute-start.6
  68.8 0.0 collective-permute-done.8.arrived
  68.8 3.3 %collective-permute-start.7 = (bf16[1,4,240,512]{3,2,1,0:T(8,128)(2,1)}, bf16[1,4,240,512]{3,2,1,0:T(8,128)(2,1)S(1)}, u32[]{:S(2)}, u32[]{:S(2)}) collective-permute-start(bf16[1,4,240,512]{3,2,1,0:T(8,128)(2,1)} %get-tuple-element.24), channel_id=1, source_target_pairs={{0,4},{4,0},{8,12},{12,8},{16,20},{20,16},{24,28},{28,24},{1,5},{5... | collective-permute-start | bytes 2949128 | tf_op jit(solution)/shard_map/ppermute | solution.py:497
  72.1 24.2 %collective-permute-done.3.arrived = bf16[1,4,320,512]{3,2,1,0:T(8,128)(2,1)S(1)} collective-permute-done((bf16[1,4,320,512]{3,2,1,0:T(8,128)(2,1)}, bf16[1,4,320,512]{3,2,1,0:T(8,128)(2,1)S(1)}, u32[]{:S(2)}, u32[]{:S(2)}) %collective-permute-start.3) | collective-permute-done | bytes 1310752 | tf_op jit(solution)/shard_map/ppermute | solution.py:496
  96.3 0.0 copy-start.4
  96.3 1.5 collective-permute-start.4
  97.8 0.0 collective-permute-done.2.relay_all
  97.8 0.0 copy-start.3
  97.8 1.1 copy-done.3
  98.9 0.0 copy-done.4
  98.9 3.2 %collective-permute-start.5 = (bf16[1,4,80,512]{3,2,1,0:T(8,128)(2,1)}, bf16[1,4,80,512]{3,2,1,0:T(8,128)(2,1)S(1)}, u32[]{:S(2)}, u32[]{:S(2)}) collective-permute-start(bf16[1,4,80,512]{3,2,1,0:T(8,128)(2,1)} %get-tuple-element.21), channel_id=1, source_target_pairs={{0,4},{4,0},{8,12},{12,8},{16,20},{20,16},{24,28},{28,24},{1,5},{5... | collective-permute-start | bytes 983048 | tf_op jit(solution)/shard_map/ppermute | solution.py:498
  102.2 0.0 copy-done.7
  102.2 2.3 %copy.12.step = f32[2,8,320,1]{3,2,1,0:T(8,128)} copy(f32[2,8,320,1]{2,1,0,3:T(8,128)S(1)} %bitcast.9) | data formatting | bytes 40960 | tf_op jit(solution)/shard_map/broadcast_in_dim | solution.py:500
  104.5 0.0 copy-done.2
  104.5 21.4 %shard_map.95.base = f32[1,8,320,512]{3,2,1,0:T(8,128)} custom-call(s32[2,8]{1,0:T(2,128)} %bitcast.7, s32[1]{0:T(128)} %bitcast.1.here, f32[8,8]{1,0:T(8,128)} %constant.6.clone.table, s32[1,4]{1,0:T(1,128)} %left.9, s32[1,4]{1,0:T(1,128)} %right.9, bf16[2,8,320,512]{3,2,1,0:T(8,128)(2,1)} %state_hbm.7, ...), custom_call_target="tpu_custom_call" | custom-call | flops 1677721600 | bytes 20643840 | tf_op jit(solution)/shard_map/pallas_call | solution.py:245
  125.9 0.0 copy-done.6
  125.9 21.5 %shard_map.93 = (f32[1,8,320,512]{3,2,1,0:T(8,128)}, f32[1,8,80,512]{3,2,1,0:T(8,128)S(1)}, f32[8,80,128]{2,1,0:T(8,128)S(1)}) custom-call(s32[2,8]{1,0:T(2,128)} %bitcast.8, s32[1]{0:T(128)} %bitcast.1.here, f32[8,8]{1,0:T(8,128)} %constant.6.clone.table, s32[1,4]{1,0:T(1,128)} %left.9, s32[1,4]{1,0:T(1,128)} %right.9, bf16[2,8,320,512]{3,2,1,0:T(8,128)(2,1)} %state_hbm.7, ...), custom_call_target="tpu_custom_call" | custom-call | flops 1677721600 | bytes 20643840 | tf_op jit(solution)/shard_map/pallas_call | solution.py:245
  147.4 0.0 collective-permute-done.9.far
  147.5 6.5 %shard_map.97.rest_1_ = bf16[2,8,320,512]{3,2,1,0:T(8,128)(2,1)} custom-call(s32[1,4]{1,0:T(1,128)} %left.9, s32[1,4]{1,0:T(1,128)} %right.9, f32[1,8,320,512]{3,2,1,0:T(8,128)} %shard_map.95.base, f32[2,8,320,1]{3,2,1,0:T(8,128)} %copy.12.step, bf16[1,6,320,512]{3,2,1,0:T(8,128)(2,1)} %collective-permute-done.9.far, bf16[1,1,320,512]{3,2,1,0:T(8,128)(2,1)} %copy-done.6, ...), custom_call_target="tpu_custom_call" | custom-call | flops 26214400 | bytes 13107200 | tf_op jit(solution)/shard_map/pallas_call | solution.py:398
  153.9 0.0 collective-permute-done.7.rest_0_
  153.9 0.0 copy-start.5
  153.9 0.0 collective-permute-done.6.far
  153.9 1.0 copy-done.5
  154.9 0.0 copy-start
  154.9 0.0 copy-start.1
  154.9 4.8 %shard_map.98.old = bf16[2,8,320,512]{3,2,1,0:T(8,128)(2,1)} custom-call(s32[1,4]{1,0:T(1,128)} %left.9, s32[1,4]{1,0:T(1,128)} %right.9, f32[1,8,320,512]{3,2,1,0:T(8,128)} %get-tuple-element.22.base, f32[2,8,320,1]{3,2,1,0:T(8,128)} %copy.12.step, bf16[1,6,240,512]{3,2,1,0:T(8,128)(2,1)} %collective-permute-done.6.far, ...), custom_call_target="tpu_custom_call", output_to_operand_aliasing={{}: (6, {})} | custom-call | flops 19660800 | bytes 9830400 | tf_op jit(solution)/shard_map/pallas_call | solution.py:398
  159.7 0.0 collective-permute-done.5.arrived
  159.7 0.0 collective-permute-done.4.far
  159.7 0.0 copy-done
  159.7 0.0 copy-done.1
  159.7 1.7 %last.1 = bf16[2,8,320,512]{3,2,1,0:T(8,128)(2,1)} custom-call(s32[1,4]{1,0:T(1,128)S(1)} %copy-done, s32[1,4]{1,0:T(1,128)S(1)} %copy-done.1, f32[1,8,80,512]{3,2,1,0:T(8,128)S(1)} %get-tuple-element.18.base, f32[8,80,128]{2,1,0:T(8,128)S(1)} %get-tuple-element.19.step, ...), custom_call_target="tpu_custom_call", output_to_operand_aliasing={{}: (6, {})} | custom-call | flops 6553600 | bytes 3276800 | tf_op jit(solution)/shard_map/last/pallas_call | solution.py:441
Async XLA Ops:
  0.0 18.3 %collective-permute-start = (bf16[2,8,320,512]{3,2,1,0:T(8,128)(2,1)}, bf16[2,8,320,512]{3,2,1,0:T(8,128)(2,1)}, u32[]{:S(2)}, u32[]{:S(2)}) collective-permute-start(bf16[2,8,320,512]{3,2,1,0:T(8,128)(2,1)} %state_hbm.7), channel_id=1, source_target_pairs={{0,1},{1,0},{2,3},{3,2},{4,5},{5,4},{6,7},{7,6},{8,9},{9,8},{10,11... | collective-permute-start | bytes 15728648 | tf_op jit(solution)/shard_map/ppermute | solution.py:482
  1.4 65.8 %collective-permute-start.1 = (bf16[2,2,320,512]{3,2,1,0:T(8,128)(2,1)S(1)}, bf16[2,2,320,512]{3,2,1,0:T(8,128)(2,1)S(1)}, u32[]{:S(2)}, u32[]{:S(2)}) collective-permute-start(bf16[2,2,320,512]{3,2,1,0:T(8,128)(2,1)S(1)} %get-tuple-element.16), channel_id=1, source_target_pairs={{0,2},{1,3},{2,0},{3,1},{4,6},{5,7},{6,4},{7,5},{8,10},{9,11},{10,... | collective-permute-start | bytes 3932168 | tf_op jit(solution)/shard_map/ppermute | solution.py:480
  5.6 61.6 %collective-permute-start.11 = (bf16[1,3,320,512]{3,2,1,0:T(8,128)(2,1)}, bf16[1,3,320,512]{3,2,1,0:T(8,128)(2,1)}, u32[]{:S(2)}, u32[]{:S(2)}) collective-permute-start(bf16[1,3,320,512]{3,2,1,0:T(8,128)(2,1)} %shard_map.96), channel_id=1, source_target_pairs={{0,4},{4,0},{8,12},{12,8},{16,20},{20,16},{24,28},{28,24},{1,5},{5... | collective-permute-start | bytes 2949128 | tf_op jit(solution)/shard_map/ppermute | solution.py:485
  11.3 57.5 %collective-permute-start.8 = (bf16[1,4,320,512]{3,2,1,0:T(8,128)(2,1)}, bf16[1,4,320,512]{3,2,1,0:T(8,128)(2,1)}, u32[]{:S(2)}, u32[]{:S(2)}) collective-permute-start(bf16[1,4,320,512]{3,2,1,0:T(8,128)(2,1)} %shard_map.94), channel_id=1, source_target_pairs={{0,28},{4,8},{8,4},{12,16},{16,12},{20,24},{24,20},{28,0},{1,29},{... | collective-permute-start | bytes 3932168 | tf_op jit(solution)/shard_map/ppermute | solution.py:488
  15.1 49.8 %collective-permute-start.10 = (bf16[1,1,320,512]{3,2,1,0:T(8,128)(2,1)S(1)}, bf16[1,1,320,512]{3,2,1,0:T(8,128)(2,1)S(1)}, u32[]{:S(2)}, u32[]{:S(2)}) collective-permute-start(bf16[1,1,320,512]{3,2,1,0:T(8,128)(2,1)S(1)} %get-tuple-element.26), channel_id=1, source_target_pairs={{0,4},{4,0},{8,12},{12,8},{16,20},{20,16},{24,28},{28,24},{1,5},{5... | collective-permute-start | bytes 983048 | tf_op jit(solution)/shard_map/ppermute | solution.py:481
  25.6 76.6 %copy-start.7 = (f32[2,8,320]{2,1,0:T(8,128)S(1)}, f32[2,8,320]{2,1,0:T(8,128)}, u32[]{:S(2)}) copy-start(f32[2,8,320]{2,1,0:T(8,128)} %param.16) | copy-start | bytes 61444
  25.6 121.9 %collective-permute-start.9 = (bf16[1,6,320,512]{3,2,1,0:T(8,128)(2,1)}, bf16[1,6,320,512]{3,2,1,0:T(8,128)(2,1)}, u32[]{:S(2)}, u32[]{:S(2)}) collective-permute-start(bf16[1,6,320,512]{3,2,1,0:T(8,128)(2,1)} %get-tuple-element.25), channel_id=1, source_target_pairs={{0,2},{1,3},{2,0},{3,1},{4,6},{5,7},{6,4},{7,5},{8,10},{9,11},{10,... | collective-permute-start | bytes 5898248 | tf_op jit(solution)/shard_map/ppermute | solution.py:490
  64.9 61.0 %copy-start.6 = (bf16[1,1,320,512]{3,2,1,0:T(8,128)(2,1)}, bf16[1,1,320,512]{3,2,1,0:T(8,128)(2,1)S(1)}, u32[]{:S(2)}) copy-start(bf16[1,1,320,512]{3,2,1,0:T(8,128)(2,1)S(1)} %collective-permute-done.10.rest_0_) | copy-start | bytes 983044
  64.9 31.4 %collective-permute-start.3 = (bf16[1,4,320,512]{3,2,1,0:T(8,128)(2,1)}, bf16[1,4,320,512]{3,2,1,0:T(8,128)(2,1)S(1)}, u32[]{:S(2)}, u32[]{:S(2)}) collective-permute-start(bf16[1,4,320,512]{3,2,1,0:T(8,128)(2,1)} %get-tuple-element.17), channel_id=1, source_target_pairs={{0,28},{4,8},{8,4},{12,16},{16,12},{20,24},{24,20},{28,0},{1,29},{... | collective-permute-start | bytes 3932168 | tf_op jit(solution)/shard_map/ppermute | solution.py:496
  67.2 37.2 %copy-start.2 = (bf16[2,2,320,512]{3,2,1,0:T(8,128)(2,1)}, bf16[2,2,320,512]{3,2,1,0:T(8,128)(2,1)S(1)}, u32[]{:S(2)}) copy-start(bf16[2,2,320,512]{3,2,1,0:T(8,128)(2,1)S(1)} %collective-permute-done.1.far_all) | copy-start | bytes 3932164
  67.2 30.6 %collective-permute-start.2 = (bf16[2,2,320,512]{3,2,1,0:T(8,128)(2,1)S(1)}, bf16[2,2,320,512]{3,2,1,0:T(8,128)(2,1)S(1)}, u32[]{:S(2)}, u32[]{:S(2)}) collective-permute-start(bf16[2,2,320,512]{3,2,1,0:T(8,128)(2,1)S(1)} %collective-permute-done.1.far_all), channel_id=1, source_target_pairs={{0,1},{1,0},{2,3},{3,2},{4,5},{5,4},{6,7},{7,6},{8,9},{9,8},{10,11... | collective-permute-start | bytes 3932168 | tf_op jit(solution)/shard_map/ppermute | solution.py:499
  67.2 86.7 %collective-permute-start.6 = (bf16[1,6,240,512]{3,2,1,0:T(8,128)(2,1)}, bf16[1,6,240,512]{3,2,1,0:T(8,128)(2,1)}, u32[]{:S(2)}, u32[]{:S(2)}) collective-permute-start(bf16[1,6,240,512]{3,2,1,0:T(8,128)(2,1)} %get-tuple-element.23), channel_id=1, source_target_pairs={{0,2},{1,3},{2,0},{3,1},{4,6},{5,7},{6,4},{7,5},{8,10},{9,11},{10,... | collective-permute-start | bytes 4423688 | tf_op jit(solution)/shard_map/ppermute | solution.py:491
  68.8 85.1 %collective-permute-start.7 = (bf16[1,4,240,512]{3,2,1,0:T(8,128)(2,1)}, bf16[1,4,240,512]{3,2,1,0:T(8,128)(2,1)S(1)}, u32[]{:S(2)}, u32[]{:S(2)}) collective-permute-start(bf16[1,4,240,512]{3,2,1,0:T(8,128)(2,1)} %get-tuple-element.24), channel_id=1, source_target_pairs={{0,4},{4,0},{8,12},{12,8},{16,20},{20,16},{24,28},{28,24},{1,5},{5... | collective-permute-start | bytes 2949128 | tf_op jit(solution)/shard_map/ppermute | solution.py:497
  96.3 2.7 %copy-start.4 = (bf16[1,4,320,512]{3,2,1,0:T(8,128)(2,1)}, bf16[1,4,320,512]{3,2,1,0:T(8,128)(2,1)S(1)}, u32[]{:S(2)}) copy-start(bf16[1,4,320,512]{3,2,1,0:T(8,128)(2,1)S(1)} %collective-permute-done.3.arrived) | copy-start | bytes 3932164
  96.3 63.5 %collective-permute-start.4 = (bf16[1,6,80,512]{3,2,1,0:T(8,128)(2,1)}, bf16[1,6,80,512]{3,2,1,0:T(8,128)(2,1)S(1)}, u32[]{:S(2)}, u32[]{:S(2)}) collective-permute-start(bf16[1,6,80,512]{3,2,1,0:T(8,128)(2,1)} %get-tuple-element.20), channel_id=1, source_target_pairs={{0,2},{1,3},{2,0},{3,1},{4,6},{5,7},{6,4},{7,5},{8,10},{9,11},{10,... | collective-permute-start | bytes 1474568 | tf_op jit(solution)/shard_map/ppermute | solution.py:492
  97.8 1.2 copy-start.3
  98.9 60.8 %collective-permute-start.5 = (bf16[1,4,80,512]{3,2,1,0:T(8,128)(2,1)}, bf16[1,4,80,512]{3,2,1,0:T(8,128)(2,1)S(1)}, u32[]{:S(2)}, u32[]{:S(2)}) collective-permute-start(bf16[1,4,80,512]{3,2,1,0:T(8,128)(2,1)} %get-tuple-element.21), channel_id=1, source_target_pairs={{0,4},{4,0},{8,12},{12,8},{16,20},{20,16},{24,28},{28,24},{1,5},{5... | collective-permute-start | bytes 983048 | tf_op jit(solution)/shard_map/ppermute | solution.py:498
  153.9 1.0 copy-start.5
  154.9 4.8 %copy-start = (s32[1,4]{1,0:T(1,128)S(1)}, s32[1,4]{1,0:T(1,128)}, u32[]{:S(2)}) copy-start(s32[1,4]{1,0:T(1,128)} %left.9) | copy-start | bytes 52
  154.9 4.8 %copy-start.1 = (s32[1,4]{1,0:T(1,128)S(1)}, s32[1,4]{1,0:T(1,128)}, u32[]{:S(2)}) copy-start(s32[1,4]{1,0:T(1,128)} %right.9) | copy-start | bytes 52

commit v5 on v4

--- a/solution.py
+++ b/solution.py
@@ -473,19 +473,21 @@
     pair = [(i, i ^ 1) for i in range(parts)]
     other = [(i, (i + 2 * (i % 2) - 1) % parts) for i in range(parts)]
     codes = off_columns.T
-    cut, first, half = 240, 2, iface - 1
+    cut, first, half = 256, 2, iface - 1
 
     ranges, pieces = [(0, half, iface - half)], [(0, iface - half, 0, dof)]
     pair0a, passed = remote_terms(0, iface, ranges, pieces, codes, adjoint, off, first)
     far0 = lax.ppermute(passed, "tm", swap_chip)
     from_pair0a = lax.ppermute(pair0a, "space", pair)
     near = lax.ppermute(adjoint, "tm", swap_core)
-    ranges, pieces = [(0, 0, half)], [(0, half, 0, dof)]
+    ranges, pieces = [(0, 1, half - 1)], [(0, half - 1, 0, dof)]
     (pair0b,) = remote_terms(0, iface, ranges, pieces, codes, adjoint, off)
     from_pair0b = lax.ppermute(pair0b, "space", pair)
-    ranges, pieces = [(1, 0, iface)], [(0, iface, 0, dof)]
-    (other0,) = remote_terms(0, iface, ranges, pieces, codes, adjoint, off)
+    ranges = [(1, 0, iface), (0, 0, 1)]
+    pieces = [(0, iface, 0, dof), (iface, iface + 1, 0, dof)]
+    other0, pair0c = remote_terms(0, iface, ranges, pieces, codes, adjoint, off)
     from_other0 = lax.ppermute(other0, "space", other)
+    from_pair0c = lax.ppermute(pair0c, "space", pair)
     mixed = mix(here, table, adjoint, near, first, [(0, 0, dof), (1, 0, cut), (1, cut, dof)])
     far1 = lax.ppermute(mixed[0], "tm", swap_chip)
     far2a = lax.ppermute(mixed[1], "tm", swap_chip)
@@ -502,7 +504,7 @@
     (base0,) = local_part(0, 0, *common, from_other0, diag, off, grad, step)
     base1, base1b, step1b = local_part(1, dof - cut, *common, from_other1, diag, off, grad, step)
     faces = (left, right)
-    arrivals = [(half, from_pair0a), (0, from_pair0b)]
+    arrivals = [(half, from_pair0a), (1, from_pair0b), (0, from_pair0c)]
     out = final_part(0, 0, dof, 2, *faces, base0, step, far1, arrivals, 58, None)
     out = final_part(1, 0, cut, 4, *faces, base1, step, far2a, [(0, from_pair1a)], 58, out)
     return last_part(1, cut, *faces, base1b, step1b, far2b, from_pair1b, out)

time: 162 us -> 167 us (1.031)
  the two profiles are of different devices: /device:TPU:6 before, /device:TPU:0 now
where the time goes in v5:
time: 167 us; the launch traced here: 164 us
  Pallas kernels  81.8 us (49%)
  waiting for transfers between devices  66.2 us (40%)
  starting transfers between devices  11.3 us (7%)
  local copies, waits for them, and re-layouts  4.35 us (3%)
    pallas_call x2, Pallas kernels, local_part(): pl.pallas_call(functools.partial(local_kernel, inst, insts, couple, first...  39.5 us
    ppermute x1, waiting for transfers between devices, per_device(): from_other1 = lax.ppermute(other1, 'space', other)  29.7 us
    ppermute x1, waiting for transfers between devices, per_device(): from_pair0c = lax.ppermute(pair0c, 'space', pair)  26 us
    pallas_call x4, Pallas kernels, remote_terms(): pl.pallas_call(functools.partial(remote_kernel, inst, iface, ranges, piec...  22 us
    pallas_call x2, Pallas kernels, final_part(): pl.pallas_call(functools.partial(final_kernel, group, first, [offset for...  11.5 us
    ppermute x1, waiting for transfers between devices, per_device(): from_pair0a = lax.ppermute(pair0a, 'space', pair)  10.5 us
    pallas_call x1, Pallas kernels, mix(): pl.pallas_call(functools.partial(mix_kernel, insts, pieces), grid=(count,...  7.28 us
  transfers between devices with their start and end apart: 13, of which 3 were waited for; matrix products, arithmetic and copies ran while one was open for 1% of the time, Pallas kernels for 49%

profile of v5, /device:TPU:0, one launch (start us, length us, event | category | flops | bytes accessed | tf_op | source)
XLA Modules:
  0.0 163.8 jit_solution(5459280092743417068)
XLA Ops:
  0.0 0.5 collective-permute-start
  0.5 1.4 shard_map.91
  1.9 2.6 %collective-permute-start.1 = (bf16[2,2,320,512]{3,2,1,0:T(8,128)(2,1)S(1)}, bf16[2,2,320,512]{3,2,1,0:T(8,128)(2,1)S(1)}, u32[]{:S(2)}, u32[]{:S(2)}) collective-permute-start(bf16[2,2,320,512]{3,2,1,0:T(8,128)(2,1)S(1)} %get-tuple-element.18), channel_id=1, source_target_pairs={{0,2},{1,3},{2,0},{3,1},{4,6},{5,7},{6,4},{7,5},{8,10},{9,11},{10,... | collective-permute-start | bytes 3932168 | tf_op jit(solution)/shard_map/ppermute | solution.py:480
  4.5 7.9 %shard_map.94 = (bf16[1,4,320,512]{3,2,1,0:T(8,128)(2,1)}, bf16[1,1,320,512]{3,2,1,0:T(8,128)(2,1)}) custom-call(s32[2,8]{1,0:T(2,128)} %bitcast.4, bf16[2,8,320,512]{3,2,1,0:T(8,128)(2,1)} %state_hbm.7, bf16[2,8,2,320,320]{4,3,2,1,0:T(8,128)(2,1)} %off_hbm.7), custom_call_target="tpu_custom_call" | custom-call | flops 524288000 | bytes 2662400 | tf_op jit(solution)/shard_map/pallas_call | solution.py:148
  12.4 2.0 %collective-permute-start.8 = (bf16[1,4,320,512]{3,2,1,0:T(8,128)(2,1)}, bf16[1,4,320,512]{3,2,1,0:T(8,128)(2,1)}, u32[]{:S(2)}, u32[]{:S(2)}) collective-permute-start(bf16[1,4,320,512]{3,2,1,0:T(8,128)(2,1)} %get-tuple-element.27), channel_id=1, source_target_pairs={{0,28},{4,8},{8,4},{12,16},{16,12},{20,24},{24,20},{28,0},{1,29},{... | collective-permute-start | bytes 3932168 | tf_op jit(solution)/shard_map/ppermute | solution.py:489
  14.4 0.0 collective-permute-start.12
  14.4 3.5 %shard_map.96 = bf16[1,2,320,512]{3,2,1,0:T(8,128)(2,1)} custom-call(s32[2,8]{1,0:T(2,128)} %bitcast.5, bf16[2,8,320,512]{3,2,1,0:T(8,128)(2,1)} %state_hbm.7, bf16[2,8,2,320,320]{4,3,2,1,0:T(8,128)(2,1)} %off_hbm.7), custom_call_target="tpu_custom_call" | custom-call | flops 209715200 | bytes 1064960 | tf_op jit(solution)/shard_map/pallas_call | solution.py:148
  17.9 0.3 collective-permute-start.11
  18.2 0.0 collective-permute-done.near_all.near
  18.2 1.8 %collective-permute-start.10 = (bf16[1,1,320,512]{3,2,1,0:T(8,128)(2,1)S(1)}, bf16[1,1,320,512]{3,2,1,0:T(8,128)(2,1)}, u32[]{:S(2)}, u32[]{:S(2)}) collective-permute-start(bf16[1,1,320,512]{3,2,1,0:T(8,128)(2,1)S(1)} %get-tuple-element.29), channel_id=1, source_target_pairs={{0,4},{4,0},{8,12},{12,8},{16,20},{20,16},{24,28},{28,24},{1,5},{5... | collective-permute-start | bytes 983048 | tf_op jit(solution)/shard_map/ppermute | solution.py:481
  20.0 7.3 %mix.1 = (bf16[1,6,320,512]{3,2,1,0:T(8,128)(2,1)}, bf16[1,6,256,512]{3,2,1,0:T(8,128)(2,1)}, bf16[1,6,64,512]{3,2,1,0:T(8,128)(2,1)}) custom-call(s32[1]{0:T(128)} %bitcast.1.here, f32[8,8]{1,0:T(8,128)} %constant.6.clone.table, bf16[2,8,320,512]{3,2,1,0:T(8,128)(2,1)} %state_hbm.7, bf16[2,8,320,512]{3,2,1,0:T(8,128)(2,1)} %collective-permute-done.near_all.near), custom_call_target="tpu_custom_call" | custom-call | flops 15728640 | bytes 11796480 | tf_op jit(solution)/shard_map/mix/pallas_call | solution.py:302
  27.3 26.0 %collective-permute-done.12.rest_2_ = bf16[1,1,320,512]{3,2,1,0:T(8,128)(2,1)S(1)} collective-permute-done((bf16[1,1,320,512]{3,2,1,0:T(8,128)(2,1)}, bf16[1,1,320,512]{3,2,1,0:T(8,128)(2,1)S(1)}, u32[]{:S(2)}, u32[]{:S(2)}) %collective-permute-start.12) | collective-permute-done | bytes 327712 | tf_op jit(solution)/shard_map/ppermute | solution.py:490
  53.3 0.0 copy-start.5
  53.3 0.0 copy-start.6
  53.3 0.4 collective-permute-start.9
  53.6 9.2 %shard_map.92 = (bf16[1,4,320,512]{3,2,1,0:T(8,128)(2,1)}, bf16[1,4,256,512]{3,2,1,0:T(8,128)(2,1)}, bf16[1,4,64,512]{3,2,1,0:T(8,128)(2,1)}) custom-call(s32[2,8]{1,0:T(2,128)} %bitcast.6, bf16[2,8,320,512]{3,2,1,0:T(8,128)(2,1)} %state_hbm.7, bf16[2,8,2,320,320]{4,3,2,1,0:T(8,128)(2,1)} %off_hbm.7), custom_call_target="tpu_custom_call" | custom-call | flops 838860800 | bytes 4259840 | tf_op jit(solution)/shard_map/pallas_call | solution.py:148
  62.9 0.0 copy-done.5
  62.9 10.5 %collective-permute-done.10.rest_0_ = bf16[1,1,320,512]{3,2,1,0:T(8,128)(2,1)} collective-permute-done((bf16[1,1,320,512]{3,2,1,0:T(8,128)(2,1)S(1)}, bf16[1,1,320,512]{3,2,1,0:T(8,128)(2,1)}, u32[]{:S(2)}, u32[]{:S(2)}) %collective-permute-start.10) | collective-permute-done | bytes 327712 | tf_op jit(solution)/shard_map/ppermute | solution.py:481
  73.4 0.0 copy-start.7
  73.4 2.7 %collective-permute-start.3 = (bf16[1,4,320,512]{3,2,1,0:T(8,128)(2,1)}, bf16[1,4,320,512]{3,2,1,0:T(8,128)(2,1)S(1)}, u32[]{:S(2)}, u32[]{:S(2)}) collective-permute-start(bf16[1,4,320,512]{3,2,1,0:T(8,128)(2,1)} %get-tuple-element.19), channel_id=1, source_target_pairs={{0,28},{4,8},{8,4},{12,16},{16,12},{20,24},{24,20},{28,0},{1,29},{... | collective-permute-start | bytes 3932168 | tf_op jit(solution)/shard_map/ppermute | solution.py:498
  76.2 0.0 collective-permute-done.1.far_all
  76.2 0.0 copy-start.2
  76.2 0.0 collective-permute-start.2
  76.2 0.0 collective-permute-done.11.rest_1_
  76.2 0.4 collective-permute-start.6
  76.6 0.0 collective-permute-done.8.arrived
  76.6 0.0 collective-permute-start.7
  76.6 29.7 %collective-permute-done.3.arrived = bf16[1,4,320,512]{3,2,1,0:T(8,128)(2,1)S(1)} collective-permute-done((bf16[1,4,320,512]{3,2,1,0:T(8,128)(2,1)}, bf16[1,4,320,512]{3,2,1,0:T(8,128)(2,1)S(1)}, u32[]{:S(2)}, u32[]{:S(2)}) %collective-permute-start.3) | collective-permute-done | bytes 1310752 | tf_op jit(solution)/shard_map/ppermute | solution.py:498
  106.2 0.0 copy-start.3
  106.2 1.1 copy-done.3
  107.3 0.6 collective-permute-start.4
  108.0 0.0 copy-done.6
  108.0 2.3 %copy.12.step = f32[2,8,320,1]{3,2,1,0:T(8,128)} copy(f32[2,8,320,1]{2,1,0,3:T(8,128)S(1)} %bitcast.9) | data formatting | bytes 40960 | tf_op jit(solution)/shard_map/broadcast_in_dim | solution.py:502
  110.2 0.0 collective-permute-done.2.relay_all
  110.2 0.0 copy-done.7
  110.2 0.0 collective-permute-start.5
  110.2 0.0 copy-done.2
  110.3 19.7 %shard_map.95.base = f32[1,8,320,512]{3,2,1,0:T(8,128)} custom-call(s32[2,8]{1,0:T(2,128)} %bitcast.7, s32[1]{0:T(128)} %bitcast.1.here, f32[8,8]{1,0:T(8,128)} %constant.6.clone.table, s32[1,4]{1,0:T(1,128)} %left.9, s32[1,4]{1,0:T(1,128)} %right.9, bf16[2,8,320,512]{3,2,1,0:T(8,128)(2,1)} %state_hbm.7, ...), custom_call_target="tpu_custom_call" | custom-call | flops 1677721600 | bytes 20643840 | tf_op jit(solution)/shard_map/pallas_call | solution.py:245
  130.0 19.8 %shard_map.93 = (f32[1,8,320,512]{3,2,1,0:T(8,128)}, f32[1,8,64,512]{3,2,1,0:T(8,128)S(1)}, f32[8,64,128]{2,1,0:T(8,128)S(1)}) custom-call(s32[2,8]{1,0:T(2,128)} %bitcast.8, s32[1]{0:T(128)} %bitcast.1.here, f32[8,8]{1,0:T(8,128)} %constant.6.clone.table, s32[1,4]{1,0:T(1,128)} %left.9, s32[1,4]{1,0:T(1,128)} %right.9, bf16[2,8,320,512]{3,2,1,0:T(8,128)(2,1)} %state_hbm.7, ...), custom_call_target="tpu_custom_call" | custom-call | flops 1677721600 | bytes 20643840 | tf_op jit(solution)/shard_map/pallas_call | solution.py:245
  149.7 0.0 collective-permute-done.9.far
  149.7 6.4 %shard_map.97.rest_1_ = bf16[2,8,320,512]{3,2,1,0:T(8,128)(2,1)} custom-call(s32[1,4]{1,0:T(1,128)} %left.9, s32[1,4]{1,0:T(1,128)} %right.9, f32[1,8,320,512]{3,2,1,0:T(8,128)} %shard_map.95.base, f32[2,8,320,1]{3,2,1,0:T(8,128)} %copy.12.step, bf16[1,6,320,512]{3,2,1,0:T(8,128)(2,1)} %collective-permute-done.9.far, ...), custom_call_target="tpu_custom_call" | custom-call | flops 26214400 | bytes 13107200 | tf_op jit(solution)/shard_map/pallas_call | solution.py:398
  156.2 0.0 collective-permute-done.7.rest_0_
  156.2 0.0 copy-start.4
  156.2 0.0 collective-permute-done.6.far
  156.2 1.0 copy-done.4
  157.2 0.0 copy-start
  157.2 0.0 copy-start.1
  157.2 5.0 %shard_map.98.old = bf16[2,8,320,512]{3,2,1,0:T(8,128)(2,1)} custom-call(s32[1,4]{1,0:T(1,128)} %left.9, s32[1,4]{1,0:T(1,128)} %right.9, f32[1,8,320,512]{3,2,1,0:T(8,128)} %get-tuple-element.24.base, f32[2,8,320,1]{3,2,1,0:T(8,128)} %copy.12.step, bf16[1,6,256,512]{3,2,1,0:T(8,128)(2,1)} %collective-permute-done.6.far, ...), custom_call_target="tpu_custom_call", output_to_operand_aliasing={{}: (6, {})} | custom-call | flops 20971520 | bytes 10485760 | tf_op jit(solution)/shard_map/pallas_call | solution.py:398
  162.2 0.0 collective-permute-done.5.arrived
  162.2 0.0 collective-permute-done.4.far
  162.2 0.0 copy-done
  162.2 0.0 copy-done.1
  162.2 1.6 last.1
Async XLA Ops:
  0.0 18.2 %collective-permute-start = (bf16[2,8,320,512]{3,2,1,0:T(8,128)(2,1)}, bf16[2,8,320,512]{3,2,1,0:T(8,128)(2,1)}, u32[]{:S(2)}, u32[]{:S(2)}) collective-permute-start(bf16[2,8,320,512]{3,2,1,0:T(8,128)(2,1)} %state_hbm.7), channel_id=1, source_target_pairs={{0,1},{1,0},{2,3},{3,2},{4,5},{5,4},{6,7},{7,6},{8,9},{9,8},{10,11... | collective-permute-start | bytes 15728648 | tf_op jit(solution)/shard_map/ppermute | solution.py:482
  1.9 74.3 %collective-permute-start.1 = (bf16[2,2,320,512]{3,2,1,0:T(8,128)(2,1)S(1)}, bf16[2,2,320,512]{3,2,1,0:T(8,128)(2,1)S(1)}, u32[]{:S(2)}, u32[]{:S(2)}) collective-permute-start(bf16[2,2,320,512]{3,2,1,0:T(8,128)(2,1)S(1)} %get-tuple-element.18), channel_id=1, source_target_pairs={{0,2},{1,3},{2,0},{3,1},{4,6},{5,7},{6,4},{7,5},{8,10},{9,11},{10,... | collective-permute-start | bytes 3932168 | tf_op jit(solution)/shard_map/ppermute | solution.py:480
  12.4 64.2 %collective-permute-start.8 = (bf16[1,4,320,512]{3,2,1,0:T(8,128)(2,1)}, bf16[1,4,320,512]{3,2,1,0:T(8,128)(2,1)}, u32[]{:S(2)}, u32[]{:S(2)}) collective-permute-start(bf16[1,4,320,512]{3,2,1,0:T(8,128)(2,1)} %get-tuple-element.27), channel_id=1, source_target_pairs={{0,28},{4,8},{8,4},{12,16},{16,12},{20,24},{24,20},{28,0},{1,29},{... | collective-permute-start | bytes 3932168 | tf_op jit(solution)/shard_map/ppermute | solution.py:489
  14.4 38.9 %collective-permute-start.12 = (bf16[1,1,320,512]{3,2,1,0:T(8,128)(2,1)}, bf16[1,1,320,512]{3,2,1,0:T(8,128)(2,1)S(1)}, u32[]{:S(2)}, u32[]{:S(2)}) collective-permute-start(bf16[1,1,320,512]{3,2,1,0:T(8,128)(2,1)} %get-tuple-element.30), channel_id=1, source_target_pairs={{0,4},{4,0},{8,12},{12,8},{16,20},{20,16},{24,28},{28,24},{1,5},{5... | collective-permute-start | bytes 983048 | tf_op jit(solution)/shard_map/ppermute | solution.py:490
  17.9 58.3 %collective-permute-start.11 = (bf16[1,2,320,512]{3,2,1,0:T(8,128)(2,1)}, bf16[1,2,320,512]{3,2,1,0:T(8,128)(2,1)}, u32[]{:S(2)}, u32[]{:S(2)}) collective-permute-start(bf16[1,2,320,512]{3,2,1,0:T(8,128)(2,1)} %shard_map.96), channel_id=1, source_target_pairs={{0,4},{4,0},{8,12},{12,8},{16,20},{20,16},{24,28},{28,24},{1,5},{5... | collective-permute-start | bytes 1966088 | tf_op jit(solution)/shard_map/ppermute | solution.py:485
  18.2 55.2 %collective-permute-start.10 = (bf16[1,1,320,512]{3,2,1,0:T(8,128)(2,1)S(1)}, bf16[1,1,320,512]{3,2,1,0:T(8,128)(2,1)}, u32[]{:S(2)}, u32[]{:S(2)}) collective-permute-start(bf16[1,1,320,512]{3,2,1,0:T(8,128)(2,1)S(1)} %get-tuple-element.29), channel_id=1, source_target_pairs={{0,4},{4,0},{8,12},{12,8},{16,20},{20,16},{24,28},{28,24},{1,5},{5... | collective-permute-start | bytes 983048 | tf_op jit(solution)/shard_map/ppermute | solution.py:481
  53.3 9.6 %copy-start.5 = (bf16[1,1,320,512]{3,2,1,0:T(8,128)(2,1)}, bf16[1,1,320,512]{3,2,1,0:T(8,128)(2,1)S(1)}, u32[]{:S(2)}) copy-start(bf16[1,1,320,512]{3,2,1,0:T(8,128)(2,1)S(1)} %collective-permute-done.12.rest_2_) | copy-start | bytes 983044
  53.3 54.7 %copy-start.6 = (f32[2,8,320]{2,1,0:T(8,128)S(1)}, f32[2,8,320]{2,1,0:T(8,128)}, u32[]{:S(2)}) copy-start(f32[2,8,320]{2,1,0:T(8,128)} %param.16) | copy-start | bytes 61444
  53.3 96.5 %collective-permute-start.9 = (bf16[1,6,320,512]{3,2,1,0:T(8,128)(2,1)}, bf16[1,6,320,512]{3,2,1,0:T(8,128)(2,1)}, u32[]{:S(2)}, u32[]{:S(2)}) collective-permute-start(bf16[1,6,320,512]{3,2,1,0:T(8,128)(2,1)} %get-tuple-element.28), channel_id=1, source_target_pairs={{0,2},{1,3},{2,0},{3,1},{4,6},{5,7},{6,4},{7,5},{8,10},{9,11},{10,... | collective-permute-start | bytes 5898248 | tf_op jit(solution)/shard_map/ppermute | solution.py:492
  73.4 36.8 %copy-start.7 = (bf16[1,4,64,512]{3,2,1,0:T(8,128)(2,1)S(1)}, bf16[1,4,64,512]{3,2,1,0:T(8,128)(2,1)}, u32[]{:S(2)}) copy-start(bf16[1,4,64,512]{3,2,1,0:T(8,128)(2,1)} %get-tuple-element.23) | copy-start | bytes 786436
  73.4 32.8 %collective-permute-start.3 = (bf16[1,4,320,512]{3,2,1,0:T(8,128)(2,1)}, bf16[1,4,320,512]{3,2,1,0:T(8,128)(2,1)S(1)}, u32[]{:S(2)}, u32[]{:S(2)}) collective-permute-start(bf16[1,4,320,512]{3,2,1,0:T(8,128)(2,1)} %get-tuple-element.19), channel_id=1, source_target_pairs={{0,28},{4,8},{8,4},{12,16},{16,12},{20,24},{24,20},{28,0},{1,29},{... | collective-permute-start | bytes 3932168 | tf_op jit(solution)/shard_map/ppermute | solution.py:498
  76.2 34.1 %copy-start.2 = (bf16[2,2,320,512]{3,2,1,0:T(8,128)(2,1)}, bf16[2,2,320,512]{3,2,1,0:T(8,128)(2,1)S(1)}, u32[]{:S(2)}) copy-start(bf16[2,2,320,512]{3,2,1,0:T(8,128)(2,1)S(1)} %collective-permute-done.1.far_all) | copy-start | bytes 3932164
  76.2 34.1 %collective-permute-start.2 = (bf16[2,2,320,512]{3,2,1,0:T(8,128)(2,1)S(1)}, bf16[2,2,320,512]{3,2,1,0:T(8,128)(2,1)}, u32[]{:S(2)}, u32[]{:S(2)}) collective-permute-start(bf16[2,2,320,512]{3,2,1,0:T(8,128)(2,1)S(1)} %collective-permute-done.1.far_all), channel_id=1, source_target_pairs={{0,1},{1,0},{2,3},{3,2},{4,5},{5,4},{6,7},{7,6},{8,9},{9,8},{10,11... | collective-permute-start | bytes 3932168 | tf_op jit(solution)/shard_map/ppermute | solution.py:501
  76.2 80.0 %collective-permute-start.6 = (bf16[1,6,256,512]{3,2,1,0:T(8,128)(2,1)}, bf16[1,6,256,512]{3,2,1,0:T(8,128)(2,1)}, u32[]{:S(2)}, u32[]{:S(2)}) collective-permute-start(bf16[1,6,256,512]{3,2,1,0:T(8,128)(2,1)} %get-tuple-element.25), channel_id=1, source_target_pairs={{0,2},{1,3},{2,0},{3,1},{4,6},{5,7},{6,4},{7,5},{8,10},{9,11},{10,... | collective-permute-start | bytes 4718600 | tf_op jit(solution)/shard_map/ppermute | solution.py:493
  76.6 79.6 %collective-permute-start.7 = (bf16[1,4,256,512]{3,2,1,0:T(8,128)(2,1)}, bf16[1,4,256,512]{3,2,1,0:T(8,128)(2,1)S(1)}, u32[]{:S(2)}, u32[]{:S(2)}) collective-permute-start(bf16[1,4,256,512]{3,2,1,0:T(8,128)(2,1)} %get-tuple-element.26), channel_id=1, source_target_pairs={{0,4},{4,0},{8,12},{12,8},{16,20},{20,16},{24,28},{28,24},{1,5},{5... | collective-permute-start | bytes 3145736 | tf_op jit(solution)/shard_map/ppermute | solution.py:499
  106.2 1.1 copy-start.3
  107.3 54.9 %collective-permute-start.4 = (bf16[1,6,64,512]{3,2,1,0:T(8,128)(2,1)}, bf16[1,6,64,512]{3,2,1,0:T(8,128)(2,1)S(1)}, u32[]{:S(2)}, u32[]{:S(2)}) collective-permute-start(bf16[1,6,64,512]{3,2,1,0:T(8,128)(2,1)} %get-tuple-element.22), channel_id=1, source_target_pairs={{0,2},{1,3},{2,0},{3,1},{4,6},{5,7},{6,4},{7,5},{8,10},{9,11},{10,... | collective-permute-start | bytes 1179656 | tf_op jit(solution)/shard_map/ppermute | solution.py:494
  110.2 52.0 %collective-permute-start.5 = (bf16[1,4,64,512]{3,2,1,0:T(8,128)(2,1)S(1)}, bf16[1,4,64,512]{3,2,1,0:T(8,128)(2,1)S(1)}, u32[]{:S(2)}, u32[]{:S(2)}) collective-permute-start(bf16[1,4,64,512]{3,2,1,0:T(8,128)(2,1)S(1)} %copy-done.7), channel_id=1, source_target_pairs={{0,4},{4,0},{8,12},{12,8},{16,20},{20,16},{24,28},{28,24},{1,5},{5... | collective-permute-start | bytes 786440 | tf_op jit(solution)/shard_map/ppermute | solution.py:500
  156.2 1.0 copy-start.4
  157.2 5.1 %copy-start = (s32[1,4]{1,0:T(1,128)S(1)}, s32[1,4]{1,0:T(1,128)}, u32[]{:S(2)}) copy-start(s32[1,4]{1,0:T(1,128)} %left.9) | copy-start | bytes 52
  157.2 5.1 %copy-start.1 = (s32[1,4]{1,0:T(1,128)S(1)}, s32[1,4]{1,0:T(1,128)}, u32[]{:S(2)}) copy-start(s32[1,4]{1,0:T(1,128)} %right.9) | copy-start | bytes 52
